TPU v7x, 256 devices: a whole 4x4x8 slice. The times are simulated.
256 devices in a mesh: seq: 16 (over y_lo, z), tp: 8 (over y_hi, x), dp: 2 (over core).
Axes of the slice: x: 4, y: 4 (y_hi: 2, y_lo: 2; y = y_hi * 2 + y_lo), z: 8, core: 2. Of those that a mesh axis runs over, the one named last changes fastest.
Arguments:
- img_query: bfloat16 [16384, 3072], P(('dp', 'seq'), 'tp'), parts along dimension 0, may hold values from -6 to 6
- img_key: bfloat16 [16384, 3072], P(('dp', 'seq'), 'tp'), parts along dimension 0, may hold values from -6 to 6
- img_value: bfloat16 [16384, 3072], P(('dp', 'seq'), 'tp'), parts along dimension 0, may hold values from -12 to 12
- text_key: bfloat16 [512, 3072], P(('dp', 'seq'), 'tp'), parts along dimension 0, may hold values from -6 to 6
- text_value: bfloat16 [512, 3072], P(('dp', 'seq'), 'tp'), parts along dimension 0, may hold values from -12 to 12
- residual_in: bfloat16 [16384, 3072], P(('dp', 'seq', 'tp')), parts along dimension 0, may hold values from -12 to 12
- mod_shift: float32 [6144], P('dp'), parts along dimension 0, may hold values from -3 to 3
- mod_scale: float32 [6144], P('dp'), parts along dimension 0, may hold values from -0.5 to 0.5
- gate_attn: float32 [6144], P('dp'), parts along dimension 0, may hold values from 0.5 to 1.5
- gate_mlp: float32 [6144], P('dp'), parts along dimension 0, may hold values from 0.5 to 1.5
- out_weight: bfloat16 [3072, 3072], P('tp'), may hold values from -0.109375 to 0.109375
- out_bias: float32 [3072], replicated, may hold values from -3 to 3
- up_weight: bfloat16 [3072, 6144], P(None, 'tp'), may hold values from -0.109375 to 0.109375
- up_bias: float32 [6144], P('tp'), may hold values from -3 to 3
- down_weight: bfloat16 [6144, 3072], P('tp'), may hold values from -0.078125 to 0.078125
- down_bias: float32 [3072], replicated, may hold values from -3 to 3
Outputs:
- stream_out: bfloat16 [16384, 3072], P(('dp', 'seq', 'tp')), parts along dimension 0
There are 2 independent parts, one for each index of `dp`. A program takes and returns all parts, laid end to end along the dimension named above; an argument that names none is the same for every part. Nothing has to cross between parts.
All inputs are finite; a program needn't handle non-finite values.
Results may differ from a plain program's by a relative error of at most 0.015.
Values may be sent and summed in bfloat16 or wider, within the bound.
No kernel may reach another device: no remote copies, remote signals or barrier semaphores. Data moves between devices by JAX's collectives and lax.ppermute only.
A program may use at most 192 MiB of HBM per device.

v0:
```python
import functools
import math

import jax
import jax.numpy as jnp
from jax import lax
from jax.experimental import pallas as pl
from jax.experimental.pallas import tpu as pltpu
from jax.sharding import Mesh, PartitionSpec as P

HD = 128
LOG2E = math.log2(math.e)
SCORE_TO_LOG2 = LOG2E / math.sqrt(HD)

FINE = (("yl", 2), ("z", 8), ("yh", 2), ("x", 4), ("dp", 2))


def attend_body(pieces, first, last, *refs):
    q_ref = refs[0]
    k_refs = refs[1 : 1 + pieces]
    v_refs = refs[1 + pieces : 1 + 2 * pieces]
    at = 1 + 2 * pieces
    if not first:
        m_in, l_in, acc_in = refs[at : at + 3]
        at += 3
    outs = refs[at:]
    q = q_ref[...]
    scores = [
        lax.dot_general(k[...], q, (((1,), (1,)), ((), ())), preferred_element_type=jnp.float32)
        for k in k_refs
    ]
    m = functools.reduce(jnp.maximum, [jnp.max(s, axis=0, keepdims=True) for s in scores])
    if not first:
        m_old = m_in[0]
        m = jnp.maximum(m, m_old)
    den = None
    acc = None
    for s, v in zip(scores, v_refs):
        e = jnp.exp2((s - m) * SCORE_TO_LOG2)
        part = jnp.sum(e, axis=0, keepdims=True)
        den = part if den is None else den + part
        mixed = lax.dot_general(
            v[...],
            e.astype(jnp.bfloat16),
            (((0,), (0,)), ((), ())),
            preferred_element_type=jnp.float32,
        )
        acc = mixed if acc is None else acc + mixed
    if not first:
        factor = jnp.exp2((m_old - m) * SCORE_TO_LOG2)
        den = den + factor * l_in[0]
        acc = acc + factor * acc_in[...]
    if last:
        o_ref, lse_ref = outs
        o_ref[...] = (acc / den).T.astype(jnp.bfloat16)
        lse_ref[0] = m * SCORE_TO_LOG2 + jnp.log2(den)
    else:
        m_out, l_out, acc_out = outs
        m_out[0] = m
        l_out[0] = den
        acc_out[...] = acc


def attend(q, pairs, state, last, block=512):
    rows, width = q.shape
    heads = width // HD
    ks = vs = pairs
    first = state is None
    q_spec = pl.BlockSpec((block, HD), lambda h, j: (j, h))
    k_specs = [pl.BlockSpec((k.shape[0], HD), lambda h, j: (0, h)) for k in ks]
    v_specs = [pl.BlockSpec((v.shape[0], HD), lambda h, j: (0, heads + h)) for v in vs]
    stat = pl.BlockSpec((1, 1, block), lambda h, j: (h, 0, j))
    acc = pl.BlockSpec((HD, block), lambda h, j: (h, j))
    stat_shape = jax.ShapeDtypeStruct((heads, 1, rows), jnp.float32)
    if last:
        out_specs = [q_spec, stat]
        out_shape = [jax.ShapeDtypeStruct((rows, width), jnp.bfloat16), stat_shape]
    else:
        out_specs = [stat, stat, acc]
        out_shape = [stat_shape, stat_shape, jax.ShapeDtypeStruct((width, rows), jnp.float32)]
    keys = sum(k.shape[0] for k in ks)
    return pl.pallas_call(
        functools.partial(attend_body, len(ks), first, last),
        grid=(heads, rows // block),
        in_specs=[q_spec, *k_specs, *v_specs, *(() if first else (stat, stat, acc))],
        out_specs=out_specs,
        out_shape=out_shape,
        cost_estimate=pl.CostEstimate(
            flops=4 * rows * keys * width,
            transcendentals=rows * keys * heads,
            bytes_accessed=2 * (rows + 2 * keys) * width,
        ),
        compiler_params=pltpu.CompilerParams(vmem_limit_bytes=48 << 20),
    )(q, *ks, *vs, *(() if first else state))


def join_project_body(part_ref, other_ref, lse_ref, lse_other_ref, weight_ref, out_ref):
    pieces = []
    for h in range(part_ref.shape[1] // HD):
        cols = slice(h * HD, (h + 1) * HD)
        share = 1.0 / (1.0 + jnp.exp2(lse_other_ref[h] - lse_ref[h]))
        share = jnp.broadcast_to(share, (HD, share.shape[1])).T
        own = part_ref[:, cols].astype(jnp.float32)
        other = other_ref[:, cols].astype(jnp.float32)
        pieces.append((other + share * (own - other)).astype(jnp.bfloat16))
    attended = jnp.concatenate(pieces, axis=1)
    out_ref[...] = jnp.dot(
        attended, weight_ref[...], preferred_element_type=jnp.float32
    ).astype(jnp.bfloat16)


def join_project(part, other, lse, lse_other, weight, block=768):
    rows, width = other.shape
    cols = weight.shape[1]
    first = pl.BlockSpec((rows, width), lambda j: (0, 0))
    stat = pl.BlockSpec((lse.shape[0], 1, rows), lambda j: (0, 0, 0))
    return pl.pallas_call(
        join_project_body,
        grid=(cols // block,),
        in_specs=[first, first, stat, stat, pl.BlockSpec((width, block), lambda j: (0, j))],
        out_specs=pl.BlockSpec((rows, block), lambda j: (0, j)),
        out_shape=jax.ShapeDtypeStruct((rows, cols), jnp.bfloat16),
        cost_estimate=pl.CostEstimate(
            flops=2 * rows * width * cols, transcendentals=0, bytes_accessed=2 * width * cols
        ),
        compiler_params=pltpu.CompilerParams(vmem_limit_bytes=32 << 20),
    )(part, other, lse, lse_other, weight)


def stream_norm_body(
    terms_ref, residual_ref, gate_ref, bias_ref, scale_ref, shift_ref, stream_ref, normed_ref
):
    proj = terms_ref[0].astype(jnp.float32)
    for g in range(1, terms_ref.shape[0]):
        proj = proj + terms_ref[g].astype(jnp.float32)
    stream = residual_ref[...].astype(jnp.float32) + gate_ref[...] * (proj + bias_ref[...])
    center = jnp.mean(stream, axis=-1, keepdims=True)
    off = stream - center
    spread = jnp.mean(off * off, axis=-1, keepdims=True)
    normed = off * lax.rsqrt(spread + 1e-06) * (1.0 + scale_ref[...]) + shift_ref[...]
    stream_ref[...] = stream
    normed_ref[...] = normed.astype(jnp.bfloat16)


def stream_norm(terms, residual, gate, bias, scale, shift_by, block=16):
    groups, rows, d_model = terms.shape
    row = pl.BlockSpec((block, d_model), lambda i: (i, 0))
    vec = pl.BlockSpec((1, d_model), lambda i: (0, 0))
    return pl.pallas_call(
        stream_norm_body,
        grid=(rows // block,),
        in_specs=[pl.BlockSpec((groups, block, d_model), lambda i: (0, i, 0)), row, vec, vec, vec, vec],
        out_specs=[row, row],
        out_shape=[
            jax.ShapeDtypeStruct((rows, d_model), jnp.float32),
            jax.ShapeDtypeStruct((rows, d_model), jnp.bfloat16),
        ],
        cost_estimate=pl.CostEstimate(
            flops=20 * rows * d_model, transcendentals=0, bytes_accessed=24 * rows * d_model
        ),
        compiler_params=pltpu.CompilerParams(vmem_limit_bytes=32 << 20),
    )(terms, residual, *(v.reshape(1, -1) for v in (gate, bias, scale, shift_by)))


def mlp_body(order, x_ref, up_ref, down_ref, bias_ref, bias_far_ref, *refs):
    n = 4
    up_far, down_far, out_ref = refs[:n], refs[n : n + 2], refs[n + 2]
    near, far, hid_near, hid_far, up_buf, down_buf, sems = refs[n + 3 :]
    i = pl.program_id(0)
    quarter = up_ref.shape[0]

    def copies():
        for j in range(n):
            yield pltpu.make_async_copy(up_far[j], up_buf.at[j], sems.at[j])
        for j in range(n):
            cols = pl.ds((j % 2) * quarter, quarter)
            yield pltpu.make_async_copy(down_far[j // 2].at[:, cols], down_buf.at[j], sems.at[n + j])

    @pl.when(i == 0)
    def _():
        for copy in copies():
            copy.start()
        near[...] = jnp.broadcast_to(bias_ref[...], near.shape)
        far[...] = jnp.broadcast_to(bias_far_ref[...], far.shape)

    for j, copy in enumerate(copies()):

        @pl.when(i == j)
        def _(copy=copy):
            copy.wait()

    @pl.when(i < n)
    def _():
        at = pl.multiple_of(i * quarter, quarter)
        near[...] += jnp.dot(
            x_ref[:, pl.ds(at, quarter)], up_ref[...], preferred_element_type=jnp.float32
        )
        at = pl.multiple_of(order[i] * quarter, quarter)
        far[...] += jnp.dot(
            x_ref[:, pl.ds(at, quarter)], up_buf[i], preferred_element_type=jnp.float32
        )

    @pl.when(i == n - 1)
    def _():
        hid_near[...] = jax.nn.gelu(near[...], approximate=True).astype(jnp.bfloat16)
        hid_far[...] = jax.nn.gelu(far[...], approximate=True).astype(jnp.bfloat16)

    @pl.when(i >= n)
    def _():
        out_ref[...] = (
            jnp.dot(hid_near[...], down_ref[...], preferred_element_type=jnp.float32)
            + jnp.dot(hid_far[...], down_buf[i - n], preferred_element_type=jnp.float32)
        ).astype(jnp.bfloat16)


def mlp(x, up, down, bias, bias_far, up_far, down_far, order):
    rows, d_model = x.shape
    hidden = up.shape[1]
    n = len(up_far)
    quarter = d_model // n
    whole = lambda i, order: (0, 0)
    column = lambda i, order: (0, order[jnp.maximum(i, n)])
    far_spec = pl.BlockSpec(memory_space=pltpu.MemorySpace.HBM)
    return pl.pallas_call(
        mlp_body,
        grid_spec=pltpu.PrefetchScalarGridSpec(
            num_scalar_prefetch=1,
            grid=(2 * n,),
            in_specs=[
                pl.BlockSpec((rows, d_model), whole),
                pl.BlockSpec((quarter, hidden), lambda i, order: (jnp.minimum(i, n - 1), 0)),
                pl.BlockSpec((hidden, quarter), column),
                pl.BlockSpec((1, hidden), whole),
                pl.BlockSpec((1, hidden), whole),
                *[far_spec] * (n + 2),
            ],
            out_specs=pl.BlockSpec((rows, quarter), column),
            scratch_shapes=[
                pltpu.VMEM((rows, hidden), jnp.float32),
                pltpu.VMEM((rows, hidden), jnp.float32),
                pltpu.VMEM((rows, hidden), jnp.bfloat16),
                pltpu.VMEM((rows, hidden), jnp.bfloat16),
                pltpu.VMEM((n, quarter, hidden), jnp.bfloat16),
                pltpu.VMEM((n, hidden, quarter), jnp.bfloat16),
                pltpu.SemaphoreType.DMA((2 * n,)),
            ],
        ),
        out_shape=jax.ShapeDtypeStruct((rows, d_model), jnp.bfloat16),
        cost_estimate=pl.CostEstimate(
            flops=8 * rows * d_model * hidden,
            transcendentals=rows * hidden * 2,
            bytes_accessed=8 * d_model * hidden,
        ),
        compiler_params=pltpu.CompilerParams(vmem_limit_bytes=40 << 20),
    )(order, x, up, down, bias.reshape(1, -1), bias_far.reshape(1, -1), *up_far, *down_far)


def shift(array, axis, size, by):
    return lax.ppermute(array, axis, [(i, (i + by) % size) for i in range(size)])


def cross(array):
    return lax.ppermute(array, ("yl", "yh"), [(0, 3), (3, 0), (1, 2), (2, 1)])


def part_of(array, parts, index, axis):
    n = array.shape[axis] // parts
    return lax.dynamic_slice_in_dim(array, index * n, n, axis)


tie = lax.optimization_barrier


def gather_x(rows):
    n = rows.shape[0] // 2
    left = shift(rows, "x", 4, 1)
    right = shift(rows, "x", 4, 3)
    far = jnp.concatenate([shift(left[:n], "x", 4, 1), shift(right[n:], "x", 4, 3)], axis=0)
    return rows, left, right, far


def shards(
    img_query,
    img_key,
    img_value,
    text_key,
    text_value,
    residual_in,
    mod_shift,
    mod_scale,
    gate_attn,
    gate_mlp,
    out_weight,
    out_bias,
    up_weight,
    up_bias,
    down_weight,
    down_bias,
):
    yl_at, core = lax.axis_index("yl"), lax.axis_index("dp")
    rows_own = img_query.shape[0]
    row_block, d_model = residual_in.shape

    up_a = cross(part_of(up_weight, 4, yl_at * 2 + core, 0))
    down_a = cross(part_of(down_weight, 2, core, 1))
    order = jnp.bitwise_xor(
        jnp.array([2, 2, 2, 2, 0, 0, 0, 0], jnp.int32) * (1 - yl_at)
        + core * jnp.array([1, 1, 1, 1, 2, 2, 2, 2], jnp.int32),
        jnp.array([0, 2, 1, 3, 0, 1, 2, 3], jnp.int32),
    )

    q_other = shift(img_query, "yl", 2, 1)
    own = jnp.concatenate(
        [
            jnp.concatenate([img_key, text_key], axis=0),
            jnp.concatenate([img_value, text_value], axis=0),
        ],
        axis=1,
    )
    cut = -(-own.shape[0] // 32) * 16

    def around(up, down):
        return [shift(up, "z", 8, 1), shift(down, "z", 8, 7)]

    one = around(own, own)
    one, q_other = tie((one, q_other))
    queries = jnp.concatenate([img_query, q_other], axis=0)
    two = around(*one)
    state = attend(queries, [own], None, False)
    state = attend(queries, one, state, False)
    two, state, up_a = tie((two, state, up_a))
    three = around(*two)
    up_b = shift(up_a, "yl", 2, 1)
    state = attend(queries, two, state, False)
    three, state = tie((three, state))
    four = around(three[0][:cut], three[1][cut:])
    state = attend(queries, three, state, False)
    four, state = tie((four, state))
    part, lse = attend(queries, four, state, True)
    part, up_b, down_a = tie((part, up_b, down_a))

    part_other = shift(part[rows_own:], "yl", 2, 1)
    lse_other = shift(lse[:, :, rows_own:], "yl", 2, 1)
    terms = join_project(part, part_other, lse, lse_other, out_weight)
    terms = lax.all_to_all(
        terms.reshape(8, row_block, d_model), ("yh", "x"), split_axis=0, concat_axis=0, tiled=True
    )
    up_far = [up_a, up_b, shift(up_a, "dp", 2, 1), shift(up_b, "dp", 2, 1)]
    down_far = [down_a, shift(down_a, "dp", 2, 1)]
    bias_far = cross(up_bias)
    terms, up_far, down_far, bias_far = tie((terms, up_far, down_far, bias_far))
    stream, normed = stream_norm(terms, residual_in, gate_attn, out_bias, mod_scale, mod_shift)
    everyone = jnp.concatenate(gather_x(normed), axis=0)
    out = mlp(everyone, up_weight, down_weight, up_bias, bias_far, up_far, down_far, order)
    blocks = out.reshape(4, row_block, d_model)
    total = blocks[0].astype(jnp.float32)
    total = total + shift(blocks[1], "x", 4, 3).astype(jnp.float32)
    total = total + shift(blocks[2], "x", 4, 1).astype(jnp.float32)
    total = total + shift(blocks[3], "x", 4, 2).astype(jnp.float32)
    return (stream + gate_mlp * (total + down_bias)).astype(jnp.bfloat16)


def solution(mesh):
    fine = Mesh(mesh.devices.reshape([n for _, n in FINE]), [name for name, _ in FINE])
    seq, tp = ("yl", "z"), ("yh", "x")
    tokens = P(("dp", *seq), tp)
    rows = P(("dp", *seq, *tp), None)
    in_specs = (
        tokens,
        tokens,
        tokens,
        tokens,
        tokens,
        rows,
        P("dp"),
        P("dp"),
        P("dp"),
        P("dp"),
        P(tp, None),
        P(),
        P(None, tp),
        P(tp),
        P(tp, None),
        P(),
    )
    return jax.shard_map(shards, mesh=fine, in_specs=in_specs, out_specs=rows, check_vma=False)
```

profile of v0, /device:TPU:8, one launch (start us, length us, event | category | flops | bytes accessed | tf_op | source)
XLA Modules:
  0.0 202.6 jit_solution(1929960000235923469)
XLA Ops:
  0.0 1.3 maximum_maximum_fusion.refs_1_.refs_2_
  1.3 2.0 collective-permute-start
  3.3 4.0 %collective-permute-start.1 = (bf16[528,768]{1,0:T(8,128)(2,1)S(1)}, bf16[528,768]{1,0:T(8,128)(2,1)}, u32[]{:S(2)}, u32[]{:S(2)}) collective-permute-start(bf16[528,768]{1,0:T(8,128)(2,1)S(1)} %maximum_maximum_fusion.refs_1_.refs_2_), channel_id=1, source_target_pairs={{0,112},{16,0},{32,16},{48,32},{64,48},{80,64},{96,80},{112,96},{1... | collective-permute-start | bytes 2433032 | tf_op jit(solution)/shard_map/ppermute | solution.py:259
  7.7 2.4 %constant_dynamic-slice_fusion.1 = bf16[768,768]{1,0:T(8,128)(2,1)} fusion(bf16[3072,768]{1,0:T(8,128)(2,1)} %up_ref.1, s32[]{:T(128)S(6)} %select_n.6), kind=kLoop, calls=%fused_computation.11 | loop fusion | bytes 2359300 | tf_op jit(solution)/shard_map/dynamic_slice | solution.py:268
  10.2 2.4 %collective-permute-start.5 = (bf16[768,768]{1,0:T(8,128)(2,1)}, bf16[768,768]{1,0:T(8,128)(2,1)S(1)}, u32[]{:S(2)}, u32[]{:S(2)}) collective-permute-start(bf16[768,768]{1,0:T(8,128)(2,1)} %constant_dynamic-slice_fusion.1), channel_id=1, source_target_pairs={{0,136},{136,0},{8,128},{128,8},{1,137},{137,1},{9,129},{129,9},{2... | collective-permute-start | bytes 3538952 | tf_op jit(solution)/shard_map/ppermute | solution.py:263
  12.6 3.2 %constant_dynamic-slice_fusion = bf16[768,1536]{1,0:T(8,128)(2,1)} fusion(bf16[768,3072]{1,0:T(8,128)(2,1)} %down_ref.1, s32[]{:T(128)S(6)} %select_n.7), kind=kLoop, calls=%fused_computation.10 | loop fusion | bytes 4718596 | tf_op jit(solution)/shard_map/dynamic_slice | solution.py:268
  15.8 2.2 %collective-permute-done.2 = bf16[512,384]{1,0:T(8,128)(2,1)} collective-permute-done((bf16[512,384]{1,0:T(8,128)(2,1)S(1)}, bf16[512,384]{1,0:T(8,128)(2,1)}, u32[]{:S(2)}, u32[]{:S(2)}) %collective-permute-start.2) | collective-permute-done | bytes 393248 | tf_op jit(solution)/shard_map/ppermute | solution.py:259
  18.0 7.3 %collective-permute-done.refs_1_.refs_3_ = bf16[528,768]{1,0:T(8,128)(2,1)S(1)} collective-permute-done((bf16[528,768]{1,0:T(8,128)(2,1)S(1)}, bf16[528,768]{1,0:T(8,128)(2,1)S(1)}, u32[]{:S(2)}, u32[]{:S(2)}) %collective-permute-start) | collective-permute-done | bytes 811040 | tf_op jit(solution)/shard_map/ppermute | solution.py:259
  25.3 3.2 %collective-permute-start.4 = (bf16[528,768]{1,0:T(8,128)(2,1)}, bf16[528,768]{1,0:T(8,128)(2,1)S(1)}, u32[]{:S(2)}, u32[]{:S(2)}) collective-permute-start(bf16[528,768]{1,0:T(8,128)(2,1)} %collective-permute-done.1.refs_2_.refs_4_), channel_id=1, source_target_pairs={{0,112},{16,0},{32,16},{48,32},{64,48},{80,64},{96,80},{112,96},{1... | collective-permute-start | bytes 2433032 | tf_op jit(solution)/shard_map/ppermute | solution.py:259
  28.6 1.1 constant_dynamic-update-slice_fusion.refs_0_
  29.6 5.1 %shard_map.181 = (f32[3,1,1024]{2,1,0:T(1,128)S(1)}, f32[3,1,1024]{2,1,0:T(1,128)S(1)}, f32[384,1024]{1,0:T(8,128)S(1)}) custom-call(bf16[1024,384]{1,0:T(8,128)(2,1)S(1)} %constant_dynamic-update-slice_fusion.refs_0_, bf16[528,768]{1,0:T(8,128)(2,1)S(1)} %maximum_maximum_fusion.refs_1_.refs_2_, bf16[528,768]{1,0:T(8,128)(2,1)S(1)} %maximum_maximum_fusion.refs_1_.refs_2_), custom_call_target="tpu_custom_call" | custom-call | flops 830472192 | bytes 1597440 | tf_op jit(solution)/shard_map/pallas_call | solution.py:82
  34.7 8.8 %shard_map.182 = (f32[3,1,1024]{2,1,0:T(1,128)S(1)}, f32[3,1,1024]{2,1,0:T(1,128)S(1)}, f32[384,1024]{1,0:T(8,128)S(1)}) custom-call(bf16[1024,384]{1,0:T(8,128)(2,1)S(1)} %constant_dynamic-update-slice_fusion.refs_0_, bf16[528,768]{1,0:T(8,128)(2,1)S(1)} %collective-permute-done.refs_1_.refs_3_, bf16[528,768]{1,0:T(8,128)(2,1)} %collective-permute-done.1.refs_2_.refs_4_, ...), custom_call_target="tpu_custom_call" | custom-call | flops 1660944384 | bytes 2408448 | tf_op jit(solution)/shard_map/pallas_call | solution.py:82
  43.6 1.1 copy-done.13
  44.7 1.0 collective-permute-done.3.refs_1_.refs_3_
  45.7 2.1 %collective-permute-start.6 = (bf16[528,768]{1,0:T(8,128)(2,1)S(1)}, bf16[528,768]{1,0:T(8,128)(2,1)S(1)}, u32[]{:S(2)}, u32[]{:S(2)}) collective-permute-start(bf16[528,768]{1,0:T(8,128)(2,1)S(1)} %collective-permute-done.3.refs_1_.refs_3_), channel_id=1, source_target_pairs={{0,16},{16,32},{32,48},{48,64},{64,80},{80,96},{96,112},{112,0},{1... | collective-permute-start | bytes 2433032 | tf_op jit(solution)/shard_map/ppermute | solution.py:259
  47.9 1.1 collective-permute-start.7
  49.4 1.4 copy-done.14
  50.8 7.9 %shard_map.183 = (f32[3,1,1024]{2,1,0:T(1,128)S(1)}, f32[3,1,1024]{2,1,0:T(1,128)S(1)}, f32[384,1024]{1,0:T(8,128)S(1)}) custom-call(bf16[1024,384]{1,0:T(8,128)(2,1)S(1)} %constant_dynamic-update-slice_fusion.refs_0_, bf16[528,768]{1,0:T(8,128)(2,1)S(1)} %collective-permute-done.3.refs_1_.refs_3_, ...), custom_call_target="tpu_custom_call" | custom-call | flops 1660944384 | bytes 2408448 | tf_op jit(solution)/shard_map/pallas_call | solution.py:82
  58.8 6.5 %collective-permute-done.6.refs_1_.refs_3_ = bf16[528,768]{1,0:T(8,128)(2,1)S(1)} collective-permute-done((bf16[528,768]{1,0:T(8,128)(2,1)S(1)}, bf16[528,768]{1,0:T(8,128)(2,1)S(1)}, u32[]{:S(2)}, u32[]{:S(2)}) %collective-permute-start.6) | collective-permute-done | bytes 811040 | tf_op jit(solution)/shard_map/ppermute | solution.py:259
  65.3 1.8 collective-permute-start.8
  67.2 1.7 collective-permute-start.9
  68.9 8.0 %shard_map.184 = (f32[3,1,1024]{2,1,0:T(1,128)S(1)}, f32[3,1,1024]{2,1,0:T(1,128)S(1)}, f32[384,1024]{1,0:T(8,128)S(1)}) custom-call(bf16[1024,384]{1,0:T(8,128)(2,1)S(1)} %constant_dynamic-update-slice_fusion.refs_0_, bf16[528,768]{1,0:T(8,128)(2,1)S(1)} %collective-permute-done.6.refs_1_.refs_3_, ...), custom_call_target="tpu_custom_call" | custom-call | flops 1660944384 | bytes 2408448 | tf_op jit(solution)/shard_map/pallas_call | solution.py:82
  76.9 5.7 %shard_map.185 = (bf16[1024,384]{1,0:T(8,128)(2,1)S(1)}, f32[3,1,1024]{2,1,0:T(1,128)S(1)}) custom-call(bf16[1024,384]{1,0:T(8,128)(2,1)S(1)} %constant_dynamic-update-slice_fusion.refs_0_, bf16[272,768]{1,0:T(8,128)(2,1)S(1)} %collective-permute-done.8.refs_1_.refs_3_, bf16[256,768]{1,0:T(8,128)(2,1)S(1)} %collective-permute-done.9.refs_2_.refs_4_, ...), custom_call_target="tpu_custom_call" | custom-call | flops 830472192 | bytes 1597440 | tf_op jit(solution)/shard_map/pallas_call | solution.py:82
  82.6 6.1 %collective-permute-done.11.refs_4_ = bf16[768,1536]{1,0:T(8,128)(2,1)S(1)} collective-permute-done((bf16[768,1536]{1,0:T(8,128)(2,1)}, bf16[768,1536]{1,0:T(8,128)(2,1)S(1)}, u32[]{:S(2)}, u32[]{:S(2)}) %collective-permute-start.11) | collective-permute-done | bytes 2359328 | tf_op jit(solution)/shard_map/ppermute | solution.py:263
  88.8 2.2 %collective-permute-start.12 = (bf16[512,384]{1,0:T(8,128)(2,1)S(1)}, bf16[512,384]{1,0:T(8,128)(2,1)S(1)}, u32[]{:S(2)}, u32[]{:S(2)}) collective-permute-start(bf16[512,384]{1,0:T(8,128)(2,1)S(1)} %slice.36), channel_id=1, source_target_pairs={{0,128},{128,0},{1,129},{129,1},{2,130},{130,2},{3,131},{131,3},{4... | collective-permute-start | bytes 1179656 | tf_op jit(solution)/shard_map/ppermute | solution.py:259
  91.1 7.6 %collective-permute-done.13.lse_other_ref = f32[3,1,512]{2,1,0:T(1,128)S(1)} collective-permute-done((f32[3,1,512]{2,1,0:T(1,128)S(1)}, f32[3,1,512]{2,1,0:T(1,128)S(1)}, u32[]{:S(2)}, u32[]{:S(2)}) %collective-permute-start.13) | collective-permute-done | bytes 6176 | tf_op jit(solution)/shard_map/ppermute | solution.py:259
  98.8 3.1 %shard_map.186 = bf16[512,3072]{1,0:T(8,128)(2,1)S(1)} custom-call(bf16[1024,384]{1,0:T(8,128)(2,1)S(1)} %get-tuple-element.83.part_ref, bf16[512,384]{1,0:T(8,128)(2,1)S(1)} %collective-permute-done.12.other_ref, f32[3,1,1024]{2,1,0:T(1,128)S(1)} %get-tuple-element.84.lse_ref, f32[3,1,512]{2,1,0:T(1,128)S(1)} %collective-permute-done.13.lse_other_ref, ...), custom_call_target="tpu_custom_call" | custom-call | flops 1207959552 | bytes 2359296 | tf_op jit(solution)/shard_map/pallas_call | solution.py:117
  102.0 1.6 copy-done
  103.6 6.6 %all-to-all-start = ((bf16[8,64,3072]{2,1,0:T(8,128)(2,1)}), bf16[8,64,3072]{2,1,0:T(8,128)(2,1)S(1)}, u32[]{:S(2)}, u32[]{:S(2)}) async-start(bf16[8,64,3072]{2,1,0:T(8,128)(2,1)} %bitcast.5), calls=%async_computation | async-start | bytes 6291456 | tf_op jit(solution)/shard_map/all_to_all | solution.py:345
  110.8 2.3 %collective-permute-start.17 = (f32[768]{0:T(1024)S(1)}, f32[768]{0:T(1024)}, u32[]{:S(2)}, u32[]{:S(2)}) collective-permute-start(f32[768]{0:T(1024)S(1)} %copy-done.18), channel_id=1, source_target_pairs={{0,136},{136,0},{8,128},{128,8},{1,137},{137,1},{9,129},{129,9},{2... | collective-permute-start | bytes 9224 | tf_op jit(solution)/shard_map/ppermute | solution.py:263
  113.1 2.3 %collective-permute-done.17 = f32[768]{0:T(1024)} collective-permute-done((f32[768]{0:T(1024)S(1)}, f32[768]{0:T(1024)}, u32[]{:S(2)}, u32[]{:S(2)}) %collective-permute-start.17) | collective-permute-done | bytes 3104 | tf_op jit(solution)/shard_map/ppermute | solution.py:263
  115.4 1.3 collective-permute-done.14.refs_2_
  116.8 1.7 collective-permute-done.15.refs_3_
  118.5 29.0 %all-to-all-done.terms_ref = bf16[8,64,3072]{2,1,0:T(8,128)(2,1)S(1)} async-done(((bf16[8,64,3072]{2,1,0:T(8,128)(2,1)}), bf16[8,64,3072]{2,1,0:T(8,128)(2,1)S(1)}, u32[]{:S(2)}, u32[]{:S(2)}) %all-to-all-start) | async-done | bytes 3145760 | tf_op jit(solution)/shard_map/all_to_all | solution.py:345
  147.5 0.7 copy-done.10
  148.2 0.7 copy-done.11
  149.6 1.6 shard_map.187
  151.2 0.9 collective-permute-start.18
  152.2 2.4 %collective-permute-start.19 = (bf16[64,3072]{1,0:T(8,128)(2,1)S(1)}, bf16[64,3072]{1,0:T(8,128)(2,1)S(1)}, u32[]{:S(2)}, u32[]{:S(2)}) collective-permute-start(bf16[64,3072]{1,0:T(8,128)(2,1)S(1)} %get-tuple-element.89), channel_id=1, source_target_pairs={{0,6},{2,0},{4,2},{6,4},{1,7},{3,1},{5,3},{7,5},{8,14},{10,8},{12,... | collective-permute-start | bytes 1179656 | tf_op jit(solution)/shard_map/ppermute | solution.py:259
  155.3 7.9 %collective-permute-done.18 = bf16[64,3072]{1,0:T(8,128)(2,1)S(1)} collective-permute-done((bf16[64,3072]{1,0:T(8,128)(2,1)S(1)}, bf16[64,3072]{1,0:T(8,128)(2,1)S(1)}, u32[]{:S(2)}, u32[]{:S(2)}) %collective-permute-start.18) | collective-permute-done | bytes 393248 | tf_op jit(solution)/shard_map/ppermute | solution.py:259
  163.3 3.3 %collective-permute-start.21 = (bf16[32,3072]{1,0:T(8,128)(2,1)S(1)}, bf16[32,3072]{1,0:T(8,128)(2,1)S(1)}, u32[]{:S(2)}, u32[]{:S(2)}) collective-permute-start(bf16[32,3072]{1,0:T(8,128)(2,1)S(1)} %slice.45), channel_id=1, source_target_pairs={{0,6},{2,0},{4,2},{6,4},{1,7},{3,1},{5,3},{7,5},{8,14},{10,8},{12,... | collective-permute-start | bytes 589832 | tf_op jit(solution)/shard_map/ppermute | solution.py:259
  166.7 3.5 %collective-permute-done.20 = bf16[32,3072]{1,0:T(8,128)(2,1)S(1)} collective-permute-done((bf16[32,3072]{1,0:T(8,128)(2,1)S(1)}, bf16[32,3072]{1,0:T(8,128)(2,1)S(1)}, u32[]{:S(2)}, u32[]{:S(2)}) %collective-permute-start.20) | collective-permute-done | bytes 196640 | tf_op jit(solution)/shard_map/ppermute | solution.py:259
  170.3 12.1 %shard_map.188 = bf16[256,3072]{1,0:T(8,128)(2,1)S(1)} custom-call(s32[8]{0:T(128)S(1)} %add_xor_fusion.order, bf16[256,3072]{1,0:T(8,128)(2,1)S(1)} %constant_dynamic-update-slice_fusion.2.x_ref, bf16[3072,768]{1,0:T(8,128)(2,1)} %up_ref.1, bf16[768,3072]{1,0:T(8,128)(2,1)} %down_ref.1, f32[1,768]{1,0:T(1,128)S(1)} %reshape.37.bias_ref, ...), custom_call_target="tpu_custom_call" | custom-call | flops 4831838208 | bytes 18874368 | tf_op jit(solution)/shard_map/pallas_call | solution.py:224
  182.5 1.6 collective-permute-start.24
  184.1 2.6 %collective-permute-start.23 = (bf16[64,3072]{1,0:T(8,128)(2,1)S(1)}, bf16[64,3072]{1,0:T(8,128)(2,1)S(1)}, u32[]{:S(2)}, u32[]{:S(2)}) collective-permute-start(bf16[64,3072]{1,0:T(8,128)(2,1)S(1)} %get-tuple-element.99), channel_id=1, source_target_pairs={{0,2},{2,4},{4,6},{6,0},{1,3},{3,5},{5,7},{7,1},{8,10},{10,12},{12... | collective-permute-start | bytes 1179656 | tf_op jit(solution)/shard_map/ppermute | solution.py:259
  187.3 8.8 %collective-permute-done.24 = bf16[64,3072]{1,0:T(8,128)(2,1)S(1)} collective-permute-done((bf16[64,3072]{1,0:T(8,128)(2,1)S(1)}, bf16[64,3072]{1,0:T(8,128)(2,1)S(1)}, u32[]{:S(2)}, u32[]{:S(2)}) %collective-permute-start.24) | collective-permute-done | bytes 393248 | tf_op jit(solution)/shard_map/ppermute | solution.py:259
  196.1 5.0 %collective-permute-done.23 = bf16[64,3072]{1,0:T(8,128)(2,1)S(1)} collective-permute-done((bf16[64,3072]{1,0:T(8,128)(2,1)S(1)}, bf16[64,3072]{1,0:T(8,128)(2,1)S(1)}, u32[]{:S(2)}, u32[]{:S(2)}) %collective-permute-start.23) | collective-permute-done | bytes 393248 | tf_op jit(solution)/shard_map/ppermute | solution.py:259
  201.5 1.0 add_convert_fusion
  (77 shorter events, 4.5 us)
Async XLA Ops:
  0.0 7.3 %copy-start.15 = (bf16[512,384]{1,0:T(8,128)(2,1)S(1)}, bf16[512,384]{1,0:T(8,128)(2,1)}, u32[]{:S(2)}) copy-start(bf16[512,384]{1,0:T(8,128)(2,1)} %param.19) | copy-start | bytes 1179652
  1.3 24.0 %collective-permute-start = (bf16[528,768]{1,0:T(8,128)(2,1)S(1)}, bf16[528,768]{1,0:T(8,128)(2,1)S(1)}, u32[]{:S(2)}, u32[]{:S(2)}) collective-permute-start(bf16[528,768]{1,0:T(8,128)(2,1)S(1)} %maximum_maximum_fusion.refs_1_.refs_2_), channel_id=1, source_target_pairs={{0,16},{16,32},{32,48},{48,64},{64,80},{80,96},{96,112},{112,0},{1... | collective-permute-start | bytes 2433032 | tf_op jit(solution)/shard_map/ppermute | solution.py:259
  3.3 22.0 %collective-permute-start.1 = (bf16[528,768]{1,0:T(8,128)(2,1)S(1)}, bf16[528,768]{1,0:T(8,128)(2,1)}, u32[]{:S(2)}, u32[]{:S(2)}) collective-permute-start(bf16[528,768]{1,0:T(8,128)(2,1)S(1)} %maximum_maximum_fusion.refs_1_.refs_2_), channel_id=1, source_target_pairs={{0,112},{16,0},{32,16},{48,32},{64,48},{80,64},{96,80},{112,96},{1... | collective-permute-start | bytes 2433032 | tf_op jit(solution)/shard_map/ppermute | solution.py:259
  7.3 10.7 %collective-permute-start.2 = (bf16[512,384]{1,0:T(8,128)(2,1)S(1)}, bf16[512,384]{1,0:T(8,128)(2,1)}, u32[]{:S(2)}, u32[]{:S(2)}) collective-permute-start(bf16[512,384]{1,0:T(8,128)(2,1)S(1)} %copy-done.15), channel_id=1, source_target_pairs={{0,128},{128,0},{1,129},{129,1},{2,130},{130,2},{3,131},{131,3},{4... | collective-permute-start | bytes 1179656 | tf_op jit(solution)/shard_map/ppermute | solution.py:259
  10.2 34.5 %collective-permute-start.5 = (bf16[768,768]{1,0:T(8,128)(2,1)}, bf16[768,768]{1,0:T(8,128)(2,1)S(1)}, u32[]{:S(2)}, u32[]{:S(2)}) collective-permute-start(bf16[768,768]{1,0:T(8,128)(2,1)} %constant_dynamic-slice_fusion.1), channel_id=1, source_target_pairs={{0,136},{136,0},{8,128},{128,8},{1,137},{137,1},{9,129},{129,9},{2... | collective-permute-start | bytes 3538952 | tf_op jit(solution)/shard_map/ppermute | solution.py:263
  15.8 72.9 %collective-permute-start.11 = (bf16[768,1536]{1,0:T(8,128)(2,1)}, bf16[768,1536]{1,0:T(8,128)(2,1)S(1)}, u32[]{:S(2)}, u32[]{:S(2)}) collective-permute-start(bf16[768,1536]{1,0:T(8,128)(2,1)} %constant_dynamic-slice_fusion), channel_id=1, source_target_pairs={{0,136},{136,0},{8,128},{128,8},{1,137},{137,1},{9,129},{129,9},{2... | collective-permute-start | bytes 7077896 | tf_op jit(solution)/shard_map/ppermute | solution.py:263
  25.3 20.5 %collective-permute-start.3 = (bf16[528,768]{1,0:T(8,128)(2,1)S(1)}, bf16[528,768]{1,0:T(8,128)(2,1)S(1)}, u32[]{:S(2)}, u32[]{:S(2)}) collective-permute-start(bf16[528,768]{1,0:T(8,128)(2,1)S(1)} %collective-permute-done.refs_1_.refs_3_), channel_id=1, source_target_pairs={{0,16},{16,32},{32,48},{48,64},{64,80},{80,96},{96,112},{112,0},{1... | collective-permute-start | bytes 2433032 | tf_op jit(solution)/shard_map/ppermute | solution.py:259
  25.3 20.5 %collective-permute-start.4 = (bf16[528,768]{1,0:T(8,128)(2,1)}, bf16[528,768]{1,0:T(8,128)(2,1)S(1)}, u32[]{:S(2)}, u32[]{:S(2)}) collective-permute-start(bf16[528,768]{1,0:T(8,128)(2,1)} %collective-permute-done.1.refs_2_.refs_4_), channel_id=1, source_target_pairs={{0,112},{16,0},{32,16},{48,32},{64,48},{80,64},{96,80},{112,96},{1... | collective-permute-start | bytes 2433032 | tf_op jit(solution)/shard_map/ppermute | solution.py:259
  43.6 1.2 copy-start.13
  44.7 14.1 %copy-start.4 = (bf16[768,768]{1,0:T(8,128)(2,1)}, bf16[768,768]{1,0:T(8,128)(2,1)S(1)}, u32[]{:S(2)}) copy-start(bf16[768,768]{1,0:T(8,128)(2,1)S(1)} %collective-permute-done.5.refs_0_) | copy-start | bytes 3538948
  45.7 19.5 %collective-permute-start.6 = (bf16[528,768]{1,0:T(8,128)(2,1)S(1)}, bf16[528,768]{1,0:T(8,128)(2,1)S(1)}, u32[]{:S(2)}, u32[]{:S(2)}) collective-permute-start(bf16[528,768]{1,0:T(8,128)(2,1)S(1)} %collective-permute-done.3.refs_1_.refs_3_), channel_id=1, source_target_pairs={{0,16},{16,32},{32,48},{48,64},{64,80},{80,96},{96,112},{112,0},{1... | collective-permute-start | bytes 2433032 | tf_op jit(solution)/shard_map/ppermute | solution.py:259
  47.9 17.4 %collective-permute-start.7 = (bf16[528,768]{1,0:T(8,128)(2,1)S(1)}, bf16[528,768]{1,0:T(8,128)(2,1)S(1)}, u32[]{:S(2)}, u32[]{:S(2)}) collective-permute-start(bf16[528,768]{1,0:T(8,128)(2,1)S(1)} %collective-permute-done.4.refs_2_.refs_4_), channel_id=1, source_target_pairs={{0,112},{16,0},{32,16},{48,32},{64,48},{80,64},{96,80},{112,96},{1... | collective-permute-start | bytes 2433032 | tf_op jit(solution)/shard_map/ppermute | solution.py:259
  49.0 39.8 %collective-permute-start.10 = (bf16[768,768]{1,0:T(8,128)(2,1)S(1)}, bf16[768,768]{1,0:T(8,128)(2,1)S(1)}, u32[]{:S(2)}, u32[]{:S(2)}) collective-permute-start(bf16[768,768]{1,0:T(8,128)(2,1)S(1)} %collective-permute-done.5.refs_0_), channel_id=1, source_target_pairs={{0,128},{128,0},{1,129},{129,1},{2,130},{130,2},{3,131},{131,3},{4... | collective-permute-start | bytes 3538952 | tf_op jit(solution)/shard_map/ppermute | solution.py:259
  49.4 1.4 copy-start.14
  65.3 11.6 %collective-permute-start.8 = (bf16[272,768]{1,0:T(8,128)(2,1)S(1)}, bf16[272,768]{1,0:T(8,128)(2,1)S(1)}, u32[]{:S(2)}, u32[]{:S(2)}) collective-permute-start(bf16[272,768]{1,0:T(8,128)(2,1)S(1)} %slice.34), channel_id=1, source_target_pairs={{0,16},{16,32},{32,48},{48,64},{64,80},{80,96},{96,112},{112,0},{1... | collective-permute-start | bytes 1253384 | tf_op jit(solution)/shard_map/ppermute | solution.py:259
  67.2 9.7 %collective-permute-start.9 = (bf16[256,768]{1,0:T(8,128)(2,1)S(1)}, bf16[256,768]{1,0:T(8,128)(2,1)S(1)}, u32[]{:S(2)}, u32[]{:S(2)}) collective-permute-start(bf16[256,768]{1,0:T(8,128)(2,1)S(1)} %slice.35), channel_id=1, source_target_pairs={{0,112},{16,0},{32,16},{48,32},{64,48},{80,64},{96,80},{112,96},{1... | collective-permute-start | bytes 1179656 | tf_op jit(solution)/shard_map/ppermute | solution.py:259
  76.9 21.8 %copy-start.1 = (bf16[384,3072]{1,0:T(8,128)(2,1)S(1)}, bf16[384,3072]{1,0:T(8,128)(2,1)}, u32[]{:S(2)}) copy-start(bf16[384,3072]{1,0:T(8,128)(2,1)} %weight_ref.1) | copy-start | bytes 7077892
  88.7 13.2 %copy-start.2 = (bf16[768,1536]{1,0:T(8,128)(2,1)}, bf16[768,1536]{1,0:T(8,128)(2,1)S(1)}, u32[]{:S(2)}) copy-start(bf16[768,1536]{1,0:T(8,128)(2,1)S(1)} %collective-permute-done.11.refs_4_) | copy-start | bytes 7077892
  88.8 13.2 %copy-start.6 = (bf16[768,768]{1,0:T(8,128)(2,1)}, bf16[768,768]{1,0:T(8,128)(2,1)S(1)}, u32[]{:S(2)}) copy-start(bf16[768,768]{1,0:T(8,128)(2,1)S(1)} %collective-permute-done.10.refs_1_) | copy-start | bytes 3538948
  88.8 10.0 %collective-permute-start.12 = (bf16[512,384]{1,0:T(8,128)(2,1)S(1)}, bf16[512,384]{1,0:T(8,128)(2,1)S(1)}, u32[]{:S(2)}, u32[]{:S(2)}) collective-permute-start(bf16[512,384]{1,0:T(8,128)(2,1)S(1)} %slice.36), channel_id=1, source_target_pairs={{0,128},{128,0},{1,129},{129,1},{2,130},{130,2},{3,131},{131,3},{4... | collective-permute-start | bytes 1179656 | tf_op jit(solution)/shard_map/ppermute | solution.py:259
  91.0 7.8 %collective-permute-start.13 = (f32[3,1,512]{2,1,0:T(1,128)S(1)}, f32[3,1,512]{2,1,0:T(1,128)S(1)}, u32[]{:S(2)}, u32[]{:S(2)}) collective-permute-start(f32[3,1,512]{2,1,0:T(1,128)S(1)} %slice.37), channel_id=1, source_target_pairs={{0,128},{128,0},{1,129},{129,1},{2,130},{130,2},{3,131},{131,3},{4... | collective-permute-start | bytes 18440 | tf_op jit(solution)/shard_map/ppermute | solution.py:259
  101.9 1.6 copy-start
  103.6 7.2 %copy-start.18 = (f32[768]{0:T(1024)S(1)}, f32[768]{0:T(1024)}, u32[]{:S(2)}) copy-start(f32[768]{0:T(1024)} %param.32) | copy-start | bytes 9220
  103.6 43.9 %copy-start.8 = (bf16[64,3072]{1,0:T(8,128)(2,1)S(1)}, bf16[64,3072]{1,0:T(8,128)(2,1)}, u32[]{:S(2)}) copy-start(bf16[64,3072]{1,0:T(8,128)(2,1)} %residual_ref.1) | copy-start | bytes 1179652
  103.6 43.9 %copy-start.9 = (f32[3072]{0:T(1024)S(1)}, f32[3072]{0:T(1024)}, u32[]{:S(2)}) copy-start(f32[3072]{0:T(1024)} %param.27) | copy-start | bytes 36868
  103.6 43.9 %all-to-all-start = ((bf16[8,64,3072]{2,1,0:T(8,128)(2,1)}), bf16[8,64,3072]{2,1,0:T(8,128)(2,1)S(1)}, u32[]{:S(2)}, u32[]{:S(2)}) async-start(bf16[8,64,3072]{2,1,0:T(8,128)(2,1)} %bitcast.5), calls=%async_computation | async-start | bytes 6291456 | tf_op jit(solution)/shard_map/all_to_all | solution.py:345
  110.2 8.3 %collective-permute-start.16 = (bf16[768,1536]{1,0:T(8,128)(2,1)}, bf16[768,1536]{1,0:T(8,128)(2,1)}, u32[]{:S(2)}, u32[]{:S(2)}) collective-permute-start(bf16[768,1536]{1,0:T(8,128)(2,1)} %copy-done.2), channel_id=1, source_target_pairs={{0,1},{1,0},{2,3},{3,2},{4,5},{5,4},{6,7},{7,6},{8,9},{9,8},{10,11... | collective-permute-start | bytes 7077896 | tf_op jit(solution)/shard_map/ppermute | solution.py:259
  110.2 6.6 %collective-permute-start.14 = (bf16[768,768]{1,0:T(8,128)(2,1)}, bf16[768,768]{1,0:T(8,128)(2,1)}, u32[]{:S(2)}, u32[]{:S(2)}) collective-permute-start(bf16[768,768]{1,0:T(8,128)(2,1)} %copy-done.4), channel_id=1, source_target_pairs={{0,1},{1,0},{2,3},{3,2},{4,5},{5,4},{6,7},{7,6},{8,9},{9,8},{10,11... | collective-permute-start | bytes 3538952 | tf_op jit(solution)/shard_map/ppermute | solution.py:259
  110.7 7.7 %collective-permute-start.15 = (bf16[768,768]{1,0:T(8,128)(2,1)}, bf16[768,768]{1,0:T(8,128)(2,1)}, u32[]{:S(2)}, u32[]{:S(2)}) collective-permute-start(bf16[768,768]{1,0:T(8,128)(2,1)} %copy-done.6), channel_id=1, source_target_pairs={{0,1},{1,0},{2,3},{3,2},{4,5},{5,4},{6,7},{7,6},{8,9},{9,8},{10,11... | collective-permute-start | bytes 3538952 | tf_op jit(solution)/shard_map/ppermute | solution.py:259
  110.8 4.6 %collective-permute-start.17 = (f32[768]{0:T(1024)S(1)}, f32[768]{0:T(1024)}, u32[]{:S(2)}, u32[]{:S(2)}) collective-permute-start(f32[768]{0:T(1024)S(1)} %copy-done.18), channel_id=1, source_target_pairs={{0,136},{136,0},{8,128},{128,8},{1,137},{137,1},{9,129},{129,9},{2... | collective-permute-start | bytes 9224 | tf_op jit(solution)/shard_map/ppermute | solution.py:263
  147.5 0.7 copy-start.10
  148.2 0.7 copy-start.11
  148.9 0.7 copy-start.12
  149.6 5.0 %copy-start.19 = (s32[8]{0:T(128)S(1)}, s32[8]{0:T(128)}, u32[]{:S(2)}) copy-start(s32[8]{0:T(128)} %constant.28.clone) | copy-start | bytes 100
  149.6 5.0 %copy-start.20 = (s32[8]{0:T(128)S(1)}, s32[8]{0:T(128)}, u32[]{:S(2)}) copy-start(s32[8]{0:T(128)} %constant.27.clone) | copy-start | bytes 100
  149.6 5.0 %copy-start.21 = (s32[8]{0:T(128)S(1)}, s32[8]{0:T(128)}, u32[]{:S(2)}) copy-start(s32[8]{0:T(128)} %constant.26.clone) | copy-start | bytes 100
  149.6 20.6 %copy-start.7 = (bf16[768,768]{1,0:T(8,128)(2,1)S(1)}, bf16[768,768]{1,0:T(8,128)(2,1)}, u32[]{:S(2)}) copy-start(bf16[768,768]{1,0:T(8,128)(2,1)} %copy-done.6) | copy-start | bytes 3538948
  151.2 12.0 %collective-permute-start.18 = (bf16[64,3072]{1,0:T(8,128)(2,1)S(1)}, bf16[64,3072]{1,0:T(8,128)(2,1)S(1)}, u32[]{:S(2)}, u32[]{:S(2)}) collective-permute-start(bf16[64,3072]{1,0:T(8,128)(2,1)S(1)} %get-tuple-element.89), channel_id=1, source_target_pairs={{0,2},{2,4},{4,6},{6,0},{1,3},{3,5},{5,7},{7,1},{8,10},{10,12},{12... | collective-permute-start | bytes 1179656 | tf_op jit(solution)/shard_map/ppermute | solution.py:259
  152.2 11.1 %collective-permute-start.19 = (bf16[64,3072]{1,0:T(8,128)(2,1)S(1)}, bf16[64,3072]{1,0:T(8,128)(2,1)S(1)}, u32[]{:S(2)}, u32[]{:S(2)}) collective-permute-start(bf16[64,3072]{1,0:T(8,128)(2,1)S(1)} %get-tuple-element.89), channel_id=1, source_target_pairs={{0,6},{2,0},{4,2},{6,4},{1,7},{3,1},{5,3},{7,5},{8,14},{10,8},{12,... | collective-permute-start | bytes 1179656 | tf_op jit(solution)/shard_map/ppermute | solution.py:259
  155.3 15.0 %copy-start.5 = (bf16[768,768]{1,0:T(8,128)(2,1)S(1)}, bf16[768,768]{1,0:T(8,128)(2,1)}, u32[]{:S(2)}) copy-start(bf16[768,768]{1,0:T(8,128)(2,1)} %copy-done.4) | copy-start | bytes 3538948
  155.3 15.0 %copy-start.3 = (bf16[768,1536]{1,0:T(8,128)(2,1)S(1)}, bf16[768,1536]{1,0:T(8,128)(2,1)}, u32[]{:S(2)}) copy-start(bf16[768,1536]{1,0:T(8,128)(2,1)} %copy-done.2) | copy-start | bytes 7077892
  163.2 7.0 %collective-permute-start.20 = (bf16[32,3072]{1,0:T(8,128)(2,1)S(1)}, bf16[32,3072]{1,0:T(8,128)(2,1)S(1)}, u32[]{:S(2)}, u32[]{:S(2)}) collective-permute-start(bf16[32,3072]{1,0:T(8,128)(2,1)S(1)} %slice.44), channel_id=1, source_target_pairs={{0,2},{2,4},{4,6},{6,0},{1,3},{3,5},{5,7},{7,1},{8,10},{10,12},{12... | collective-permute-start | bytes 589832 | tf_op jit(solution)/shard_map/ppermute | solution.py:259
  163.3 6.9 %collective-permute-start.21 = (bf16[32,3072]{1,0:T(8,128)(2,1)S(1)}, bf16[32,3072]{1,0:T(8,128)(2,1)S(1)}, u32[]{:S(2)}, u32[]{:S(2)}) collective-permute-start(bf16[32,3072]{1,0:T(8,128)(2,1)S(1)} %slice.45), channel_id=1, source_target_pairs={{0,6},{2,0},{4,2},{6,4},{1,7},{3,1},{5,3},{7,5},{8,14},{10,8},{12,... | collective-permute-start | bytes 589832 | tf_op jit(solution)/shard_map/ppermute | solution.py:259
  182.4 19.1 %copy-start.16 = (f32[3072]{0:T(1024)S(1)}, f32[3072]{0:T(1024)}, u32[]{:S(2)}) copy-start(f32[3072]{0:T(1024)} %param.34) | copy-start | bytes 36868
  182.4 19.1 %copy-start.17 = (f32[3072]{0:T(1024)S(1)}, f32[3072]{0:T(1024)}, u32[]{:S(2)}) copy-start(f32[3072]{0:T(1024)} %param.28) | copy-start | bytes 36868
  182.5 13.6 %collective-permute-start.24 = (bf16[64,3072]{1,0:T(8,128)(2,1)S(1)}, bf16[64,3072]{1,0:T(8,128)(2,1)S(1)}, u32[]{:S(2)}, u32[]{:S(2)}) collective-permute-start(bf16[64,3072]{1,0:T(8,128)(2,1)S(1)} %get-tuple-element.98), channel_id=1, source_target_pairs={{0,4},{2,6},{4,0},{6,2},{1,5},{3,7},{5,1},{7,3},{8,12},{10,14},{12... | collective-permute-start | bytes 1179656 | tf_op jit(solution)/shard_map/ppermute | solution.py:259
  184.1 17.0 %collective-permute-start.23 = (bf16[64,3072]{1,0:T(8,128)(2,1)S(1)}, bf16[64,3072]{1,0:T(8,128)(2,1)S(1)}, u32[]{:S(2)}, u32[]{:S(2)}) collective-permute-start(bf16[64,3072]{1,0:T(8,128)(2,1)S(1)} %get-tuple-element.99), channel_id=1, source_target_pairs={{0,2},{2,4},{4,6},{6,0},{1,3},{3,5},{5,7},{7,1},{8,10},{10,12},{12... | collective-permute-start | bytes 1179656 | tf_op jit(solution)/shard_map/ppermute | solution.py:259
  186.7 14.8 %collective-permute-start.22 = (bf16[64,3072]{1,0:T(8,128)(2,1)S(1)}, bf16[64,3072]{1,0:T(8,128)(2,1)S(1)}, u32[]{:S(2)}, u32[]{:S(2)}) collective-permute-start(bf16[64,3072]{1,0:T(8,128)(2,1)S(1)} %get-tuple-element.97), channel_id=1, source_target_pairs={{0,6},{2,0},{4,2},{6,4},{1,7},{3,1},{5,3},{7,5},{8,14},{10,8},{12,... | collective-permute-start | bytes 1179656 | tf_op jit(solution)/shard_map/ppermute | solution.py:259
where the time goes:
time: 204 us; the launch traced here: 203 us
  waiting for transfers between devices  90.7 us (44%)
  Pallas kernels  52.4 us (26%)
  starting transfers between devices  42.7 us (21%)
  local copies, waits for them, and re-layouts  14.1 us (7%)
  other arithmetic  2.32 us (1%)
    ppermute x22, waiting for transfers between devices, shift(): lax.ppermute(array, axis, [(i, (i + by) % size) for i in range(size)])  53.2 us
    pallas_call x5, Pallas kernels, attend(): pl.pallas_call(functools.partial(attend_body, len(ks), first, last), grid...  35.5 us
    ppermute x22, starting transfers between devices, shift(): lax.ppermute(array, axis, [(i, (i + by) % size) for i in range(size)])  31.4 us
    all_to_all x1, waiting for transfers between devices, shards(): lax.all_to_all(terms.reshape(8, row_block, d_model), ('yh', 'x'), split_a...  29 us
    pallas_call x1, Pallas kernels, mlp(): pl.pallas_call(mlp_body, grid_spec=pltpu.PrefetchScalarGridSpec(num_scala...  12.1 us
    ppermute x3, waiting for transfers between devices, cross(): return lax.ppermute(array, ('yl', 'yh'), [(0, 3), (3, 0), (1, 2), (2, 1)])  8.45 us
    all_to_all x1, starting transfers between devices, shards(): lax.all_to_all(terms.reshape(8, row_block, d_model), ('yh', 'x'), split_a...  6.62 us
    unnamed x49, local copies, waits for them, and re-layouts  6.5 us
  transfers between devices with their start and end apart: 26, of which 15 were waited for; matrix products, arithmetic and copies ran while one was open for 4% of the time, Pallas kernels for 18%

commit v1 on v0

--- a/solution.py
+++ b/solution.py
@@ -13,6 +13,33 @@
 SCORE_TO_LOG2 = LOG2E / math.sqrt(HD)
 
 FINE = (("yl", 2), ("z", 8), ("yh", 2), ("x", 4), ("dp", 2))
+
+
+def store_part(o_ref, part, lse):
+    h = pl.program_id(1)
+    terms = []
+    rest = lse
+    for _ in range(3):
+        terms.append(rest.astype(jnp.bfloat16).astype(jnp.float32))
+        rest = rest - terms[-1]
+    row = lax.broadcasted_iota(jnp.int32, (HD, lse.shape[1]), 0) - 3 * h
+    stats = jnp.zeros((HD, lse.shape[1]), jnp.float32)
+    for k, term in enumerate(terms):
+        stats = jnp.where(row == k, term, stats)
+    stats = stats.T.astype(jnp.bfloat16)
+    _, x_size, yh_size, rows, width = o_ref.shape
+    for x in range(x_size):
+        for yh in range(yh_size):
+            at = slice((yh * x_size + x) * rows, (yh * x_size + x + 1) * rows)
+            o_ref[0, x, yh, :, pl.ds(pl.multiple_of(h * HD, HD), HD)] = part[at]
+
+            @pl.when(h == 0)
+            def _(x=x, yh=yh, at=at):
+                o_ref[0, x, yh, :, width - HD :] = stats[at]
+
+            @pl.when(h > 0)
+            def _(x=x, yh=yh, at=at):
+                o_ref[0, x, yh, :, width - HD :] += stats[at]
 
 
 def attend_body(pieces, first, last, *refs):
@@ -51,9 +78,7 @@
         den = den + factor * l_in[0]
         acc = acc + factor * acc_in[...]
     if last:
-        o_ref, lse_ref = outs
-        o_ref[...] = (acc / den).T.astype(jnp.bfloat16)
-        lse_ref[0] = m * SCORE_TO_LOG2 + jnp.log2(den)
+        store_part(outs[0], (acc / den).T.astype(jnp.bfloat16), m * SCORE_TO_LOG2 + jnp.log2(den))
     else:
         m_out, l_out, acc_out = outs
         m_out[0] = m
@@ -61,27 +86,31 @@
         acc_out[...] = acc
 
 
-def attend(q, pairs, state, last, block=512):
+def attend(q, pairs, state, last=None, block=512):
     rows, width = q.shape
     heads = width // HD
     ks = vs = pairs
     first = state is None
-    q_spec = pl.BlockSpec((block, HD), lambda h, j: (j, h))
-    k_specs = [pl.BlockSpec((k.shape[0], HD), lambda h, j: (0, h)) for k in ks]
-    v_specs = [pl.BlockSpec((v.shape[0], HD), lambda h, j: (0, heads + h)) for v in vs]
-    stat = pl.BlockSpec((1, 1, block), lambda h, j: (h, 0, j))
-    acc = pl.BlockSpec((HD, block), lambda h, j: (h, j))
-    stat_shape = jax.ShapeDtypeStruct((heads, 1, rows), jnp.float32)
     if last:
-        out_specs = [q_spec, stat]
-        out_shape = [jax.ShapeDtypeStruct((rows, width), jnp.bfloat16), stat_shape]
+        grid, at = (rows // block, heads), lambda f: lambda j, h: f(h, j)
     else:
+        grid, at = (heads, rows // block), lambda f: f
+    q_spec = pl.BlockSpec((block, HD), at(lambda h, j: (j, h)))
+    k_specs = [pl.BlockSpec((k.shape[0], HD), at(lambda h, j: (0, h))) for k in ks]
+    v_specs = [pl.BlockSpec((v.shape[0], HD), at(lambda h, j: (0, heads + h))) for v in vs]
+    stat = pl.BlockSpec((1, 1, block), at(lambda h, j: (h, 0, j)))
+    acc = pl.BlockSpec((HD, block), at(lambda h, j: (h, j)))
+    if last:
+        out_specs = [pl.BlockSpec((1, *last[1:]), at(lambda h, j: (j, 0, 0, 0, 0)))]
+        out_shape = [jax.ShapeDtypeStruct(last, jnp.bfloat16)]
+    else:
+        stat_shape = jax.ShapeDtypeStruct((heads, 1, rows), jnp.float32)
         out_specs = [stat, stat, acc]
         out_shape = [stat_shape, stat_shape, jax.ShapeDtypeStruct((width, rows), jnp.float32)]
     keys = sum(k.shape[0] for k in ks)
     return pl.pallas_call(
-        functools.partial(attend_body, len(ks), first, last),
-        grid=(heads, rows // block),
+        functools.partial(attend_body, len(ks), first, bool(last)),
+        grid=grid,
         in_specs=[q_spec, *k_specs, *v_specs, *(() if first else (stat, stat, acc))],
         out_specs=out_specs,
         out_shape=out_shape,
@@ -94,72 +123,102 @@
     )(q, *ks, *vs, *(() if first else state))
 
 
-def join_project_body(part_ref, other_ref, lse_ref, lse_other_ref, weight_ref, out_ref):
-    pieces = []
-    for h in range(part_ref.shape[1] // HD):
-        cols = slice(h * HD, (h + 1) * HD)
-        share = 1.0 / (1.0 + jnp.exp2(lse_other_ref[h] - lse_ref[h]))
-        share = jnp.broadcast_to(share, (HD, share.shape[1])).T
-        own = part_ref[:, cols].astype(jnp.float32)
-        other = other_ref[:, cols].astype(jnp.float32)
-        pieces.append((other + share * (own - other)).astype(jnp.bfloat16))
-    attended = jnp.concatenate(pieces, axis=1)
-    out_ref[...] = jnp.dot(
-        attended, weight_ref[...], preferred_element_type=jnp.float32
-    ).astype(jnp.bfloat16)
-
-
-def join_project(part, other, lse, lse_other, weight, block=768):
-    rows, width = other.shape
-    cols = weight.shape[1]
-    first = pl.BlockSpec((rows, width), lambda j: (0, 0))
-    stat = pl.BlockSpec((lse.shape[0], 1, rows), lambda j: (0, 0, 0))
+def join_project_body(order, yh, part_ref, mine_ref, mate_ref, own_ref, away_ref, attended):
+    i = pl.program_id(0)
+    x_size = part_ref.shape[0] // 2
+    rows = part_ref.shape[1] // 2
+    width = part_ref.shape[2] - HD
+
+    @pl.when(i == 0)
+    def _():
+        for side in range(2):
+            at = pl.ds(pl.multiple_of((yh[0] if side == 0 else 1 - yh[0]) * rows, rows), rows)
+            for x in range(x_size):
+                a = part_ref[x, at, :].astype(jnp.float32)
+                b = part_ref[x_size + x, at, :].astype(jnp.float32)
+                for h in range(width // HD):
+                    k = width + 3 * h
+                    lse_a = a[:, k : k + 1] + a[:, k + 1 : k + 2] + a[:, k + 2 : k + 3]
+                    lse_b = b[:, k : k + 1] + b[:, k + 1 : k + 2] + b[:, k + 2 : k + 3]
+                    share = 1.0 / (1.0 + jnp.exp2(lse_b - lse_a))
+                    cols = slice(h * HD, (h + 1) * HD)
+                    joined = b[:, cols] + share * (a[:, cols] - b[:, cols])
+                    attended[
+                        side * rows : (side + 1) * rows, x * width + h * HD : x * width + (h + 1) * HD
+                    ] = joined.astype(jnp.bfloat16)
+
+    def project(weight_ref):
+        out = jnp.dot(attended[...], weight_ref[...], preferred_element_type=jnp.float32)
+        own_ref[...] = out[:rows]
+        away_ref[...] = out[rows:].astype(jnp.bfloat16)
+
+    @pl.when(i < 2)
+    def _():
+        project(mine_ref)
+
+    @pl.when(i >= 2)
+    def _():
+        project(mate_ref)
+
+
+def join_project(parts, mine, mate, order, yh):
+    n, both, wide = parts.shape
+    k, half = mine.shape
+    block, rows = half // 2, both // 2
+    out = pl.BlockSpec((rows, block), lambda i, order, yh: (0, order[i]))
     return pl.pallas_call(
         join_project_body,
-        grid=(cols // block,),
-        in_specs=[first, first, stat, stat, pl.BlockSpec((width, block), lambda j: (0, j))],
-        out_specs=pl.BlockSpec((rows, block), lambda j: (0, j)),
-        out_shape=jax.ShapeDtypeStruct((rows, cols), jnp.bfloat16),
+        grid_spec=pltpu.PrefetchScalarGridSpec(
+            num_scalar_prefetch=2,
+            grid=(4,),
+            in_specs=[
+                pl.BlockSpec((n, both, wide), lambda i, order, yh: (0, 0, 0)),
+                pl.BlockSpec((k, block), lambda i, order, yh: (0, jnp.minimum(i, 1))),
+                pl.BlockSpec((k, block), lambda i, order, yh: (0, jnp.maximum(i - 2, 0))),
+            ],
+            out_specs=[out, out],
+            scratch_shapes=[pltpu.VMEM((both, k), jnp.bfloat16)],
+        ),
+        out_shape=[
+            jax.ShapeDtypeStruct((rows, 2 * half), jnp.float32),
+            jax.ShapeDtypeStruct((rows, 2 * half), jnp.bfloat16),
+        ],
         cost_estimate=pl.CostEstimate(
-            flops=2 * rows * width * cols, transcendentals=0, bytes_accessed=2 * width * cols
-        ),
-        compiler_params=pltpu.CompilerParams(vmem_limit_bytes=32 << 20),
-    )(part, other, lse, lse_other, weight)
-
-
-def stream_norm_body(
-    terms_ref, residual_ref, gate_ref, bias_ref, scale_ref, shift_ref, stream_ref, normed_ref
-):
-    proj = terms_ref[0].astype(jnp.float32)
-    for g in range(1, terms_ref.shape[0]):
-        proj = proj + terms_ref[g].astype(jnp.float32)
-    stream = residual_ref[...].astype(jnp.float32) + gate_ref[...] * (proj + bias_ref[...])
+            flops=4 * both * k * half, transcendentals=0, bytes_accessed=4 * k * half
+        ),
+        compiler_params=pltpu.CompilerParams(vmem_limit_bytes=40 << 20),
+    )(order, yh, parts, mine, mate)
+
+
+def stream_norm_body(own_ref, other_ref, residual_ref, vectors_ref, stream_ref, normed_ref):
+    gate, bias, scale, shift_by = (vectors_ref[i : i + 1, :] for i in range(4))
+    proj = own_ref[...] + other_ref[...].astype(jnp.float32)
+    stream = residual_ref[...].astype(jnp.float32) + gate * (proj + bias)
     center = jnp.mean(stream, axis=-1, keepdims=True)
     off = stream - center
     spread = jnp.mean(off * off, axis=-1, keepdims=True)
-    normed = off * lax.rsqrt(spread + 1e-06) * (1.0 + scale_ref[...]) + shift_ref[...]
+    normed = off * lax.rsqrt(spread + 1e-06) * (1.0 + scale) + shift_by
     stream_ref[...] = stream
     normed_ref[...] = normed.astype(jnp.bfloat16)
 
 
-def stream_norm(terms, residual, gate, bias, scale, shift_by, block=16):
-    groups, rows, d_model = terms.shape
+def stream_norm(own, other, residual, vectors, block=16):
+    rows, d_model = own.shape
     row = pl.BlockSpec((block, d_model), lambda i: (i, 0))
-    vec = pl.BlockSpec((1, d_model), lambda i: (0, 0))
     return pl.pallas_call(
         stream_norm_body,
         grid=(rows // block,),
-        in_specs=[pl.BlockSpec((groups, block, d_model), lambda i: (0, i, 0)), row, vec, vec, vec, vec],
+        in_specs=[row, row, row, pl.BlockSpec(vectors.shape, lambda i: (0, 0))],
         out_specs=[row, row],
         out_shape=[
             jax.ShapeDtypeStruct((rows, d_model), jnp.float32),
             jax.ShapeDtypeStruct((rows, d_model), jnp.bfloat16),
         ],
         cost_estimate=pl.CostEstimate(
-            flops=20 * rows * d_model, transcendentals=0, bytes_accessed=24 * rows * d_model
+            flops=20 * rows * d_model, transcendentals=0, bytes_accessed=14 * rows * d_model
         ),
         compiler_params=pltpu.CompilerParams(vmem_limit_bytes=32 << 20),
-    )(terms, residual, *(v.reshape(1, -1) for v in (gate, bias, scale, shift_by)))
+    )(own, other, residual, vectors)
 
 
 def mlp_body(order, x_ref, up_ref, down_ref, bias_ref, bias_far_ref, *refs):
@@ -297,12 +356,14 @@
     down_weight,
     down_bias,
 ):
-    yl_at, core = lax.axis_index("yl"), lax.axis_index("dp")
-    rows_own = img_query.shape[0]
+    yl_at, yh_at, core = lax.axis_index("yl"), lax.axis_index("yh"), lax.axis_index("dp")
+    rows_own, width = img_query.shape
     row_block, d_model = residual_in.shape
 
     up_a = cross(part_of(up_weight, 4, yl_at * 2 + core, 0))
     down_a = cross(part_of(down_weight, 2, core, 1))
+    out_mine = lax.all_gather(part_of(out_weight, 2, core, 1), "x", axis=0, tiled=True)
+    vectors = jnp.stack([gate_attn, out_bias, mod_scale, mod_shift])
     order = jnp.bitwise_xor(
         jnp.array([2, 2, 2, 2, 0, 0, 0, 0], jnp.int32) * (1 - yl_at)
         + core * jnp.array([1, 1, 1, 1, 2, 2, 2, 2], jnp.int32),
@@ -324,32 +385,37 @@
 
     one = around(own, own)
     one, q_other = tie((one, q_other))
-    queries = jnp.concatenate([img_query, q_other], axis=0)
+    queries = jnp.where(
+        yl_at == 0,
+        jnp.concatenate([img_query, q_other], axis=0),
+        jnp.concatenate([q_other, img_query], axis=0),
+    )
     two = around(*one)
-    state = attend(queries, [own], None, False)
-    state = attend(queries, one, state, False)
+    state = attend(queries, [own], None)
+    state = attend(queries, one, state)
     two, state, up_a = tie((two, state, up_a))
     three = around(*two)
     up_b = shift(up_a, "yl", 2, 1)
-    state = attend(queries, two, state, False)
+    state = attend(queries, two, state)
     three, state = tie((three, state))
     four = around(three[0][:cut], three[1][cut:])
-    state = attend(queries, three, state, False)
+    state = attend(queries, three, state)
     four, state = tie((four, state))
-    part, lse = attend(queries, four, state, True)
-    part, up_b, down_a = tie((part, up_b, down_a))
-
-    part_other = shift(part[rows_own:], "yl", 2, 1)
-    lse_other = shift(lse[:, :, rows_own:], "yl", 2, 1)
-    terms = join_project(part, part_other, lse, lse_other, out_weight)
-    terms = lax.all_to_all(
-        terms.reshape(8, row_block, d_model), ("yh", "x"), split_axis=0, concat_axis=0, tiled=True
+    shape = (2, 4, 2, row_block, width + HD)
+    (part,) = attend(queries, four, state, shape)
+    part, up_b, out_mine, down_a = tie((part, up_b, out_mine, down_a))
+    out_mate = shift(out_mine, "dp", 2, 1)
+
+    parts = lax.all_to_all(
+        part.reshape(8, 2 * row_block, width + HD), ("yl", "x"), split_axis=0, concat_axis=0, tiled=True
     )
+    proj_own, proj_away = join_project(parts, out_mine, out_mate, order[4:], yh_at.reshape(1))
+    proj_other = shift(proj_away, "yh", 2, 1)
     up_far = [up_a, up_b, shift(up_a, "dp", 2, 1), shift(up_b, "dp", 2, 1)]
     down_far = [down_a, shift(down_a, "dp", 2, 1)]
     bias_far = cross(up_bias)
-    terms, up_far, down_far, bias_far = tie((terms, up_far, down_far, bias_far))
-    stream, normed = stream_norm(terms, residual_in, gate_attn, out_bias, mod_scale, mod_shift)
+    proj_other, up_far, down_far, bias_far = tie((proj_other, up_far, down_far, bias_far))
+    stream, normed = stream_norm(proj_own, proj_other, residual_in, vectors)
     everyone = jnp.concatenate(gather_x(normed), axis=0)
     out = mlp(everyone, up_weight, down_weight, up_bias, bias_far, up_far, down_far, order)
     blocks = out.reshape(4, row_block, d_model)

time: 204 us -> 203 us (level)
  waiting for transfers between devices: 90.7 us -> 71.1 us
  between operations: 0.33 us -> 13.7 us
  Pallas kernels: 52.4 us -> 59.9 us
  local copies, waits for them, and re-layouts: 14.1 us -> 11.4 us
    all_to_all x1, waiting for transfers between devices: 29 us -> 13.9 us  [shards(): lax.all_to_all(part.reshape(8, 2 * row_block, width + HD), ('yl', 'x'), s...]
    pallas_call x7, Pallas kernels: 40.3 us -> 47.1 us  [the longest x5 39.2 us: attend(): pl.pallas_call(functools.partial(attend_body, len(ks), first, bool(last))...]
    ppermute x22, waiting for transfers between devices: 53.2 us -> 50 us  [shift(): lax.ppermute(array, axis, [(i, (i + by) % size) for i in range(size)])]
    unnamed x49 -> x42, local copies, waits for them, and re-layouts: 6.5 us -> 4.34 us
    dynamic_slice x2 -> x3, local copies, waits for them, and re-layouts: 5.64 us -> 6.76 us  [part_of(): return lax.dynamic_slice_in_dim(array, index * n, n, axis)]
  transfers between devices with their start and end apart: 26 -> 27, of which waited for: 15 -> 12; matrix products, arithmetic and copies ran while one was open for 4% -> 4% of each run, Pallas kernels for 18% -> 23%
where the time goes in v1:
time: 203 us; the launch traced here: 201 us
  waiting for transfers between devices  71.1 us (35%)
  Pallas kernels  59.9 us (30%)
  starting transfers between devices  41.7 us (21%)
  between operations  13.7 us (7%)
  local copies, waits for them, and re-layouts  11.4 us (6%)
  other arithmetic  3.61 us (2%)
    ppermute x22, waiting for transfers between devices, shift(): lax.ppermute(array, axis, [(i, (i + by) % size) for i in range(size)])  50 us
    pallas_call x5, Pallas kernels, attend(): pl.pallas_call(functools.partial(attend_body, len(ks), first, bool(last))...  39.2 us
    ppermute x22, starting transfers between devices, shift(): lax.ppermute(array, axis, [(i, (i + by) % size) for i in range(size)])  32.4 us
    all_to_all x1, waiting for transfers between devices, shards(): lax.all_to_all(part.reshape(8, 2 * row_block, width + HD), ('yl', 'x'), s...  13.9 us
    pallas_call x1, Pallas kernels, mlp(): pl.pallas_call(mlp_body, grid_spec=pltpu.PrefetchScalarGridSpec(num_scala...  12.9 us
    ppermute x3, waiting for transfers between devices, cross(): return lax.ppermute(array, ('yl', 'yh'), [(0, 3), (3, 0), (1, 2), (2, 1)])  7.13 us
    dynamic_slice x3, local copies, waits for them, and re-layouts, part_of(): return lax.dynamic_slice_in_dim(array, index * n, n, axis)  6.76 us
    pallas_call x1, Pallas kernels, join_project(): pl.pallas_call(join_project_body, grid_spec=pltpu.PrefetchScalarGridSpec(...  6.76 us
  transfers between devices with their start and end apart: 27, of which 12 were waited for; matrix products, arithmetic and copies ran while one was open for 4% of the time, Pallas kernels for 23%

profile of v1, /device:TPU:8, one launch (start us, length us, event | category | flops | bytes accessed | tf_op | source)
XLA Modules:
  0.0 201.4 jit_solution(2615438393709066887)
XLA Ops:
  6.5 1.7 copy-done
  8.2 1.2 constant_dynamic-slice_fusion.1
  9.4 0.2 copy-done.6
  9.6 1.0 maximum_maximum_fusion.refs_1_.refs_2_
  10.6 1.9 collective-permute-start
  12.5 3.9 %collective-permute-start.1 = (bf16[528,768]{1,0:T(8,128)(2,1)}, bf16[528,768]{1,0:T(8,128)(2,1)}, u32[]{:S(2)}, u32[]{:S(2)}) collective-permute-start(bf16[528,768]{1,0:T(8,128)(2,1)} %maximum_maximum_fusion.refs_1_.refs_2_), channel_id=1, source_target_pairs={{0,112},{16,0},{32,16},{48,32},{64,48},{80,64},{96,80},{112,96},{1... | collective-permute-start | bytes 2433032 | tf_op jit(solution)/shard_map/ppermute | solution.py:318
  16.5 0.4 collective-permute-start.2
  16.9 2.4 %constant_dynamic-slice_fusion.2 = bf16[768,768]{1,0:T(8,128)(2,1)} fusion(bf16[3072,768]{1,0:T(8,128)(2,1)} %up_ref.1, s32[]{:T(128)S(6)} %select_n.17), kind=kLoop, calls=%fused_computation.11 | loop fusion | bytes 2359300 | tf_op jit(solution)/shard_map/dynamic_slice | solution.py:327
  19.3 2.4 %collective-permute-start.5 = (bf16[768,768]{1,0:T(8,128)(2,1)}, bf16[768,768]{1,0:T(8,128)(2,1)S(1)}, u32[]{:S(2)}, u32[]{:S(2)}) collective-permute-start(bf16[768,768]{1,0:T(8,128)(2,1)} %constant_dynamic-slice_fusion.2), channel_id=1, source_target_pairs={{0,136},{136,0},{8,128},{128,8},{1,137},{137,1},{9,129},{129,9},{2... | collective-permute-start | bytes 3538952 | tf_op jit(solution)/shard_map/ppermute | solution.py:322
  21.7 3.2 %constant_dynamic-slice_fusion = bf16[768,1536]{1,0:T(8,128)(2,1)} fusion(bf16[768,3072]{1,0:T(8,128)(2,1)} %down_ref.1, s32[]{:T(128)S(6)} %select_n.18), kind=kLoop, calls=%fused_computation.9 | loop fusion | bytes 4718596 | tf_op jit(solution)/shard_map/dynamic_slice | solution.py:327
  24.9 2.5 %collective-permute-done.2 = bf16[512,384]{1,0:T(8,128)(2,1)} collective-permute-done((bf16[512,384]{1,0:T(8,128)(2,1)}, bf16[512,384]{1,0:T(8,128)(2,1)}, u32[]{:S(2)}, u32[]{:S(2)}) %collective-permute-start.2) | collective-permute-done | bytes 393248 | tf_op jit(solution)/shard_map/ppermute | solution.py:318
  27.3 7.5 %collective-permute-done.refs_1_.refs_3_ = bf16[528,768]{1,0:T(8,128)(2,1)} collective-permute-done((bf16[528,768]{1,0:T(8,128)(2,1)}, bf16[528,768]{1,0:T(8,128)(2,1)}, u32[]{:S(2)}, u32[]{:S(2)}) %collective-permute-start) | collective-permute-done | bytes 811040 | tf_op jit(solution)/shard_map/ppermute | solution.py:318
  34.8 3.2 %collective-permute-start.4 = (bf16[528,768]{1,0:T(8,128)(2,1)}, bf16[528,768]{1,0:T(8,128)(2,1)}, u32[]{:S(2)}, u32[]{:S(2)}) collective-permute-start(bf16[528,768]{1,0:T(8,128)(2,1)} %collective-permute-done.1.refs_2_.refs_4_), channel_id=1, source_target_pairs={{0,112},{16,0},{32,16},{48,32},{64,48},{80,64},{96,80},{112,96},{1... | collective-permute-start | bytes 2433032 | tf_op jit(solution)/shard_map/ppermute | solution.py:318
  38.1 1.5 maximum_select_fusion.refs_0_
  39.6 6.2 %shard_map.181 = (f32[3,1,1024]{2,1,0:T(1,128)S(1)}, f32[3,1,1024]{2,1,0:T(1,128)S(1)}, f32[384,1024]{1,0:T(8,128)S(1)}) custom-call(bf16[1024,384]{1,0:T(8,128)(2,1)S(1)} %maximum_select_fusion.refs_0_, bf16[528,768]{1,0:T(8,128)(2,1)} %maximum_maximum_fusion.refs_1_.refs_2_, bf16[528,768]{1,0:T(8,128)(2,1)} %maximum_maximum_fusion.refs_1_.refs_2_), custom_call_target="tpu_custom_call" | custom-call | flops 830472192 | bytes 1597440 | tf_op jit(solution)/shard_map/pallas_call | solution.py:111
  45.9 8.9 %shard_map.182 = (f32[3,1,1024]{2,1,0:T(1,128)S(1)}, f32[3,1,1024]{2,1,0:T(1,128)S(1)}, f32[384,1024]{1,0:T(8,128)S(1)}) custom-call(bf16[1024,384]{1,0:T(8,128)(2,1)S(1)} %maximum_select_fusion.refs_0_, bf16[528,768]{1,0:T(8,128)(2,1)} %collective-permute-done.refs_1_.refs_3_, bf16[528,768]{1,0:T(8,128)(2,1)} %collective-permute-done.1.refs_2_.refs_4_, ...), custom_call_target="tpu_custom_call" | custom-call | flops 1660944384 | bytes 2408448 | tf_op jit(solution)/shard_map/pallas_call | solution.py:111
  54.8 0.8 collective-permute-done.3.refs_1_.refs_3_
  55.6 1.8 collective-permute-start.6
  57.4 1.4 collective-permute-start.7
  58.9 0.4 collective-permute-start.10
  59.3 8.9 %shard_map.183 = (f32[3,1,1024]{2,1,0:T(1,128)S(1)}, f32[3,1,1024]{2,1,0:T(1,128)S(1)}, f32[384,1024]{1,0:T(8,128)S(1)}) custom-call(bf16[1024,384]{1,0:T(8,128)(2,1)S(1)} %maximum_select_fusion.refs_0_, bf16[528,768]{1,0:T(8,128)(2,1)} %collective-permute-done.3.refs_1_.refs_3_, bf16[528,768]{1,0:T(8,128)(2,1)} %collective-permute-done.4.refs_2_.refs_4_, ...), custom_call_target="tpu_custom_call" | custom-call | flops 1660944384 | bytes 2408448 | tf_op jit(solution)/shard_map/pallas_call | solution.py:111
  68.2 7.2 %collective-permute-done.6.refs_1_.refs_3_ = bf16[528,768]{1,0:T(8,128)(2,1)S(1)} collective-permute-done((bf16[528,768]{1,0:T(8,128)(2,1)}, bf16[528,768]{1,0:T(8,128)(2,1)S(1)}, u32[]{:S(2)}, u32[]{:S(2)}) %collective-permute-start.6) | collective-permute-done | bytes 811040 | tf_op jit(solution)/shard_map/ppermute | solution.py:318
  75.4 1.6 collective-permute-start.8
  77.1 2.0 collective-permute-start.9
  79.0 8.0 %shard_map.184 = (f32[3,1,1024]{2,1,0:T(1,128)S(1)}, f32[3,1,1024]{2,1,0:T(1,128)S(1)}, f32[384,1024]{1,0:T(8,128)S(1)}) custom-call(bf16[1024,384]{1,0:T(8,128)(2,1)S(1)} %maximum_select_fusion.refs_0_, bf16[528,768]{1,0:T(8,128)(2,1)S(1)} %collective-permute-done.6.refs_1_.refs_3_, bf16[528,768]{1,0:T(8,128)(2,1)S(1)} %collective-permute-done.7.refs_2_.refs_4_, ...), custom_call_target="tpu_custom_call" | custom-call | flops 1660944384 | bytes 2408448 | tf_op jit(solution)/shard_map/pallas_call | solution.py:111
  87.0 7.2 %shard_map.185 = bf16[2,4,2,64,512]{4,3,2,1,0:T(8,128)(2,1)} custom-call(bf16[1024,384]{1,0:T(8,128)(2,1)S(1)} %maximum_select_fusion.refs_0_, bf16[272,768]{1,0:T(8,128)(2,1)S(1)} %collective-permute-done.8.refs_1_.refs_3_, bf16[256,768]{1,0:T(8,128)(2,1)S(1)} %collective-permute-done.9.refs_2_.refs_4_, ...), custom_call_target="tpu_custom_call" | custom-call | flops 830472192 | bytes 1597440 | tf_op jit(solution)/shard_map/pallas_call | solution.py:111
  94.3 3.7 %collective-permute-done.11.refs_4_ = bf16[768,1536]{1,0:T(8,128)(2,1)} collective-permute-done((bf16[768,1536]{1,0:T(8,128)(2,1)}, bf16[768,1536]{1,0:T(8,128)(2,1)}, u32[]{:S(2)}, u32[]{:S(2)}) %collective-permute-start.11) | collective-permute-done | bytes 2359328 | tf_op jit(solution)/shard_map/ppermute | solution.py:322
  98.0 0.5 collective-permute-start.16
  98.5 6.4 %all-to-all-start = ((bf16[8,128,512]{2,1,0:T(8,128)(2,1)}), bf16[8,128,512]{2,1,0:T(8,128)(2,1)S(1)}, u32[]{:S(2)}, u32[]{:S(2)}) async-start(bf16[8,128,512]{2,1,0:T(8,128)(2,1)} %bitcast.1), calls=%async_computation | async-start | bytes 2097152 | tf_op jit(solution)/shard_map/all_to_all | solution.py:409
  104.9 0.5 collective-permute-start.15
  105.5 13.9 %all-to-all-done.part_ref = bf16[8,128,512]{2,1,0:T(8,128)(2,1)S(1)} async-done(((bf16[8,128,512]{2,1,0:T(8,128)(2,1)}), bf16[8,128,512]{2,1,0:T(8,128)(2,1)S(1)}, u32[]{:S(2)}, u32[]{:S(2)}) %all-to-all-start) | async-done | bytes 1048608 | tf_op jit(solution)/shard_map/all_to_all | solution.py:409
  119.4 2.3 %copy-done.1 = bf16[1536,1536]{1,0:T(8,128)(2,1)S(1)} copy-done((bf16[1536,1536]{1,0:T(8,128)(2,1)S(1)}, bf16[1536,1536]{1,0:T(8,128)(2,1)}, u32[]{:S(2)}) %copy-start.1) | copy-done | bytes 4718616
  121.8 6.8 %shard_map.186 = (f32[64,3072]{1,0:T(8,128)S(1)}, bf16[64,3072]{1,0:T(8,128)(2,1)S(1)}) custom-call(s32[4]{0:T(128)S(1)} %slice.31.order, s32[1]{0:T(128)} %bitcast.yh, bf16[8,128,512]{2,1,0:T(8,128)(2,1)S(1)} %all-to-all-done.part_ref, bf16[1536,1536]{1,0:T(8,128)(2,1)S(1)} %copy-done.1, bf16[1536,1536]{1,0:T(8,128)(2,1)} %collective-permute-done.12.mate_ref), custom_call_target="tpu_custom_call" | custom-call | flops 1207959552 | bytes 9437184 | tf_op jit(solution)/shard_map/pallas_call | solution.py:169
  128.5 2.6 %collective-permute-start.13 = (bf16[64,3072]{1,0:T(8,128)(2,1)S(1)}, bf16[64,3072]{1,0:T(8,128)(2,1)S(1)}, u32[]{:S(2)}, u32[]{:S(2)}) collective-permute-start(bf16[64,3072]{1,0:T(8,128)(2,1)S(1)} %get-tuple-element.86), channel_id=1, source_target_pairs={{0,8},{8,0},{1,9},{9,1},{2,10},{10,2},{3,11},{11,3},{4,12},{12,4},... | collective-permute-start | bytes 1179656 | tf_op jit(solution)/shard_map/ppermute | solution.py:318
  131.1 0.4 collective-permute-start.17
  131.6 3.4 %collective-permute-done.17 = f32[768]{0:T(1024)S(1)} collective-permute-done((f32[768]{0:T(1024)S(1)}, f32[768]{0:T(1024)S(1)}, u32[]{:S(2)}, u32[]{:S(2)}) %collective-permute-start.17) | collective-permute-done | bytes 3104 | tf_op jit(solution)/shard_map/ppermute | solution.py:322
  135.1 5.9 %collective-permute-done.13.other_ref = bf16[64,3072]{1,0:T(8,128)(2,1)S(1)} collective-permute-done((bf16[64,3072]{1,0:T(8,128)(2,1)S(1)}, bf16[64,3072]{1,0:T(8,128)(2,1)S(1)}, u32[]{:S(2)}, u32[]{:S(2)}) %collective-permute-start.13) | collective-permute-done | bytes 393248 | tf_op jit(solution)/shard_map/ppermute | solution.py:318
  140.9 1.1 shard_map.187
  142.2 3.2 %collective-permute-start.19 = (bf16[64,3072]{1,0:T(8,128)(2,1)S(1)}, bf16[64,3072]{1,0:T(8,128)(2,1)S(1)}, u32[]{:S(2)}, u32[]{:S(2)}) collective-permute-start(bf16[64,3072]{1,0:T(8,128)(2,1)S(1)} %get-tuple-element.91), channel_id=1, source_target_pairs={{0,6},{2,0},{4,2},{6,4},{1,7},{3,1},{5,3},{7,5},{8,14},{10,8},{12,... | collective-permute-start | bytes 1179656 | tf_op jit(solution)/shard_map/ppermute | solution.py:318
  145.4 7.7 %collective-permute-done.18 = bf16[64,3072]{1,0:T(8,128)(2,1)S(1)} collective-permute-done((bf16[64,3072]{1,0:T(8,128)(2,1)S(1)}, bf16[64,3072]{1,0:T(8,128)(2,1)S(1)}, u32[]{:S(2)}, u32[]{:S(2)}) %collective-permute-start.18) | collective-permute-done | bytes 393248 | tf_op jit(solution)/shard_map/ppermute | solution.py:318
  153.2 3.5 %collective-permute-start.21 = (bf16[32,3072]{1,0:T(8,128)(2,1)S(1)}, bf16[32,3072]{1,0:T(8,128)(2,1)S(1)}, u32[]{:S(2)}, u32[]{:S(2)}) collective-permute-start(bf16[32,3072]{1,0:T(8,128)(2,1)S(1)} %slice.41), channel_id=1, source_target_pairs={{0,6},{2,0},{4,2},{6,4},{1,7},{3,1},{5,3},{7,5},{8,14},{10,8},{12,... | collective-permute-start | bytes 589832 | tf_op jit(solution)/shard_map/ppermute | solution.py:318
  156.8 3.3 %collective-permute-done.20 = bf16[32,3072]{1,0:T(8,128)(2,1)S(1)} collective-permute-done((bf16[32,3072]{1,0:T(8,128)(2,1)S(1)}, bf16[32,3072]{1,0:T(8,128)(2,1)S(1)}, u32[]{:S(2)}, u32[]{:S(2)}) %collective-permute-start.20) | collective-permute-done | bytes 196640 | tf_op jit(solution)/shard_map/ppermute | solution.py:318
  160.1 12.9 %shard_map.188 = bf16[256,3072]{1,0:T(8,128)(2,1)S(1)} custom-call(s32[8]{0:T(128)S(1)} %add_xor_fusion.order, bf16[256,3072]{1,0:T(8,128)(2,1)S(1)} %constant_dynamic-update-slice_fusion.x_ref, bf16[3072,768]{1,0:T(8,128)(2,1)} %up_ref.1, bf16[768,3072]{1,0:T(8,128)(2,1)} %down_ref.1, f32[1,768]{1,0:T(1,128)S(1)} %reshape.25.bias_ref, ...), custom_call_target="tpu_custom_call" | custom-call | flops 4831838208 | bytes 18874368 | tf_op jit(solution)/shard_map/pallas_call | solution.py:283
  173.1 3.6 %collective-permute-start.22 = (bf16[64,3072]{1,0:T(8,128)(2,1)S(1)}, bf16[64,3072]{1,0:T(8,128)(2,1)S(1)}, u32[]{:S(2)}, u32[]{:S(2)}) collective-permute-start(bf16[64,3072]{1,0:T(8,128)(2,1)S(1)} %get-tuple-element.99), channel_id=1, source_target_pairs={{0,6},{2,0},{4,2},{6,4},{1,7},{3,1},{5,3},{7,5},{8,14},{10,8},{12,... | collective-permute-start | bytes 1179656 | tf_op jit(solution)/shard_map/ppermute | solution.py:318
  176.7 1.6 collective-permute-start.24
  178.3 11.8 %collective-permute-done.22 = bf16[64,3072]{1,0:T(8,128)(2,1)S(1)} collective-permute-done((bf16[64,3072]{1,0:T(8,128)(2,1)S(1)}, bf16[64,3072]{1,0:T(8,128)(2,1)S(1)}, u32[]{:S(2)}, u32[]{:S(2)}) %collective-permute-start.22) | collective-permute-done | bytes 393248 | tf_op jit(solution)/shard_map/ppermute | solution.py:318
  190.1 3.4 %collective-permute-done.23 = bf16[64,3072]{1,0:T(8,128)(2,1)S(1)} collective-permute-done((bf16[64,3072]{1,0:T(8,128)(2,1)S(1)}, bf16[64,3072]{1,0:T(8,128)(2,1)S(1)}, u32[]{:S(2)}, u32[]{:S(2)}) %collective-permute-start.23) | collective-permute-done | bytes 393248 | tf_op jit(solution)/shard_map/ppermute | solution.py:318
  193.5 1.0 add_convert_fusion
  (74 shorter events, 0.8 us)
Async XLA Ops:
  6.5 1.7 copy-start
  6.5 91.4 %all-gather.2.cloned.1.call-start = ((), (), s32[]{:S(2)}) async-start(), calls=%async_computation.1 | async-start | bytes 5898240 | tf_op jit(solution)/shard_map/all_gather | solution.py:365
  8.2 1.2 copy-start.5
  8.2 1.4 copy-start.6
  8.2 1.4 copy-start.7
  8.2 1.4 copy-start.8
  10.6 24.2 %collective-permute-start = (bf16[528,768]{1,0:T(8,128)(2,1)}, bf16[528,768]{1,0:T(8,128)(2,1)}, u32[]{:S(2)}, u32[]{:S(2)}) collective-permute-start(bf16[528,768]{1,0:T(8,128)(2,1)} %maximum_maximum_fusion.refs_1_.refs_2_), channel_id=1, source_target_pairs={{0,16},{16,32},{32,48},{48,64},{64,80},{80,96},{96,112},{112,0},{1... | collective-permute-start | bytes 2433032 | tf_op jit(solution)/shard_map/ppermute | solution.py:318
  12.5 22.3 %collective-permute-start.1 = (bf16[528,768]{1,0:T(8,128)(2,1)}, bf16[528,768]{1,0:T(8,128)(2,1)}, u32[]{:S(2)}, u32[]{:S(2)}) collective-permute-start(bf16[528,768]{1,0:T(8,128)(2,1)} %maximum_maximum_fusion.refs_1_.refs_2_), channel_id=1, source_target_pairs={{0,112},{16,0},{32,16},{48,32},{64,48},{80,64},{96,80},{112,96},{1... | collective-permute-start | bytes 2433032 | tf_op jit(solution)/shard_map/ppermute | solution.py:318
  16.5 10.9 %collective-permute-start.2 = (bf16[512,384]{1,0:T(8,128)(2,1)}, bf16[512,384]{1,0:T(8,128)(2,1)}, u32[]{:S(2)}, u32[]{:S(2)}) collective-permute-start(bf16[512,384]{1,0:T(8,128)(2,1)} %param.19), channel_id=1, source_target_pairs={{0,128},{128,0},{1,129},{129,1},{2,130},{130,2},{3,131},{131,3},{4... | collective-permute-start | bytes 1179656 | tf_op jit(solution)/shard_map/ppermute | solution.py:318
  19.3 35.5 %collective-permute-start.5 = (bf16[768,768]{1,0:T(8,128)(2,1)}, bf16[768,768]{1,0:T(8,128)(2,1)S(1)}, u32[]{:S(2)}, u32[]{:S(2)}) collective-permute-start(bf16[768,768]{1,0:T(8,128)(2,1)} %constant_dynamic-slice_fusion.2), channel_id=1, source_target_pairs={{0,136},{136,0},{8,128},{128,8},{1,137},{137,1},{9,129},{129,9},{2... | collective-permute-start | bytes 3538952 | tf_op jit(solution)/shard_map/ppermute | solution.py:322
  24.9 73.1 %collective-permute-start.11 = (bf16[768,1536]{1,0:T(8,128)(2,1)}, bf16[768,1536]{1,0:T(8,128)(2,1)}, u32[]{:S(2)}, u32[]{:S(2)}) collective-permute-start(bf16[768,1536]{1,0:T(8,128)(2,1)} %constant_dynamic-slice_fusion), channel_id=1, source_target_pairs={{0,136},{136,0},{8,128},{128,8},{1,137},{137,1},{9,129},{129,9},{2... | collective-permute-start | bytes 7077896 | tf_op jit(solution)/shard_map/ppermute | solution.py:322
  34.8 20.8 %collective-permute-start.3 = (bf16[528,768]{1,0:T(8,128)(2,1)}, bf16[528,768]{1,0:T(8,128)(2,1)}, u32[]{:S(2)}, u32[]{:S(2)}) collective-permute-start(bf16[528,768]{1,0:T(8,128)(2,1)} %collective-permute-done.refs_1_.refs_3_), channel_id=1, source_target_pairs={{0,16},{16,32},{32,48},{48,64},{64,80},{80,96},{96,112},{112,0},{1... | collective-permute-start | bytes 2433032 | tf_op jit(solution)/shard_map/ppermute | solution.py:318
  34.8 20.8 %collective-permute-start.4 = (bf16[528,768]{1,0:T(8,128)(2,1)}, bf16[528,768]{1,0:T(8,128)(2,1)}, u32[]{:S(2)}, u32[]{:S(2)}) collective-permute-start(bf16[528,768]{1,0:T(8,128)(2,1)} %collective-permute-done.1.refs_2_.refs_4_), channel_id=1, source_target_pairs={{0,112},{16,0},{32,16},{48,32},{64,48},{80,64},{96,80},{112,96},{1... | collective-permute-start | bytes 2433032 | tf_op jit(solution)/shard_map/ppermute | solution.py:318
  54.8 13.4 %copy-start.2 = (bf16[768,768]{1,0:T(8,128)(2,1)}, bf16[768,768]{1,0:T(8,128)(2,1)S(1)}, u32[]{:S(2)}) copy-start(bf16[768,768]{1,0:T(8,128)(2,1)S(1)} %collective-permute-done.5.refs_0_) | copy-start | bytes 3538948
  55.6 19.8 %collective-permute-start.6 = (bf16[528,768]{1,0:T(8,128)(2,1)}, bf16[528,768]{1,0:T(8,128)(2,1)S(1)}, u32[]{:S(2)}, u32[]{:S(2)}) collective-permute-start(bf16[528,768]{1,0:T(8,128)(2,1)} %collective-permute-done.3.refs_1_.refs_3_), channel_id=1, source_target_pairs={{0,16},{16,32},{32,48},{48,64},{64,80},{80,96},{96,112},{112,0},{1... | collective-permute-start | bytes 2433032 | tf_op jit(solution)/shard_map/ppermute | solution.py:318
  57.4 17.9 %collective-permute-start.7 = (bf16[528,768]{1,0:T(8,128)(2,1)}, bf16[528,768]{1,0:T(8,128)(2,1)S(1)}, u32[]{:S(2)}, u32[]{:S(2)}) collective-permute-start(bf16[528,768]{1,0:T(8,128)(2,1)} %collective-permute-done.4.refs_2_.refs_4_), channel_id=1, source_target_pairs={{0,112},{16,0},{32,16},{48,32},{64,48},{80,64},{96,80},{112,96},{1... | collective-permute-start | bytes 2433032 | tf_op jit(solution)/shard_map/ppermute | solution.py:318
  58.9 39.1 %collective-permute-start.10 = (bf16[768,768]{1,0:T(8,128)(2,1)S(1)}, bf16[768,768]{1,0:T(8,128)(2,1)}, u32[]{:S(2)}, u32[]{:S(2)}) collective-permute-start(bf16[768,768]{1,0:T(8,128)(2,1)S(1)} %collective-permute-done.5.refs_0_), channel_id=1, source_target_pairs={{0,128},{128,0},{1,129},{129,1},{2,130},{130,2},{3,131},{131,3},{4... | collective-permute-start | bytes 3538952 | tf_op jit(solution)/shard_map/ppermute | solution.py:318
  75.4 11.6 %collective-permute-start.8 = (bf16[272,768]{1,0:T(8,128)(2,1)S(1)}, bf16[272,768]{1,0:T(8,128)(2,1)S(1)}, u32[]{:S(2)}, u32[]{:S(2)}) collective-permute-start(bf16[272,768]{1,0:T(8,128)(2,1)S(1)} %slice.32), channel_id=1, source_target_pairs={{0,16},{16,32},{32,48},{48,64},{64,80},{80,96},{96,112},{112,0},{1... | collective-permute-start | bytes 1253384 | tf_op jit(solution)/shard_map/ppermute | solution.py:318
  77.1 9.9 %collective-permute-start.9 = (bf16[256,768]{1,0:T(8,128)(2,1)S(1)}, bf16[256,768]{1,0:T(8,128)(2,1)S(1)}, u32[]{:S(2)}, u32[]{:S(2)}) collective-permute-start(bf16[256,768]{1,0:T(8,128)(2,1)S(1)} %slice.33), channel_id=1, source_target_pairs={{0,112},{16,0},{32,16},{48,32},{64,48},{80,64},{96,80},{112,96},{1... | collective-permute-start | bytes 1179656 | tf_op jit(solution)/shard_map/ppermute | solution.py:318
  94.2 11.2 %copy-start.16 = (s32[8]{0:T(128)S(1)}, s32[8]{0:T(128)}, u32[]{:S(2)}) copy-start(s32[8]{0:T(128)} %constant.30.clone) | copy-start | bytes 100
  94.2 11.2 %copy-start.17 = (s32[8]{0:T(128)S(1)}, s32[8]{0:T(128)}, u32[]{:S(2)}) copy-start(s32[8]{0:T(128)} %constant.31.clone) | copy-start | bytes 100
  94.2 11.2 %copy-start.18 = (s32[8]{0:T(128)S(1)}, s32[8]{0:T(128)}, u32[]{:S(2)}) copy-start(s32[8]{0:T(128)} %constant.32.clone) | copy-start | bytes 100
  98.0 21.4 %collective-permute-start.12 = (bf16[1536,1536]{1,0:T(8,128)(2,1)}, bf16[1536,1536]{1,0:T(8,128)(2,1)}, u32[]{:S(2)}, u32[]{:S(2)}) collective-permute-start(bf16[1536,1536]{1,0:T(8,128)(2,1)} %all-gather.2.cloned.1.call-done.mine_ref), channel_id=1, source_target_pairs={{0,1},{1,0},{2,3},{3,2},{4,5},{5,4},{6,7},{7,6},{8,9},{9,8},{10,11... | collective-permute-start | bytes 14155784 | tf_op jit(solution)/shard_map/ppermute | solution.py:318
  98.0 37.1 %collective-permute-start.16 = (bf16[768,1536]{1,0:T(8,128)(2,1)}, bf16[768,1536]{1,0:T(8,128)(2,1)}, u32[]{:S(2)}, u32[]{:S(2)}) collective-permute-start(bf16[768,1536]{1,0:T(8,128)(2,1)} %collective-permute-done.11.refs_4_), channel_id=1, source_target_pairs={{0,1},{1,0},{2,3},{3,2},{4,5},{5,4},{6,7},{7,6},{8,9},{9,8},{10,11... | collective-permute-start | bytes 7077896 | tf_op jit(solution)/shard_map/ppermute | solution.py:318
  98.5 20.9 %all-to-all-start = ((bf16[8,128,512]{2,1,0:T(8,128)(2,1)}), bf16[8,128,512]{2,1,0:T(8,128)(2,1)S(1)}, u32[]{:S(2)}, u32[]{:S(2)}) async-start(bf16[8,128,512]{2,1,0:T(8,128)(2,1)} %bitcast.1), calls=%async_computation | async-start | bytes 2097152 | tf_op jit(solution)/shard_map/all_to_all | solution.py:409
  104.9 30.2 %collective-permute-start.14 = (bf16[768,768]{1,0:T(8,128)(2,1)}, bf16[768,768]{1,0:T(8,128)(2,1)}, u32[]{:S(2)}, u32[]{:S(2)}) collective-permute-start(bf16[768,768]{1,0:T(8,128)(2,1)} %copy-done.2), channel_id=1, source_target_pairs={{0,1},{1,0},{2,3},{3,2},{4,5},{5,4},{6,7},{7,6},{8,9},{9,8},{10,11... | collective-permute-start | bytes 3538952 | tf_op jit(solution)/shard_map/ppermute | solution.py:318
  104.9 30.2 %collective-permute-start.15 = (bf16[768,768]{1,0:T(8,128)(2,1)}, bf16[768,768]{1,0:T(8,128)(2,1)}, u32[]{:S(2)}, u32[]{:S(2)}) collective-permute-start(bf16[768,768]{1,0:T(8,128)(2,1)} %collective-permute-done.10.refs_1_), channel_id=1, source_target_pairs={{0,1},{1,0},{2,3},{3,2},{4,5},{5,4},{6,7},{7,6},{8,9},{9,8},{10,11... | collective-permute-start | bytes 3538952 | tf_op jit(solution)/shard_map/ppermute | solution.py:318
  119.4 2.3 %copy-start.1 = (bf16[1536,1536]{1,0:T(8,128)(2,1)S(1)}, bf16[1536,1536]{1,0:T(8,128)(2,1)}, u32[]{:S(2)}) copy-start(bf16[1536,1536]{1,0:T(8,128)(2,1)} %all-gather.2.cloned.1.call-done.mine_ref) | copy-start | bytes 14155780
  121.7 9.4 %copy-start.15 = (f32[768]{0:T(1024)S(1)}, f32[768]{0:T(1024)}, u32[]{:S(2)}) copy-start(f32[768]{0:T(1024)} %param.32) | copy-start | bytes 9220
  121.7 9.8 %copy-start.11 = (f32[3072]{0:T(1024)S(1)}, f32[3072]{0:T(1024)}, u32[]{:S(2)}) copy-start(f32[3072]{0:T(1024)} %param.25) | copy-start | bytes 36868
  121.7 9.8 %copy-start.12 = (f32[3072]{0:T(1024)S(1)}, f32[3072]{0:T(1024)}, u32[]{:S(2)}) copy-start(f32[3072]{0:T(1024)} %param.26) | copy-start | bytes 36868
  121.7 9.8 %copy-start.13 = (f32[3072]{0:T(1024)S(1)}, f32[3072]{0:T(1024)}, u32[]{:S(2)}) copy-start(f32[3072]{0:T(1024)} %param.30) | copy-start | bytes 36868
  121.7 9.8 %copy-start.14 = (f32[3072]{0:T(1024)S(1)}, f32[3072]{0:T(1024)}, u32[]{:S(2)}) copy-start(f32[3072]{0:T(1024)} %param.27) | copy-start | bytes 36868
  121.7 19.2 %copy-start.4 = (bf16[64,3072]{1,0:T(8,128)(2,1)S(1)}, bf16[64,3072]{1,0:T(8,128)(2,1)}, u32[]{:S(2)}) copy-start(bf16[64,3072]{1,0:T(8,128)(2,1)} %residual_ref.1) | copy-start | bytes 1179652
  128.5 12.4 %collective-permute-start.13 = (bf16[64,3072]{1,0:T(8,128)(2,1)S(1)}, bf16[64,3072]{1,0:T(8,128)(2,1)S(1)}, u32[]{:S(2)}, u32[]{:S(2)}) collective-permute-start(bf16[64,3072]{1,0:T(8,128)(2,1)S(1)} %get-tuple-element.86), channel_id=1, source_target_pairs={{0,8},{8,0},{1,9},{9,1},{2,10},{10,2},{3,11},{11,3},{4,12},{12,4},... | collective-permute-start | bytes 1179656 | tf_op jit(solution)/shard_map/ppermute | solution.py:318
  131.1 3.9 %collective-permute-start.17 = (f32[768]{0:T(1024)S(1)}, f32[768]{0:T(1024)S(1)}, u32[]{:S(2)}, u32[]{:S(2)}) collective-permute-start(f32[768]{0:T(1024)S(1)} %copy-done.15), channel_id=1, source_target_pairs={{0,136},{136,0},{8,128},{128,8},{1,137},{137,1},{9,129},{129,9},{2... | collective-permute-start | bytes 9224 | tf_op jit(solution)/shard_map/ppermute | solution.py:322
  142.0 11.1 %collective-permute-start.18 = (bf16[64,3072]{1,0:T(8,128)(2,1)S(1)}, bf16[64,3072]{1,0:T(8,128)(2,1)S(1)}, u32[]{:S(2)}, u32[]{:S(2)}) collective-permute-start(bf16[64,3072]{1,0:T(8,128)(2,1)S(1)} %get-tuple-element.91), channel_id=1, source_target_pairs={{0,2},{2,4},{4,6},{6,0},{1,3},{3,5},{5,7},{7,1},{8,10},{10,12},{12... | collective-permute-start | bytes 1179656 | tf_op jit(solution)/shard_map/ppermute | solution.py:318
  142.2 11.0 %collective-permute-start.19 = (bf16[64,3072]{1,0:T(8,128)(2,1)S(1)}, bf16[64,3072]{1,0:T(8,128)(2,1)S(1)}, u32[]{:S(2)}, u32[]{:S(2)}) collective-permute-start(bf16[64,3072]{1,0:T(8,128)(2,1)S(1)} %get-tuple-element.91), channel_id=1, source_target_pairs={{0,6},{2,0},{4,2},{6,4},{1,7},{3,1},{5,3},{7,5},{8,14},{10,8},{12,... | collective-permute-start | bytes 1179656 | tf_op jit(solution)/shard_map/ppermute | solution.py:318
  145.4 14.7 %copy-start.3 = (bf16[768,768]{1,0:T(8,128)(2,1)S(1)}, bf16[768,768]{1,0:T(8,128)(2,1)}, u32[]{:S(2)}) copy-start(bf16[768,768]{1,0:T(8,128)(2,1)} %copy-done.2) | copy-start | bytes 3538948
  153.1 7.0 %collective-permute-start.20 = (bf16[32,3072]{1,0:T(8,128)(2,1)S(1)}, bf16[32,3072]{1,0:T(8,128)(2,1)S(1)}, u32[]{:S(2)}, u32[]{:S(2)}) collective-permute-start(bf16[32,3072]{1,0:T(8,128)(2,1)S(1)} %slice.40), channel_id=1, source_target_pairs={{0,2},{2,4},{4,6},{6,0},{1,3},{3,5},{5,7},{7,1},{8,10},{10,12},{12... | collective-permute-start | bytes 589832 | tf_op jit(solution)/shard_map/ppermute | solution.py:318
  153.2 6.9 %collective-permute-start.21 = (bf16[32,3072]{1,0:T(8,128)(2,1)S(1)}, bf16[32,3072]{1,0:T(8,128)(2,1)S(1)}, u32[]{:S(2)}, u32[]{:S(2)}) collective-permute-start(bf16[32,3072]{1,0:T(8,128)(2,1)S(1)} %slice.41), channel_id=1, source_target_pairs={{0,6},{2,0},{4,2},{6,4},{1,7},{3,1},{5,3},{7,5},{8,14},{10,8},{12,... | collective-permute-start | bytes 589832 | tf_op jit(solution)/shard_map/ppermute | solution.py:318
  173.0 20.5 %copy-start.9 = (f32[3072]{0:T(1024)S(1)}, f32[3072]{0:T(1024)}, u32[]{:S(2)}) copy-start(f32[3072]{0:T(1024)} %param.34) | copy-start | bytes 36868
  173.0 20.5 %copy-start.10 = (f32[3072]{0:T(1024)S(1)}, f32[3072]{0:T(1024)}, u32[]{:S(2)}) copy-start(f32[3072]{0:T(1024)} %param.28) | copy-start | bytes 36868
  173.1 17.0 %collective-permute-start.22 = (bf16[64,3072]{1,0:T(8,128)(2,1)S(1)}, bf16[64,3072]{1,0:T(8,128)(2,1)S(1)}, u32[]{:S(2)}, u32[]{:S(2)}) collective-permute-start(bf16[64,3072]{1,0:T(8,128)(2,1)S(1)} %get-tuple-element.99), channel_id=1, source_target_pairs={{0,6},{2,0},{4,2},{6,4},{1,7},{3,1},{5,3},{7,5},{8,14},{10,8},{12,... | collective-permute-start | bytes 1179656 | tf_op jit(solution)/shard_map/ppermute | solution.py:318
  176.7 16.8 %collective-permute-start.23 = (bf16[64,3072]{1,0:T(8,128)(2,1)S(1)}, bf16[64,3072]{1,0:T(8,128)(2,1)S(1)}, u32[]{:S(2)}, u32[]{:S(2)}) collective-permute-start(bf16[64,3072]{1,0:T(8,128)(2,1)S(1)} %get-tuple-element.101), channel_id=1, source_target_pairs={{0,2},{2,4},{4,6},{6,0},{1,3},{3,5},{5,7},{7,1},{8,10},{10,12},{12... | collective-permute-start | bytes 1179656 | tf_op jit(solution)/shard_map/ppermute | solution.py:318
  176.7 16.8 %collective-permute-start.24 = (bf16[64,3072]{1,0:T(8,128)(2,1)S(1)}, bf16[64,3072]{1,0:T(8,128)(2,1)S(1)}, u32[]{:S(2)}, u32[]{:S(2)}) collective-permute-start(bf16[64,3072]{1,0:T(8,128)(2,1)S(1)} %get-tuple-element.100), channel_id=1, source_target_pairs={{0,4},{2,6},{4,0},{6,2},{1,5},{3,7},{5,1},{7,3},{8,12},{10,14},{12... | collective-permute-start | bytes 1179656 | tf_op jit(solution)/shard_map/ppermute | solution.py:318
Sparse Core Ops, SparseCore 0:
  9.6 58.0 all-gather.1

commit v2 on v1

--- a/solution.py
+++ b/solution.py
@@ -123,19 +123,38 @@
     )(q, *ks, *vs, *(() if first else state))
 
 
-def join_project_body(order, yh, part_ref, mine_ref, mate_ref, own_ref, away_ref, attended):
+def join_project_body(order, place, part_ref, own_w, *refs):
+    mine, mate = refs[:3], refs[3:6]
+    own_ref, away_ref, attended, weights, sems = refs[6:]
     i = pl.program_id(0)
     x_size = part_ref.shape[0] // 2
     rows = part_ref.shape[1] // 2
     width = part_ref.shape[2] - HD
+    block = weights.shape[2]
+
+    def copies(n):
+        at = pl.multiple_of(order[n] * block, block)
+        yield pltpu.make_async_copy(
+            own_w.at[:, pl.ds(at, block)], weights.at[n, pl.ds(0, width)], sems.at[n, 0]
+        )
+        for p, piece in enumerate(mine if n < 2 else mate):
+            yield pltpu.make_async_copy(
+                piece.at[:, pl.ds(n % 2 * block, block)],
+                weights.at[n, pl.ds((p + 1) * width, width)],
+                sems.at[n, p + 1],
+            )
 
     @pl.when(i == 0)
     def _():
+        for n in range(4):
+            for copy in copies(n):
+                copy.start()
         for side in range(2):
-            at = pl.ds(pl.multiple_of((yh[0] if side == 0 else 1 - yh[0]) * rows, rows), rows)
-            for x in range(x_size):
-                a = part_ref[x, at, :].astype(jnp.float32)
-                b = part_ref[x_size + x, at, :].astype(jnp.float32)
+            yh = place[4] if side == 0 else 1 - place[4]
+            at = pl.ds(pl.multiple_of(yh * rows, rows), rows)
+            for p in range(x_size):
+                a = part_ref[place[p], at, :].astype(jnp.float32)
+                b = part_ref[x_size + place[p], at, :].astype(jnp.float32)
                 for h in range(width // HD):
                     k = width + 3 * h
                     lse_a = a[:, k : k + 1] + a[:, k + 1 : k + 2] + a[:, k + 2 : k + 3]
@@ -143,51 +162,51 @@
                     share = 1.0 / (1.0 + jnp.exp2(lse_b - lse_a))
                     cols = slice(h * HD, (h + 1) * HD)
                     joined = b[:, cols] + share * (a[:, cols] - b[:, cols])
-                    attended[
-                        side * rows : (side + 1) * rows, x * width + h * HD : x * width + (h + 1) * HD
-                    ] = joined.astype(jnp.bfloat16)
-
-    def project(weight_ref):
-        out = jnp.dot(attended[...], weight_ref[...], preferred_element_type=jnp.float32)
-        own_ref[...] = out[:rows]
-        away_ref[...] = out[rows:].astype(jnp.bfloat16)
-
-    @pl.when(i < 2)
-    def _():
-        project(mine_ref)
-
-    @pl.when(i >= 2)
-    def _():
-        project(mate_ref)
-
-
-def join_project(parts, mine, mate, order, yh):
+                    to = slice(p * width + h * HD, p * width + (h + 1) * HD)
+                    attended[side * rows : (side + 1) * rows, to] = joined.astype(jnp.bfloat16)
+
+    for n in range(4):
+
+        @pl.when(i == n)
+        def _(n=n):
+            for copy in copies(n):
+                copy.wait()
+            out = jnp.dot(attended[...], weights[n], preferred_element_type=jnp.float32)
+            own_ref[...] = out[:rows]
+            away_ref[...] = out[rows:].astype(jnp.bfloat16)
+
+
+def join_project(parts, own_w, mine, mate, order, place):
     n, both, wide = parts.shape
-    k, half = mine.shape
-    block, rows = half // 2, both // 2
-    out = pl.BlockSpec((rows, block), lambda i, order, yh: (0, order[i]))
+    width, d_model = own_w.shape
+    block, rows = d_model // 4, both // 2
+    out = pl.BlockSpec((rows, block), lambda i, order, place: (0, order[i]))
+    far_spec = pl.BlockSpec(memory_space=pltpu.MemorySpace.HBM)
     return pl.pallas_call(
         join_project_body,
         grid_spec=pltpu.PrefetchScalarGridSpec(
             num_scalar_prefetch=2,
             grid=(4,),
             in_specs=[
-                pl.BlockSpec((n, both, wide), lambda i, order, yh: (0, 0, 0)),
-                pl.BlockSpec((k, block), lambda i, order, yh: (0, jnp.minimum(i, 1))),
-                pl.BlockSpec((k, block), lambda i, order, yh: (0, jnp.maximum(i - 2, 0))),
+                pl.BlockSpec((n, both, wide), lambda i, order, place: (0, 0, 0)),
+                *[far_spec] * 7,
             ],
             out_specs=[out, out],
-            scratch_shapes=[pltpu.VMEM((both, k), jnp.bfloat16)],
+            scratch_shapes=[
+                pltpu.VMEM((both, 4 * width), jnp.bfloat16),
+                pltpu.VMEM((4, 4 * width, block), jnp.bfloat16),
+                pltpu.SemaphoreType.DMA((4, 4)),
+            ],
         ),
         out_shape=[
-            jax.ShapeDtypeStruct((rows, 2 * half), jnp.float32),
-            jax.ShapeDtypeStruct((rows, 2 * half), jnp.bfloat16),
+            jax.ShapeDtypeStruct((rows, d_model), jnp.float32),
+            jax.ShapeDtypeStruct((rows, d_model), jnp.bfloat16),
         ],
         cost_estimate=pl.CostEstimate(
-            flops=4 * both * k * half, transcendentals=0, bytes_accessed=4 * k * half
+            flops=8 * both * width * d_model, transcendentals=0, bytes_accessed=8 * width * d_model
         ),
         compiler_params=pltpu.CompilerParams(vmem_limit_bytes=40 << 20),
-    )(order, yh, parts, mine, mate)
+    )(order, place, parts, own_w, *mine, *mate)
 
 
 def stream_norm_body(own_ref, other_ref, residual_ref, vectors_ref, stream_ref, normed_ref):
@@ -223,41 +242,47 @@
 
 def mlp_body(order, x_ref, up_ref, down_ref, bias_ref, bias_far_ref, *refs):
     n = 4
-    up_far, down_far, out_ref = refs[:n], refs[n : n + 2], refs[n + 2]
-    near, far, hid_near, hid_far, up_buf, down_buf, sems = refs[n + 3 :]
+    up_far, down_far, out_ref = refs[:n], refs[n : 2 * n], refs[2 * n]
+    near, far, hid_near, hid_far, up_buf, down_buf, sems = refs[2 * n + 1 :]
     i = pl.program_id(0)
     quarter = up_ref.shape[0]
 
-    def copies():
-        for j in range(n):
-            yield pltpu.make_async_copy(up_far[j], up_buf.at[j], sems.at[j])
-        for j in range(n):
-            cols = pl.ds((j % 2) * quarter, quarter)
-            yield pltpu.make_async_copy(down_far[j // 2].at[:, cols], down_buf.at[j], sems.at[n + j])
+    def copies(j):
+        down = j >= n
+        a, b = (down_far if down else up_far)[j % n // 2 * 2 : j % n // 2 * 2 + 2]
+        to = (down_buf if down else up_buf).at[j % n]
+
+        def part(ref, start, size):
+            return ref.at[:, pl.ds(start, size)] if down else ref.at[pl.ds(start, size)]
+
+        if j % 2 == 0:
+            yield pltpu.make_async_copy(part(a, 0, quarter), to, sems.at[j, 0])
+            return
+        rest = a.shape[1 if down else 0] - quarter
+        yield pltpu.make_async_copy(part(a, quarter, rest), part(to, 0, rest), sems.at[j, 0])
+        yield pltpu.make_async_copy(b, part(to, rest, quarter - rest), sems.at[j, 1])
 
     @pl.when(i == 0)
     def _():
-        for copy in copies():
-            copy.start()
+        for j in range(2 * n):
+            for copy in copies(j):
+                copy.start()
         near[...] = jnp.broadcast_to(bias_ref[...], near.shape)
         far[...] = jnp.broadcast_to(bias_far_ref[...], far.shape)
 
-    for j, copy in enumerate(copies()):
+    for j in range(2 * n):
 
         @pl.when(i == j)
-        def _(copy=copy):
-            copy.wait()
+        def _(j=j):
+            for copy in copies(j):
+                copy.wait()
 
     @pl.when(i < n)
     def _():
-        at = pl.multiple_of(i * quarter, quarter)
-        near[...] += jnp.dot(
-            x_ref[:, pl.ds(at, quarter)], up_ref[...], preferred_element_type=jnp.float32
-        )
         at = pl.multiple_of(order[i] * quarter, quarter)
-        far[...] += jnp.dot(
-            x_ref[:, pl.ds(at, quarter)], up_buf[i], preferred_element_type=jnp.float32
-        )
+        x = x_ref[:, pl.ds(at, quarter)]
+        near[...] += jnp.dot(x, up_ref[...], preferred_element_type=jnp.float32)
+        far[...] += jnp.dot(x, up_buf[i], preferred_element_type=jnp.float32)
 
     @pl.when(i == n - 1)
     def _():
@@ -275,10 +300,10 @@
 def mlp(x, up, down, bias, bias_far, up_far, down_far, order):
     rows, d_model = x.shape
     hidden = up.shape[1]
-    n = len(up_far)
+    n = 4
     quarter = d_model // n
     whole = lambda i, order: (0, 0)
-    column = lambda i, order: (0, order[jnp.maximum(i, n)])
+    column = lambda i, order: (0, order[jnp.maximum(i - n, 0)])
     far_spec = pl.BlockSpec(memory_space=pltpu.MemorySpace.HBM)
     return pl.pallas_call(
         mlp_body,
@@ -287,11 +312,11 @@
             grid=(2 * n,),
             in_specs=[
                 pl.BlockSpec((rows, d_model), whole),
-                pl.BlockSpec((quarter, hidden), lambda i, order: (jnp.minimum(i, n - 1), 0)),
+                pl.BlockSpec((quarter, hidden), lambda i, order: (order[jnp.minimum(i, n - 1)], 0)),
                 pl.BlockSpec((hidden, quarter), column),
                 pl.BlockSpec((1, hidden), whole),
                 pl.BlockSpec((1, hidden), whole),
-                *[far_spec] * (n + 2),
+                *[far_spec] * (2 * n),
             ],
             out_specs=pl.BlockSpec((rows, quarter), column),
             scratch_shapes=[
@@ -301,7 +326,7 @@
                 pltpu.VMEM((rows, hidden), jnp.bfloat16),
                 pltpu.VMEM((n, quarter, hidden), jnp.bfloat16),
                 pltpu.VMEM((n, hidden, quarter), jnp.bfloat16),
-                pltpu.SemaphoreType.DMA((2 * n,)),
+                pltpu.SemaphoreType.DMA((2 * n, 2)),
             ],
         ),
         out_shape=jax.ShapeDtypeStruct((rows, d_model), jnp.bfloat16),
@@ -325,6 +350,11 @@
 def part_of(array, parts, index, axis):
     n = array.shape[axis] // parts
     return lax.dynamic_slice_in_dim(array, index * n, n, axis)
+
+
+def half_of(array, index, axis, start, stop):
+    n = array.shape[axis] // 2
+    return lax.dynamic_slice_in_dim(array, index * n + start, stop - start, axis)
 
 
 tie = lax.optimization_barrier
@@ -360,15 +390,14 @@
     rows_own, width = img_query.shape
     row_block, d_model = residual_in.shape
 
-    up_a = cross(part_of(up_weight, 4, yl_at * 2 + core, 0))
-    down_a = cross(part_of(down_weight, 2, core, 1))
-    out_mine = lax.all_gather(part_of(out_weight, 2, core, 1), "x", axis=0, tiled=True)
     vectors = jnp.stack([gate_attn, out_bias, mod_scale, mod_shift])
-    order = jnp.bitwise_xor(
-        jnp.array([2, 2, 2, 2, 0, 0, 0, 0], jnp.int32) * (1 - yl_at)
-        + core * jnp.array([1, 1, 1, 1, 2, 2, 2, 2], jnp.int32),
-        jnp.array([0, 2, 1, 3, 0, 1, 2, 3], jnp.int32),
-    )
+    order = jnp.bitwise_xor(2 * core, jnp.arange(4, dtype=jnp.int32))
+    x_at = lax.axis_index("x")
+    place = jnp.concatenate(
+        [(x_at + jnp.array([0, 3, 1, 2], jnp.int32)) % 4, yh_at.reshape(1).astype(jnp.int32)]
+    )
+    out_half = part_of(out_weight, 2, core, 1)
+    up_most, down_most = d_model // 3, d_model // 8 * 3
 
     q_other = shift(img_query, "yl", 2, 1)
     own = jnp.concatenate(
@@ -384,6 +413,9 @@
         return [shift(up, "z", 8, 1), shift(down, "z", 8, 7)]
 
     one = around(own, own)
+    up_a = cross(half_of(up_weight, core, 0, 0, up_most))
+    out_l = shift(out_half, "x", 4, 1)
+    out_r = shift(out_half, "x", 4, 3)
     one, q_other = tie((one, q_other))
     queries = jnp.where(
         yl_at == 0,
@@ -393,26 +425,37 @@
     two = around(*one)
     state = attend(queries, [own], None)
     state = attend(queries, one, state)
-    two, state, up_a = tie((two, state, up_a))
+    two, state, up_a, out_l, out_r, core, out_half = tie(
+        (two, state, up_a, out_l, out_r, core, out_half)
+    )
     three = around(*two)
-    up_b = shift(up_a, "yl", 2, 1)
+    down_a = cross(half_of(down_weight, core, 1, 0, down_most))
+    out_f = shift(out_half, "x", 4, 2)
     state = attend(queries, two, state)
-    three, state = tie((three, state))
+    three, state, core = tie((three, state, core))
+    up_late = half_of(up_weight, core, 0, up_most, d_model // 2)
+    down_late = half_of(down_weight, core, 1, down_most, d_model // 2)
     four = around(three[0][:cut], three[1][cut:])
     state = attend(queries, three, state)
     four, state = tie((four, state))
     shape = (2, 4, 2, row_block, width + HD)
     (part,) = attend(queries, four, state, shape)
-    part, up_b, out_mine, down_a = tie((part, up_b, out_mine, down_a))
-    out_mate = shift(out_mine, "dp", 2, 1)
+    out_mine = [out_l, out_r, out_f]
+    part, down_a, up_a, out_mine, up_late, down_late = tie(
+        (part, down_a, up_a, out_mine, up_late, down_late)
+    )
+    out_mate = [shift(piece, "dp", 2, 1) for piece in out_mine]
+    up_b = cross(up_late)
+    down_b = cross(down_late)
 
     parts = lax.all_to_all(
         part.reshape(8, 2 * row_block, width + HD), ("yl", "x"), split_axis=0, concat_axis=0, tiled=True
     )
-    proj_own, proj_away = join_project(parts, out_mine, out_mate, order[4:], yh_at.reshape(1))
+    parts, out_mate, up_b, down_b = tie((parts, out_mate, up_b, down_b))
+    proj_own, proj_away = join_project(parts, out_weight, out_mine, out_mate, order, place)
     proj_other = shift(proj_away, "yh", 2, 1)
     up_far = [up_a, up_b, shift(up_a, "dp", 2, 1), shift(up_b, "dp", 2, 1)]
-    down_far = [down_a, shift(down_a, "dp", 2, 1)]
+    down_far = [down_a, down_b, shift(down_a, "dp", 2, 1), shift(down_b, "dp", 2, 1)]
     bias_far = cross(up_bias)
     proj_other, up_far, down_far, bias_far = tie((proj_other, up_far, down_far, bias_far))
     stream, normed = stream_norm(proj_own, proj_other, residual_in, vectors)

time: 203 us -> 203 us (level)
  starting transfers between devices: 41.7 us -> 57.5 us
  between operations: 13.7 us -> 0.34 us
  waiting for transfers between devices: 71.1 us -> 64.4 us
  local copies, waits for them, and re-layouts: 11.4 us -> 17.5 us
  Pallas kernels: 59.9 us -> 57.3 us
    all_to_all x1, waiting for transfers between devices: 13.9 us -> 0.01 us  [shards(): lax.all_to_all(part.reshape(8, 2 * row_block, width + HD), ('yl', 'x'), s...]
    ppermute x3 -> x5, waiting for transfers between devices: 7.13 us -> 20.1 us  [cross(): return lax.ppermute(array, ('yl', 'yh'), [(0, 3), (3, 0), (1, 2), (2, 1)])]
    dynamic_slice x0 -> x4, local copies, waits for them, and re-layouts: none -> 9.93 us  [half_of(): lax.dynamic_slice_in_dim(array, index * n + start, stop - start, axis)]
    ppermute x22 -> x27, starting transfers between devices: 32.4 us -> 42.3 us  [shift(): lax.ppermute(array, axis, [(i, (i + by) % size) for i in range(size)])]
    ppermute x22 -> x27, waiting for transfers between devices: 50 us -> 44.3 us  [shift(): lax.ppermute(array, axis, [(i, (i + by) % size) for i in range(size)])]
    dynamic_slice x3 -> x1, local copies, waits for them, and re-layouts: 6.76 us -> 1.21 us  [part_of(): return lax.dynamic_slice_in_dim(array, index * n, n, axis)]
    ppermute x3 -> x5, starting transfers between devices: 2.86 us -> 7.14 us  [cross(): return lax.ppermute(array, ('yl', 'yh'), [(0, 3), (3, 0), (1, 2), (2, 1)])]
    pallas_call x1, Pallas kernels: 6.76 us -> 4.53 us  [join_project(): pl.pallas_call(join_project_body, grid_spec=pltpu.PrefetchScalarGridSpec(...]
  transfers between devices with their start and end apart: 27 -> 33, of which waited for: 12 -> 11; matrix products, arithmetic and copies ran while one was open for 4% -> 6% of each run, Pallas kernels for 23% -> 22%
where the time goes in v2:
time: 203 us; the launch traced here: 201 us
  waiting for transfers between devices  64.4 us (32%)
  starting transfers between devices  57.5 us (28%)
  Pallas kernels  57.3 us (28%)
  local copies, waits for them, and re-layouts  17.5 us (9%)
  other arithmetic  4.01 us (2%)
    ppermute x27, waiting for transfers between devices, shift(): lax.ppermute(array, axis, [(i, (i + by) % size) for i in range(size)])  44.3 us
    ppermute x27, starting transfers between devices, shift(): lax.ppermute(array, axis, [(i, (i + by) % size) for i in range(size)])  42.3 us
    pallas_call x5, Pallas kernels, attend(): pl.pallas_call(functools.partial(attend_body, len(ks), first, bool(last))...  38.7 us
    ppermute x5, waiting for transfers between devices, cross(): return lax.ppermute(array, ('yl', 'yh'), [(0, 3), (3, 0), (1, 2), (2, 1)])  20.1 us
    pallas_call x1, Pallas kernels, mlp(): pl.pallas_call(mlp_body, grid_spec=pltpu.PrefetchScalarGridSpec(num_scala...  12.9 us
    dynamic_slice x4, local copies, waits for them, and re-layouts, half_of(): lax.dynamic_slice_in_dim(array, index * n + start, stop - start, axis)  9.93 us
    all_to_all x1, starting transfers between devices, shards(): lax.all_to_all(part.reshape(8, 2 * row_block, width + HD), ('yl', 'x'), s...  8.07 us
    ppermute x5, starting transfers between devices, cross(): return lax.ppermute(array, ('yl', 'yh'), [(0, 3), (3, 0), (1, 2), (2, 1)])  7.14 us
  transfers between devices with their start and end apart: 33, of which 11 were waited for; matrix products, arithmetic and copies ran while one was open for 6% of the time, Pallas kernels for 22%

profile of v2, /device:TPU:8, one launch (start us, length us, event | category | flops | bytes accessed | tf_op | source)
XLA Modules:
  0.0 201.1 jit_solution(2416164527158175925)
XLA Ops:
  0.0 1.2 maximum_maximum_fusion.refs_1_.refs_2_
  1.2 2.0 collective-permute-start
  3.2 4.0 %collective-permute-start.1 = (bf16[528,768]{1,0:T(8,128)(2,1)S(1)}, bf16[528,768]{1,0:T(8,128)(2,1)}, u32[]{:S(2)}, u32[]{:S(2)}) collective-permute-start(bf16[528,768]{1,0:T(8,128)(2,1)S(1)} %maximum_maximum_fusion.refs_1_.refs_2_), channel_id=1, source_target_pairs={{0,112},{16,0},{32,16},{48,32},{64,48},{80,64},{96,80},{112,96},{1... | collective-permute-start | bytes 2433032 | tf_op jit(solution)/shard_map/ppermute | solution.py:343
  7.7 2.8 %constant_dynamic-slice_fusion.4 = bf16[1024,768]{1,0:T(8,128)(2,1)} fusion(bf16[3072,768]{1,0:T(8,128)(2,1)} %up_ref.1, s32[]{:T(128)S(6)} %select_n.31), kind=kLoop, calls=%fused_computation.16 | loop fusion | bytes 3145732 | tf_op jit(solution)/shard_map/dynamic_slice | solution.py:357
  10.6 2.4 %collective-permute-start.5 = (bf16[1024,768]{1,0:T(8,128)(2,1)}, bf16[1024,768]{1,0:T(8,128)(2,1)}, u32[]{:S(2)}, u32[]{:S(2)}) collective-permute-start(bf16[1024,768]{1,0:T(8,128)(2,1)} %constant_dynamic-slice_fusion.4), channel_id=1, source_target_pairs={{0,136},{136,0},{8,128},{128,8},{1,137},{137,1},{9,129},{129,9},{2... | collective-permute-start | bytes 4718600 | tf_op jit(solution)/shard_map/ppermute | solution.py:347
  13.0 1.2 constant_dynamic-slice_fusion.3
  14.2 1.5 collective-permute-start.6
  15.7 2.5 %collective-permute-done.2 = bf16[512,384]{1,0:T(8,128)(2,1)} collective-permute-done((bf16[512,384]{1,0:T(8,128)(2,1)}, bf16[512,384]{1,0:T(8,128)(2,1)}, u32[]{:S(2)}, u32[]{:S(2)}) %collective-permute-start.2) | collective-permute-done | bytes 393248 | tf_op jit(solution)/shard_map/ppermute | solution.py:343
  18.1 2.8 %collective-permute-start.7 = (bf16[384,1536]{1,0:T(8,128)(2,1)}, bf16[384,1536]{1,0:T(8,128)(2,1)}, u32[]{:S(2)}, u32[]{:S(2)}) collective-permute-start(bf16[384,1536]{1,0:T(8,128)(2,1)} %constant_dynamic-slice_fusion.3), channel_id=1, source_target_pairs={{0,6},{2,0},{4,2},{6,4},{1,7},{3,1},{5,3},{7,5},{8,14},{10,8},{12,... | collective-permute-start | bytes 3538952 | tf_op jit(solution)/shard_map/ppermute | solution.py:343
  20.9 4.4 %collective-permute-done.refs_1_.refs_3_ = bf16[528,768]{1,0:T(8,128)(2,1)} collective-permute-done((bf16[528,768]{1,0:T(8,128)(2,1)S(1)}, bf16[528,768]{1,0:T(8,128)(2,1)}, u32[]{:S(2)}, u32[]{:S(2)}) %collective-permute-start) | collective-permute-done | bytes 811040 | tf_op jit(solution)/shard_map/ppermute | solution.py:343
  25.3 3.2 %collective-permute-start.4 = (bf16[528,768]{1,0:T(8,128)(2,1)}, bf16[528,768]{1,0:T(8,128)(2,1)}, u32[]{:S(2)}, u32[]{:S(2)}) collective-permute-start(bf16[528,768]{1,0:T(8,128)(2,1)} %collective-permute-done.1.refs_2_.refs_4_), channel_id=1, source_target_pairs={{0,112},{16,0},{32,16},{48,32},{64,48},{80,64},{96,80},{112,96},{1... | collective-permute-start | bytes 2433032 | tf_op jit(solution)/shard_map/ppermute | solution.py:343
  28.6 1.6 maximum_select_fusion.refs_0_
  30.2 5.1 %shard_map.163 = (f32[3,1,1024]{2,1,0:T(1,128)S(1)}, f32[3,1,1024]{2,1,0:T(1,128)S(1)}, f32[384,1024]{1,0:T(8,128)S(1)}) custom-call(bf16[1024,384]{1,0:T(8,128)(2,1)S(1)} %maximum_select_fusion.refs_0_, bf16[528,768]{1,0:T(8,128)(2,1)S(1)} %copy-done.2, bf16[528,768]{1,0:T(8,128)(2,1)S(1)} %copy-done.2), custom_call_target="tpu_custom_call" | custom-call | flops 830472192 | bytes 1597440 | tf_op jit(solution)/shard_map/pallas_call | solution.py:111
  35.3 8.9 %shard_map.164 = (f32[3,1,1024]{2,1,0:T(1,128)S(1)}, f32[3,1,1024]{2,1,0:T(1,128)S(1)}, f32[384,1024]{1,0:T(8,128)S(1)}) custom-call(bf16[1024,384]{1,0:T(8,128)(2,1)S(1)} %maximum_select_fusion.refs_0_, bf16[528,768]{1,0:T(8,128)(2,1)} %collective-permute-done.refs_1_.refs_3_, bf16[528,768]{1,0:T(8,128)(2,1)} %collective-permute-done.1.refs_2_.refs_4_, ...), custom_call_target="tpu_custom_call" | custom-call | flops 1660944384 | bytes 2408448 | tf_op jit(solution)/shard_map/pallas_call | solution.py:111
  44.2 1.2 copy-done.10
  45.5 1.6 collective-permute-done.5.refs_0_
  47.1 3.0 %constant_dynamic-slice_fusion.2 = bf16[768,1152]{1,0:T(8,128)(2,1)} fusion(bf16[768,3072]{1,0:T(8,128)(2,1)} %down_ref.1, s32[]{:T(128)S(6)} %select_n.32), kind=kLoop, calls=%fused_computation.14 | loop fusion | bytes 3538948 | tf_op jit(solution)/shard_map/dynamic_slice | solution.py:357
  50.1 1.7 collective-permute-start.12
  52.5 2.6 %collective-permute-start.9 = (bf16[528,768]{1,0:T(8,128)(2,1)}, bf16[528,768]{1,0:T(8,128)(2,1)S(1)}, u32[]{:S(2)}, u32[]{:S(2)}) collective-permute-start(bf16[528,768]{1,0:T(8,128)(2,1)} %collective-permute-done.4.refs_2_.refs_4_), channel_id=1, source_target_pairs={{0,112},{16,0},{32,16},{48,32},{64,48},{80,64},{96,80},{112,96},{1... | collective-permute-start | bytes 2433032 | tf_op jit(solution)/shard_map/ppermute | solution.py:343
  55.1 3.0 %collective-permute-start.13 = (bf16[384,1536]{1,0:T(8,128)(2,1)}, bf16[384,1536]{1,0:T(8,128)(2,1)}, u32[]{:S(2)}, u32[]{:S(2)}) collective-permute-start(bf16[384,1536]{1,0:T(8,128)(2,1)} %constant_dynamic-slice_fusion.3), channel_id=1, source_target_pairs={{0,4},{2,6},{4,0},{6,2},{1,5},{3,7},{5,1},{7,3},{8,12},{10,14},{12... | collective-permute-start | bytes 3538952 | tf_op jit(solution)/shard_map/ppermute | solution.py:343
  58.1 8.9 %shard_map.165 = (f32[3,1,1024]{2,1,0:T(1,128)S(1)}, f32[3,1,1024]{2,1,0:T(1,128)S(1)}, f32[384,1024]{1,0:T(8,128)S(1)}) custom-call(bf16[1024,384]{1,0:T(8,128)(2,1)S(1)} %maximum_select_fusion.refs_0_, bf16[528,768]{1,0:T(8,128)(2,1)} %collective-permute-done.3.refs_1_.refs_3_, bf16[528,768]{1,0:T(8,128)(2,1)} %collective-permute-done.4.refs_2_.refs_4_, ...), custom_call_target="tpu_custom_call" | custom-call | flops 1660944384 | bytes 2408448 | tf_op jit(solution)/shard_map/pallas_call | solution.py:111
  67.0 1.2 copy-done.8
  68.8 2.5 %collective-permute-done.8.refs_1_.refs_3_ = bf16[528,768]{1,0:T(8,128)(2,1)S(1)} collective-permute-done((bf16[528,768]{1,0:T(8,128)(2,1)}, bf16[528,768]{1,0:T(8,128)(2,1)S(1)}, u32[]{:S(2)}, u32[]{:S(2)}) %collective-permute-start.8) | collective-permute-done | bytes 811040 | tf_op jit(solution)/shard_map/ppermute | solution.py:343
  73.3 2.9 %collective-permute-start.11 = (bf16[256,768]{1,0:T(8,128)(2,1)}, bf16[256,768]{1,0:T(8,128)(2,1)S(1)}, u32[]{:S(2)}, u32[]{:S(2)}) collective-permute-start(bf16[256,768]{1,0:T(8,128)(2,1)} %slice.29), channel_id=1, source_target_pairs={{0,112},{16,0},{32,16},{48,32},{64,48},{80,64},{96,80},{112,96},{1... | collective-permute-start | bytes 1179656 | tf_op jit(solution)/shard_map/ppermute | solution.py:343
  76.2 2.1 %constant_dynamic-slice_fusion = bf16[768,384]{1,0:T(8,128)(2,1)} fusion(bf16[768,3072]{1,0:T(8,128)(2,1)} %down_ref.1, s32[]{:T(128)S(6)} %select_n.34), kind=kLoop, calls=%fused_computation.12 | loop fusion | bytes 1179652 | tf_op jit(solution)/shard_map/dynamic_slice | solution.py:357
  78.2 2.1 %constant_dynamic-slice_fusion.1 = bf16[512,768]{1,0:T(8,128)(2,1)} fusion(bf16[3072,768]{1,0:T(8,128)(2,1)} %up_ref.1, s32[]{:T(128)S(6)} %select_n.33), kind=kLoop, calls=%fused_computation.13 | loop fusion | bytes 1572868 | tf_op jit(solution)/shard_map/dynamic_slice | solution.py:357
  80.3 1.4 copy-done.9
  81.7 8.0 %shard_map.166 = (f32[3,1,1024]{2,1,0:T(1,128)S(1)}, f32[3,1,1024]{2,1,0:T(1,128)S(1)}, f32[384,1024]{1,0:T(8,128)S(1)}) custom-call(bf16[1024,384]{1,0:T(8,128)(2,1)S(1)} %maximum_select_fusion.refs_0_, bf16[528,768]{1,0:T(8,128)(2,1)S(1)} %copy-done.5, bf16[528,768]{1,0:T(8,128)(2,1)S(1)} %copy-done.7, bf16[528,768]{1,0:T(8,128)(2,1)S(1)} %copy-done.5, ...), custom_call_target="tpu_custom_call" | custom-call | flops 1660944384 | bytes 2408448 | tf_op jit(solution)/shard_map/pallas_call | solution.py:111
  89.7 7.9 %shard_map.167 = bf16[2,4,2,64,512]{4,3,2,1,0:T(8,128)(2,1)} custom-call(bf16[1024,384]{1,0:T(8,128)(2,1)S(1)} %maximum_select_fusion.refs_0_, bf16[272,768]{1,0:T(8,128)(2,1)} %collective-permute-done.10.refs_1_.refs_3_, bf16[256,768]{1,0:T(8,128)(2,1)S(1)} %collective-permute-done.11.refs_2_.refs_4_, ...), custom_call_target="tpu_custom_call" | custom-call | flops 830472192 | bytes 1597440 | tf_op jit(solution)/shard_map/pallas_call | solution.py:111
  98.3 1.4 collective-permute-start.18
  100.3 8.1 %all-to-all-start = ((bf16[8,128,512]{2,1,0:T(8,128)(2,1)}), bf16[8,128,512]{2,1,0:T(8,128)(2,1)S(1)}, u32[]{:S(2)}, u32[]{:S(2)}) async-start(bf16[8,128,512]{2,1,0:T(8,128)(2,1)} %bitcast.1), calls=%async_computation | async-start | bytes 2097152 | tf_op jit(solution)/shard_map/all_to_all | solution.py:451
  108.3 18.5 %collective-permute-done.18.refs_5_ = bf16[768,384]{1,0:T(8,128)(2,1)} collective-permute-done((bf16[768,384]{1,0:T(8,128)(2,1)}, bf16[768,384]{1,0:T(8,128)(2,1)}, u32[]{:S(2)}, u32[]{:S(2)}) %collective-permute-start.18) | collective-permute-done | bytes 589856 | tf_op jit(solution)/shard_map/ppermute | solution.py:347
  129.0 4.5 %shard_map.168 = (f32[64,3072]{1,0:T(8,128)S(1)}, bf16[64,3072]{1,0:T(8,128)(2,1)S(1)}) custom-call(s32[4]{0:T(128)S(1)} %iota_xor_fusion.order, s32[5]{0:T(128)S(1)} %pad_add_fusion.place, bf16[8,128,512]{2,1,0:T(8,128)(2,1)S(1)} %all-to-all-done.part_ref, bf16[384,3072]{1,0:T(8,128)(2,1)S(1)} %copy-done, bf16[384,1536]{1,0:T(8,128)(2,1)} %collective-permute-done.6.refs_0_, ...), custom_call_target="tpu_custom_call" | custom-call | flops 1207959552 | bytes 9437184 | tf_op jit(solution)/shard_map/pallas_call | solution.py:185
  133.6 5.3 %collective-permute-start.19 = (bf16[64,3072]{1,0:T(8,128)(2,1)S(1)}, bf16[64,3072]{1,0:T(8,128)(2,1)S(1)}, u32[]{:S(2)}, u32[]{:S(2)}) collective-permute-start(bf16[64,3072]{1,0:T(8,128)(2,1)S(1)} %get-tuple-element.116), channel_id=1, source_target_pairs={{0,8},{8,0},{1,9},{9,1},{2,10},{10,2},{3,11},{11,3},{4,12},{12,4},... | collective-permute-start | bytes 1179656 | tf_op jit(solution)/shard_map/ppermute | solution.py:343
  138.9 9.2 %collective-permute-done.19.other_ref = bf16[64,3072]{1,0:T(8,128)(2,1)S(1)} collective-permute-done((bf16[64,3072]{1,0:T(8,128)(2,1)S(1)}, bf16[64,3072]{1,0:T(8,128)(2,1)S(1)}, u32[]{:S(2)}, u32[]{:S(2)}) %collective-permute-start.19) | collective-permute-done | bytes 393248 | tf_op jit(solution)/shard_map/ppermute | solution.py:343
  148.2 1.1 shard_map.169
  149.3 1.6 collective-permute-start.25
  150.9 1.7 collective-permute-start.26
  152.7 8.5 %collective-permute-done.25 = bf16[64,3072]{1,0:T(8,128)(2,1)S(1)} collective-permute-done((bf16[64,3072]{1,0:T(8,128)(2,1)S(1)}, bf16[64,3072]{1,0:T(8,128)(2,1)S(1)}, u32[]{:S(2)}, u32[]{:S(2)}) %collective-permute-start.25) | collective-permute-done | bytes 393248 | tf_op jit(solution)/shard_map/ppermute | solution.py:343
  161.5 3.0 %collective-permute-start.28 = (bf16[32,3072]{1,0:T(8,128)(2,1)S(1)}, bf16[32,3072]{1,0:T(8,128)(2,1)S(1)}, u32[]{:S(2)}, u32[]{:S(2)}) collective-permute-start(bf16[32,3072]{1,0:T(8,128)(2,1)S(1)} %slice.37), channel_id=1, source_target_pairs={{0,6},{2,0},{4,2},{6,4},{1,7},{3,1},{5,3},{7,5},{8,14},{10,8},{12,... | collective-permute-start | bytes 589832 | tf_op jit(solution)/shard_map/ppermute | solution.py:343
  164.6 3.5 %collective-permute-done.27 = bf16[32,3072]{1,0:T(8,128)(2,1)S(1)} collective-permute-done((bf16[32,3072]{1,0:T(8,128)(2,1)S(1)}, bf16[32,3072]{1,0:T(8,128)(2,1)S(1)}, u32[]{:S(2)}, u32[]{:S(2)}) %collective-permute-start.27) | collective-permute-done | bytes 196640 | tf_op jit(solution)/shard_map/ppermute | solution.py:343
  168.2 12.9 %shard_map.170 = bf16[256,3072]{1,0:T(8,128)(2,1)S(1)} custom-call(s32[4]{0:T(128)S(1)} %iota_xor_fusion.order, bf16[256,3072]{1,0:T(8,128)(2,1)S(1)} %constant_dynamic-update-slice_fusion.x_ref, bf16[3072,768]{1,0:T(8,128)(2,1)} %up_ref.1, bf16[768,3072]{1,0:T(8,128)(2,1)} %down_ref.1, f32[1,768]{1,0:T(1,128)S(1)} %reshape.25.bias_ref, ...), custom_call_target="tpu_custom_call" | custom-call | flops 4831838208 | bytes 18874368 | tf_op jit(solution)/shard_map/pallas_call | solution.py:308
  181.2 2.0 collective-permute-start.31
  183.1 2.3 %collective-permute-start.30 = (bf16[64,3072]{1,0:T(8,128)(2,1)S(1)}, bf16[64,3072]{1,0:T(8,128)(2,1)S(1)}, u32[]{:S(2)}, u32[]{:S(2)}) collective-permute-start(bf16[64,3072]{1,0:T(8,128)(2,1)S(1)} %get-tuple-element.135), channel_id=1, source_target_pairs={{0,2},{2,4},{4,6},{6,0},{1,3},{3,5},{5,7},{7,1},{8,10},{10,12},{12... | collective-permute-start | bytes 1179656 | tf_op jit(solution)/shard_map/ppermute | solution.py:343
  185.4 1.0 collective-permute-start.29
  186.4 8.5 %collective-permute-done.31 = bf16[64,3072]{1,0:T(8,128)(2,1)S(1)} collective-permute-done((bf16[64,3072]{1,0:T(8,128)(2,1)S(1)}, bf16[64,3072]{1,0:T(8,128)(2,1)S(1)}, u32[]{:S(2)}, u32[]{:S(2)}) %collective-permute-start.31) | collective-permute-done | bytes 393248 | tf_op jit(solution)/shard_map/ppermute | solution.py:343
  194.8 4.8 %collective-permute-done.30 = bf16[64,3072]{1,0:T(8,128)(2,1)S(1)} collective-permute-done((bf16[64,3072]{1,0:T(8,128)(2,1)S(1)}, bf16[64,3072]{1,0:T(8,128)(2,1)S(1)}, u32[]{:S(2)}, u32[]{:S(2)}) %collective-permute-start.30) | collective-permute-done | bytes 393248 | tf_op jit(solution)/shard_map/ppermute | solution.py:343
  200.0 1.0 add_convert_fusion
  (94 shorter events, 8.2 us)
Async XLA Ops:
  1.2 9.3 %copy-start.1 = (bf16[528,768]{1,0:T(8,128)(2,1)}, bf16[528,768]{1,0:T(8,128)(2,1)S(1)}, u32[]{:S(2)}) copy-start(bf16[528,768]{1,0:T(8,128)(2,1)S(1)} %maximum_maximum_fusion.refs_1_.refs_2_) | copy-start | bytes 2433028
  1.2 24.1 %collective-permute-start = (bf16[528,768]{1,0:T(8,128)(2,1)S(1)}, bf16[528,768]{1,0:T(8,128)(2,1)}, u32[]{:S(2)}, u32[]{:S(2)}) collective-permute-start(bf16[528,768]{1,0:T(8,128)(2,1)S(1)} %maximum_maximum_fusion.refs_1_.refs_2_), channel_id=1, source_target_pairs={{0,16},{16,32},{32,48},{48,64},{64,80},{80,96},{96,112},{112,0},{1... | collective-permute-start | bytes 2433032 | tf_op jit(solution)/shard_map/ppermute | solution.py:343
  3.2 22.1 %collective-permute-start.1 = (bf16[528,768]{1,0:T(8,128)(2,1)S(1)}, bf16[528,768]{1,0:T(8,128)(2,1)}, u32[]{:S(2)}, u32[]{:S(2)}) collective-permute-start(bf16[528,768]{1,0:T(8,128)(2,1)S(1)} %maximum_maximum_fusion.refs_1_.refs_2_), channel_id=1, source_target_pairs={{0,112},{16,0},{32,16},{48,32},{64,48},{80,64},{96,80},{112,96},{1... | collective-permute-start | bytes 2433032 | tf_op jit(solution)/shard_map/ppermute | solution.py:343
  7.3 10.9 %collective-permute-start.2 = (bf16[512,384]{1,0:T(8,128)(2,1)}, bf16[512,384]{1,0:T(8,128)(2,1)}, u32[]{:S(2)}, u32[]{:S(2)}) collective-permute-start(bf16[512,384]{1,0:T(8,128)(2,1)} %param.17), channel_id=1, source_target_pairs={{0,128},{128,0},{1,129},{129,1},{2,130},{130,2},{3,131},{131,3},{4... | collective-permute-start | bytes 1179656 | tf_op jit(solution)/shard_map/ppermute | solution.py:343
  7.7 5.3 %copy-start = (bf16[384,3072]{1,0:T(8,128)(2,1)S(1)}, bf16[384,3072]{1,0:T(8,128)(2,1)}, u32[]{:S(2)}) copy-start(bf16[384,3072]{1,0:T(8,128)(2,1)} %own_w.1) | copy-start | bytes 7077892
  10.6 36.6 %collective-permute-start.5 = (bf16[1024,768]{1,0:T(8,128)(2,1)}, bf16[1024,768]{1,0:T(8,128)(2,1)}, u32[]{:S(2)}, u32[]{:S(2)}) collective-permute-start(bf16[1024,768]{1,0:T(8,128)(2,1)} %constant_dynamic-slice_fusion.4), channel_id=1, source_target_pairs={{0,136},{136,0},{8,128},{128,8},{1,137},{137,1},{9,129},{129,9},{2... | collective-permute-start | bytes 4718600 | tf_op jit(solution)/shard_map/ppermute | solution.py:347
  14.2 31.3 %collective-permute-start.6 = (bf16[384,1536]{1,0:T(8,128)(2,1)}, bf16[384,1536]{1,0:T(8,128)(2,1)}, u32[]{:S(2)}, u32[]{:S(2)}) collective-permute-start(bf16[384,1536]{1,0:T(8,128)(2,1)} %constant_dynamic-slice_fusion.3), channel_id=1, source_target_pairs={{0,2},{2,4},{4,6},{6,0},{1,3},{3,5},{5,7},{7,1},{8,10},{10,12},{12... | collective-permute-start | bytes 3538952 | tf_op jit(solution)/shard_map/ppermute | solution.py:343
  18.1 27.3 %collective-permute-start.7 = (bf16[384,1536]{1,0:T(8,128)(2,1)}, bf16[384,1536]{1,0:T(8,128)(2,1)}, u32[]{:S(2)}, u32[]{:S(2)}) collective-permute-start(bf16[384,1536]{1,0:T(8,128)(2,1)} %constant_dynamic-slice_fusion.3), channel_id=1, source_target_pairs={{0,6},{2,0},{4,2},{6,4},{1,7},{3,1},{5,3},{7,5},{8,14},{10,8},{12,... | collective-permute-start | bytes 3538952 | tf_op jit(solution)/shard_map/ppermute | solution.py:343
  25.3 21.8 %collective-permute-start.3 = (bf16[528,768]{1,0:T(8,128)(2,1)}, bf16[528,768]{1,0:T(8,128)(2,1)}, u32[]{:S(2)}, u32[]{:S(2)}) collective-permute-start(bf16[528,768]{1,0:T(8,128)(2,1)} %collective-permute-done.refs_1_.refs_3_), channel_id=1, source_target_pairs={{0,16},{16,32},{32,48},{48,64},{64,80},{80,96},{96,112},{112,0},{1... | collective-permute-start | bytes 2433032 | tf_op jit(solution)/shard_map/ppermute | solution.py:343
  25.3 21.8 %collective-permute-start.4 = (bf16[528,768]{1,0:T(8,128)(2,1)}, bf16[528,768]{1,0:T(8,128)(2,1)}, u32[]{:S(2)}, u32[]{:S(2)}) collective-permute-start(bf16[528,768]{1,0:T(8,128)(2,1)} %collective-permute-done.1.refs_2_.refs_4_), channel_id=1, source_target_pairs={{0,112},{16,0},{32,16},{48,32},{64,48},{80,64},{96,80},{112,96},{1... | collective-permute-start | bytes 2433032 | tf_op jit(solution)/shard_map/ppermute | solution.py:343
  47.1 11.0 %copy-start.11 = (f32[384,1024]{1,0:T(8,128)S(1)}, f32[384,1024]{1,0:T(8,128)}, u32[]{:S(2)}) copy-start(f32[384,1024]{1,0:T(8,128)} %copy-done.10) | copy-start | bytes 4718596
  50.1 47.5 %collective-permute-start.12 = (bf16[768,1152]{1,0:T(8,128)(2,1)}, bf16[768,1152]{1,0:T(8,128)(2,1)}, u32[]{:S(2)}, u32[]{:S(2)}) collective-permute-start(bf16[768,1152]{1,0:T(8,128)(2,1)} %constant_dynamic-slice_fusion.2), channel_id=1, source_target_pairs={{0,136},{136,0},{8,128},{128,8},{1,137},{137,1},{9,129},{129,9},{2... | collective-permute-start | bytes 5308424 | tf_op jit(solution)/shard_map/ppermute | solution.py:347
  51.8 19.5 %collective-permute-start.8 = (bf16[528,768]{1,0:T(8,128)(2,1)}, bf16[528,768]{1,0:T(8,128)(2,1)S(1)}, u32[]{:S(2)}, u32[]{:S(2)}) collective-permute-start(bf16[528,768]{1,0:T(8,128)(2,1)} %collective-permute-done.3.refs_1_.refs_3_), channel_id=1, source_target_pairs={{0,16},{16,32},{32,48},{48,64},{64,80},{80,96},{96,112},{112,0},{1... | collective-permute-start | bytes 2433032 | tf_op jit(solution)/shard_map/ppermute | solution.py:343
  52.5 18.8 %collective-permute-start.9 = (bf16[528,768]{1,0:T(8,128)(2,1)}, bf16[528,768]{1,0:T(8,128)(2,1)S(1)}, u32[]{:S(2)}, u32[]{:S(2)}) collective-permute-start(bf16[528,768]{1,0:T(8,128)(2,1)} %collective-permute-done.4.refs_2_.refs_4_), channel_id=1, source_target_pairs={{0,112},{16,0},{32,16},{48,32},{64,48},{80,64},{96,80},{112,96},{1... | collective-permute-start | bytes 2433032 | tf_op jit(solution)/shard_map/ppermute | solution.py:343
  55.1 42.6 %collective-permute-start.13 = (bf16[384,1536]{1,0:T(8,128)(2,1)}, bf16[384,1536]{1,0:T(8,128)(2,1)}, u32[]{:S(2)}, u32[]{:S(2)}) collective-permute-start(bf16[384,1536]{1,0:T(8,128)(2,1)} %constant_dynamic-slice_fusion.3), channel_id=1, source_target_pairs={{0,4},{2,6},{4,0},{6,2},{1,5},{3,7},{5,1},{7,3},{8,12},{10,14},{12... | collective-permute-start | bytes 3538952 | tf_op jit(solution)/shard_map/ppermute | solution.py:343
  72.1 17.6 %collective-permute-start.10 = (bf16[272,768]{1,0:T(8,128)(2,1)}, bf16[272,768]{1,0:T(8,128)(2,1)}, u32[]{:S(2)}, u32[]{:S(2)}) collective-permute-start(bf16[272,768]{1,0:T(8,128)(2,1)} %slice.28), channel_id=1, source_target_pairs={{0,16},{16,32},{32,48},{48,64},{64,80},{80,96},{96,112},{112,0},{1... | collective-permute-start | bytes 1253384 | tf_op jit(solution)/shard_map/ppermute | solution.py:343
  73.3 16.4 %collective-permute-start.11 = (bf16[256,768]{1,0:T(8,128)(2,1)}, bf16[256,768]{1,0:T(8,128)(2,1)S(1)}, u32[]{:S(2)}, u32[]{:S(2)}) collective-permute-start(bf16[256,768]{1,0:T(8,128)(2,1)} %slice.29), channel_id=1, source_target_pairs={{0,112},{16,0},{32,16},{48,32},{64,48},{80,64},{96,80},{112,96},{1... | collective-permute-start | bytes 1179656 | tf_op jit(solution)/shard_map/ppermute | solution.py:343
  76.2 4.1 %copy-start.5 = (bf16[528,768]{1,0:T(8,128)(2,1)S(1)}, bf16[528,768]{1,0:T(8,128)(2,1)}, u32[]{:S(2)}) copy-start(bf16[528,768]{1,0:T(8,128)(2,1)} %copy-done.4) | copy-start | bytes 2433028
  76.2 4.1 %copy-start.7 = (bf16[528,768]{1,0:T(8,128)(2,1)S(1)}, bf16[528,768]{1,0:T(8,128)(2,1)}, u32[]{:S(2)}) copy-start(bf16[528,768]{1,0:T(8,128)(2,1)} %copy-done.6) | copy-start | bytes 2433028
  76.2 4.1 %copy-start.13 = (f32[3,1,1024]{2,1,0:T(1,128)S(1)}, f32[3,1,1024]{2,1,0:T(1,128)}, u32[]{:S(2)}) copy-start(f32[3,1,1024]{2,1,0:T(1,128)} %copy-done.12) | copy-start | bytes 36868
  97.6 29.7 %copy-start.20 = (f32[768]{0:T(1024)S(1)}, f32[768]{0:T(1024)}, u32[]{:S(2)}) copy-start(f32[768]{0:T(1024)} %param.30) | copy-start | bytes 9220
  97.6 30.7 %copy-start.21 = (s32[4]{0:T(128)S(1)}, s32[4]{0:T(128)}, u32[]{:S(2)}) copy-start(s32[4]{0:T(128)} %constant.47.clone) | copy-start | bytes 52
  97.6 29.2 %collective-permute-start.17 = (bf16[512,768]{1,0:T(8,128)(2,1)}, bf16[512,768]{1,0:T(8,128)(2,1)}, u32[]{:S(2)}, u32[]{:S(2)}) collective-permute-start(bf16[512,768]{1,0:T(8,128)(2,1)} %constant_dynamic-slice_fusion.1), channel_id=1, source_target_pairs={{0,136},{136,0},{8,128},{128,8},{1,137},{137,1},{9,129},{129,9},{2... | collective-permute-start | bytes 2359304 | tf_op jit(solution)/shard_map/ppermute | solution.py:347
  98.3 28.5 %collective-permute-start.18 = (bf16[768,384]{1,0:T(8,128)(2,1)}, bf16[768,384]{1,0:T(8,128)(2,1)}, u32[]{:S(2)}, u32[]{:S(2)}) collective-permute-start(bf16[768,384]{1,0:T(8,128)(2,1)} %constant_dynamic-slice_fusion), channel_id=1, source_target_pairs={{0,136},{136,0},{8,128},{128,8},{1,137},{137,1},{9,129},{129,9},{2... | collective-permute-start | bytes 1769480 | tf_op jit(solution)/shard_map/ppermute | solution.py:347
  99.8 27.6 %collective-permute-start.14 = (bf16[384,1536]{1,0:T(8,128)(2,1)}, bf16[384,1536]{1,0:T(8,128)(2,1)}, u32[]{:S(2)}, u32[]{:S(2)}) collective-permute-start(bf16[384,1536]{1,0:T(8,128)(2,1)} %collective-permute-done.6.refs_0_), channel_id=1, source_target_pairs={{0,1},{1,0},{2,3},{3,2},{4,5},{5,4},{6,7},{7,6},{8,9},{9,8},{10,11... | collective-permute-start | bytes 3538952 | tf_op jit(solution)/shard_map/ppermute | solution.py:343
  99.8 28.5 %collective-permute-start.15 = (bf16[384,1536]{1,0:T(8,128)(2,1)}, bf16[384,1536]{1,0:T(8,128)(2,1)}, u32[]{:S(2)}, u32[]{:S(2)}) collective-permute-start(bf16[384,1536]{1,0:T(8,128)(2,1)} %collective-permute-done.7.refs_1_), channel_id=1, source_target_pairs={{0,1},{1,0},{2,3},{3,2},{4,5},{5,4},{6,7},{7,6},{8,9},{9,8},{10,11... | collective-permute-start | bytes 3538952 | tf_op jit(solution)/shard_map/ppermute | solution.py:343
  100.3 28.0 %collective-permute-start.16 = (bf16[384,1536]{1,0:T(8,128)(2,1)}, bf16[384,1536]{1,0:T(8,128)(2,1)}, u32[]{:S(2)}, u32[]{:S(2)}) collective-permute-start(bf16[384,1536]{1,0:T(8,128)(2,1)} %collective-permute-done.13.refs_2_), channel_id=1, source_target_pairs={{0,1},{1,0},{2,3},{3,2},{4,5},{5,4},{6,7},{7,6},{8,9},{9,8},{10,11... | collective-permute-start | bytes 3538952 | tf_op jit(solution)/shard_map/ppermute | solution.py:343
  100.3 28.0 %all-to-all-start = ((bf16[8,128,512]{2,1,0:T(8,128)(2,1)}), bf16[8,128,512]{2,1,0:T(8,128)(2,1)S(1)}, u32[]{:S(2)}, u32[]{:S(2)}) async-start(bf16[8,128,512]{2,1,0:T(8,128)(2,1)} %bitcast.1), calls=%async_computation | async-start | bytes 2097152 | tf_op jit(solution)/shard_map/all_to_all | solution.py:451
  126.8 21.3 %collective-permute-start.22 = (bf16[768,1152]{1,0:T(8,128)(2,1)}, bf16[768,1152]{1,0:T(8,128)(2,1)}, u32[]{:S(2)}, u32[]{:S(2)}) collective-permute-start(bf16[768,1152]{1,0:T(8,128)(2,1)} %collective-permute-done.12.refs_4_), channel_id=1, source_target_pairs={{0,1},{1,0},{2,3},{3,2},{4,5},{5,4},{6,7},{7,6},{8,9},{9,8},{10,11... | collective-permute-start | bytes 5308424 | tf_op jit(solution)/shard_map/ppermute | solution.py:343
  126.8 12.1 %collective-permute-start.20 = (bf16[1024,768]{1,0:T(8,128)(2,1)}, bf16[1024,768]{1,0:T(8,128)(2,1)}, u32[]{:S(2)}, u32[]{:S(2)}) collective-permute-start(bf16[1024,768]{1,0:T(8,128)(2,1)} %collective-permute-done.5.refs_0_), channel_id=1, source_target_pairs={{0,1},{1,0},{2,3},{3,2},{4,5},{5,4},{6,7},{7,6},{8,9},{9,8},{10,11... | collective-permute-start | bytes 4718600 | tf_op jit(solution)/shard_map/ppermute | solution.py:343
  127.3 6.2 %collective-permute-start.24 = (f32[768]{0:T(1024)S(1)}, f32[768]{0:T(1024)S(1)}, u32[]{:S(2)}, u32[]{:S(2)}) collective-permute-start(f32[768]{0:T(1024)S(1)} %copy-done.20), channel_id=1, source_target_pairs={{0,136},{136,0},{8,128},{128,8},{1,137},{137,1},{9,129},{129,9},{2... | collective-permute-start | bytes 9224 | tf_op jit(solution)/shard_map/ppermute | solution.py:347
  128.2 19.9 %collective-permute-start.21 = (bf16[512,768]{1,0:T(8,128)(2,1)}, bf16[512,768]{1,0:T(8,128)(2,1)}, u32[]{:S(2)}, u32[]{:S(2)}) collective-permute-start(bf16[512,768]{1,0:T(8,128)(2,1)} %collective-permute-done.17.refs_1_), channel_id=1, source_target_pairs={{0,1},{1,0},{2,3},{3,2},{4,5},{5,4},{6,7},{7,6},{8,9},{9,8},{10,11... | collective-permute-start | bytes 2359304 | tf_op jit(solution)/shard_map/ppermute | solution.py:343
  128.4 19.8 %collective-permute-start.23 = (bf16[768,384]{1,0:T(8,128)(2,1)}, bf16[768,384]{1,0:T(8,128)(2,1)S(1)}, u32[]{:S(2)}, u32[]{:S(2)}) collective-permute-start(bf16[768,384]{1,0:T(8,128)(2,1)} %collective-permute-done.18.refs_5_), channel_id=1, source_target_pairs={{0,1},{1,0},{2,3},{3,2},{4,5},{5,4},{6,7},{7,6},{8,9},{9,8},{10,11... | collective-permute-start | bytes 1769480 | tf_op jit(solution)/shard_map/ppermute | solution.py:343
  129.0 9.8 %copy-start.16 = (f32[3072]{0:T(1024)S(1)}, f32[3072]{0:T(1024)}, u32[]{:S(2)}) copy-start(f32[3072]{0:T(1024)} %param.23) | copy-start | bytes 36868
  129.0 9.8 %copy-start.17 = (f32[3072]{0:T(1024)S(1)}, f32[3072]{0:T(1024)}, u32[]{:S(2)}) copy-start(f32[3072]{0:T(1024)} %param.24) | copy-start | bytes 36868
  129.0 9.8 %copy-start.18 = (f32[3072]{0:T(1024)S(1)}, f32[3072]{0:T(1024)}, u32[]{:S(2)}) copy-start(f32[3072]{0:T(1024)} %param.28) | copy-start | bytes 36868
  129.0 9.8 %copy-start.19 = (f32[3072]{0:T(1024)S(1)}, f32[3072]{0:T(1024)}, u32[]{:S(2)}) copy-start(f32[3072]{0:T(1024)} %param.25) | copy-start | bytes 36868
  129.0 19.1 %copy-start.3 = (bf16[64,3072]{1,0:T(8,128)(2,1)S(1)}, bf16[64,3072]{1,0:T(8,128)(2,1)}, u32[]{:S(2)}) copy-start(bf16[64,3072]{1,0:T(8,128)(2,1)} %residual_ref.1) | copy-start | bytes 1179652
  133.6 14.6 %collective-permute-start.19 = (bf16[64,3072]{1,0:T(8,128)(2,1)S(1)}, bf16[64,3072]{1,0:T(8,128)(2,1)S(1)}, u32[]{:S(2)}, u32[]{:S(2)}) collective-permute-start(bf16[64,3072]{1,0:T(8,128)(2,1)S(1)} %get-tuple-element.116), channel_id=1, source_target_pairs={{0,8},{8,0},{1,9},{9,1},{2,10},{10,2},{3,11},{11,3},{4,12},{12,4},... | collective-permute-start | bytes 1179656 | tf_op jit(solution)/shard_map/ppermute | solution.py:343
  149.3 11.8 %collective-permute-start.25 = (bf16[64,3072]{1,0:T(8,128)(2,1)S(1)}, bf16[64,3072]{1,0:T(8,128)(2,1)S(1)}, u32[]{:S(2)}, u32[]{:S(2)}) collective-permute-start(bf16[64,3072]{1,0:T(8,128)(2,1)S(1)} %get-tuple-element.123), channel_id=1, source_target_pairs={{0,2},{2,4},{4,6},{6,0},{1,3},{3,5},{5,7},{7,1},{8,10},{10,12},{12... | collective-permute-start | bytes 1179656 | tf_op jit(solution)/shard_map/ppermute | solution.py:343
  150.9 10.6 %collective-permute-start.26 = (bf16[64,3072]{1,0:T(8,128)(2,1)S(1)}, bf16[64,3072]{1,0:T(8,128)(2,1)S(1)}, u32[]{:S(2)}, u32[]{:S(2)}) collective-permute-start(bf16[64,3072]{1,0:T(8,128)(2,1)S(1)} %get-tuple-element.123), channel_id=1, source_target_pairs={{0,6},{2,0},{4,2},{6,4},{1,7},{3,1},{5,3},{7,5},{8,14},{10,8},{12,... | collective-permute-start | bytes 1179656 | tf_op jit(solution)/shard_map/ppermute | solution.py:343
  161.2 7.0 %collective-permute-start.27 = (bf16[32,3072]{1,0:T(8,128)(2,1)S(1)}, bf16[32,3072]{1,0:T(8,128)(2,1)S(1)}, u32[]{:S(2)}, u32[]{:S(2)}) collective-permute-start(bf16[32,3072]{1,0:T(8,128)(2,1)S(1)} %slice.36), channel_id=1, source_target_pairs={{0,2},{2,4},{4,6},{6,0},{1,3},{3,5},{5,7},{7,1},{8,10},{10,12},{12... | collective-permute-start | bytes 589832 | tf_op jit(solution)/shard_map/ppermute | solution.py:343
  161.5 6.6 %collective-permute-start.28 = (bf16[32,3072]{1,0:T(8,128)(2,1)S(1)}, bf16[32,3072]{1,0:T(8,128)(2,1)S(1)}, u32[]{:S(2)}, u32[]{:S(2)}) collective-permute-start(bf16[32,3072]{1,0:T(8,128)(2,1)S(1)} %slice.37), channel_id=1, source_target_pairs={{0,6},{2,0},{4,2},{6,4},{1,7},{3,1},{5,3},{7,5},{8,14},{10,8},{12,... | collective-permute-start | bytes 589832 | tf_op jit(solution)/shard_map/ppermute | solution.py:343
  181.0 19.0 %copy-start.14 = (f32[3072]{0:T(1024)S(1)}, f32[3072]{0:T(1024)}, u32[]{:S(2)}) copy-start(f32[3072]{0:T(1024)} %param.32) | copy-start | bytes 36868
  181.1 18.9 %copy-start.15 = (f32[3072]{0:T(1024)S(1)}, f32[3072]{0:T(1024)}, u32[]{:S(2)}) copy-start(f32[3072]{0:T(1024)} %param.26) | copy-start | bytes 36868
  181.2 13.6 %collective-permute-start.31 = (bf16[64,3072]{1,0:T(8,128)(2,1)S(1)}, bf16[64,3072]{1,0:T(8,128)(2,1)S(1)}, u32[]{:S(2)}, u32[]{:S(2)}) collective-permute-start(bf16[64,3072]{1,0:T(8,128)(2,1)S(1)} %get-tuple-element.134), channel_id=1, source_target_pairs={{0,4},{2,6},{4,0},{6,2},{1,5},{3,7},{5,1},{7,3},{8,12},{10,14},{12... | collective-permute-start | bytes 1179656 | tf_op jit(solution)/shard_map/ppermute | solution.py:343
  183.1 16.5 %collective-permute-start.30 = (bf16[64,3072]{1,0:T(8,128)(2,1)S(1)}, bf16[64,3072]{1,0:T(8,128)(2,1)S(1)}, u32[]{:S(2)}, u32[]{:S(2)}) collective-permute-start(bf16[64,3072]{1,0:T(8,128)(2,1)S(1)} %get-tuple-element.135), channel_id=1, source_target_pairs={{0,2},{2,4},{4,6},{6,0},{1,3},{3,5},{5,7},{7,1},{8,10},{10,12},{12... | collective-permute-start | bytes 1179656 | tf_op jit(solution)/shard_map/ppermute | solution.py:343
  185.4 14.6 %collective-permute-start.29 = (bf16[64,3072]{1,0:T(8,128)(2,1)S(1)}, bf16[64,3072]{1,0:T(8,128)(2,1)S(1)}, u32[]{:S(2)}, u32[]{:S(2)}) collective-permute-start(bf16[64,3072]{1,0:T(8,128)(2,1)S(1)} %get-tuple-element.133), channel_id=1, source_target_pairs={{0,6},{2,0},{4,2},{6,4},{1,7},{3,1},{5,3},{7,5},{8,14},{10,8},{12,... | collective-permute-start | bytes 1179656 | tf_op jit(solution)/shard_map/ppermute | solution.py:343
  (7 other events, 9.3 us)

commit v3 on v2

--- a/solution.py
+++ b/solution.py
@@ -119,7 +119,7 @@
             transcendentals=rows * keys * heads,
             bytes_accessed=2 * (rows + 2 * keys) * width,
         ),
-        compiler_params=pltpu.CompilerParams(vmem_limit_bytes=48 << 20),
+        compiler_params=pltpu.CompilerParams(vmem_limit_bytes=16 << 20),
     )(q, *ks, *vs, *(() if first else state))
 
 
@@ -205,7 +205,7 @@
         cost_estimate=pl.CostEstimate(
             flops=8 * both * width * d_model, transcendentals=0, bytes_accessed=8 * width * d_model
         ),
-        compiler_params=pltpu.CompilerParams(vmem_limit_bytes=40 << 20),
+        compiler_params=pltpu.CompilerParams(vmem_limit_bytes=30 << 20),
     )(order, place, parts, own_w, *mine, *mate)
 
 
@@ -236,7 +236,7 @@
         cost_estimate=pl.CostEstimate(
             flops=20 * rows * d_model, transcendentals=0, bytes_accessed=14 * rows * d_model
         ),
-        compiler_params=pltpu.CompilerParams(vmem_limit_bytes=32 << 20),
+        compiler_params=pltpu.CompilerParams(vmem_limit_bytes=8 << 20),
     )(own, other, residual, vectors)
 
 
@@ -335,7 +335,7 @@
             transcendentals=rows * hidden * 2,
             bytes_accessed=8 * d_model * hidden,
         ),
-        compiler_params=pltpu.CompilerParams(vmem_limit_bytes=40 << 20),
+        compiler_params=pltpu.CompilerParams(vmem_limit_bytes=30 << 20),
     )(order, x, up, down, bias.reshape(1, -1), bias_far.reshape(1, -1), *up_far, *down_far)
 
 
@@ -347,14 +347,45 @@
     return lax.ppermute(array, ("yl", "yh"), [(0, 3), (3, 0), (1, 2), (2, 1)])
 
 
-def part_of(array, parts, index, axis):
-    n = array.shape[axis] // parts
-    return lax.dynamic_slice_in_dim(array, index * n, n, axis)
-
-
-def half_of(array, index, axis, start, stop):
-    n = array.shape[axis] // 2
-    return lax.dynamic_slice_in_dim(array, index * n + start, stop - start, axis)
+def halves_body(core, up, down, out, up_a, up_b, down_a, down_b, out_half, sems):
+    n = up_a.shape[0] + up_b.shape[0]
+    start = pl.multiple_of(core[0] * n, n)
+    copies = (
+        (up.at[pl.ds(start, up_a.shape[0])], up_a),
+        (up.at[pl.ds(start + up_a.shape[0], up_b.shape[0])], up_b),
+        (down.at[:, pl.ds(start, down_a.shape[1])], down_a),
+        (down.at[:, pl.ds(start + down_a.shape[1], down_b.shape[1])], down_b),
+        (out.at[:, pl.ds(start, n)], out_half),
+    )
+    copies = [pltpu.make_async_copy(a, b, sems.at[i]) for i, (a, b) in enumerate(copies)]
+    for copy in copies:
+        copy.start()
+    for copy in copies:
+        copy.wait()
+
+
+def halves(core, up, down, out, up_most, down_most):
+    d_model, hidden = up.shape
+    half = d_model // 2
+    hbm = pl.BlockSpec(memory_space=pltpu.MemorySpace.HBM)
+    shapes = (
+        (up_most, hidden),
+        (half - up_most, hidden),
+        (hidden, down_most),
+        (hidden, half - down_most),
+        (out.shape[0], half),
+    )
+    return pl.pallas_call(
+        halves_body,
+        grid_spec=pltpu.PrefetchScalarGridSpec(
+            num_scalar_prefetch=1,
+            grid=(1,),
+            in_specs=[hbm] * 3,
+            out_specs=[hbm] * 5,
+            scratch_shapes=[pltpu.SemaphoreType.DMA((5,))],
+        ),
+        out_shape=[jax.ShapeDtypeStruct(shape, up.dtype) for shape in shapes],
+    )(core.reshape(1), up, down, out)
 
 
 tie = lax.optimization_barrier
@@ -396,8 +427,9 @@
     place = jnp.concatenate(
         [(x_at + jnp.array([0, 3, 1, 2], jnp.int32)) % 4, yh_at.reshape(1).astype(jnp.int32)]
     )
-    out_half = part_of(out_weight, 2, core, 1)
-    up_most, down_most = d_model // 3, d_model // 8 * 3
+    up_first, up_late, down_first, down_late, out_half = halves(
+        core, up_weight, down_weight, out_weight, d_model // 24 * 7, d_model // 8 * 3
+    )
 
     q_other = shift(img_query, "yl", 2, 1)
     own = jnp.concatenate(
@@ -413,7 +445,7 @@
         return [shift(up, "z", 8, 1), shift(down, "z", 8, 7)]
 
     one = around(own, own)
-    up_a = cross(half_of(up_weight, core, 0, 0, up_most))
+    up_a = cross(up_first)
     out_l = shift(out_half, "x", 4, 1)
     out_r = shift(out_half, "x", 4, 3)
     one, q_other = tie((one, q_other))
@@ -425,16 +457,14 @@
     two = around(*one)
     state = attend(queries, [own], None)
     state = attend(queries, one, state)
-    two, state, up_a, out_l, out_r, core, out_half = tie(
-        (two, state, up_a, out_l, out_r, core, out_half)
+    two, state, up_a, out_l, out_r, down_first, out_half = tie(
+        (two, state, up_a, out_l, out_r, down_first, out_half)
     )
     three = around(*two)
-    down_a = cross(half_of(down_weight, core, 1, 0, down_most))
+    down_a = cross(down_first)
     out_f = shift(out_half, "x", 4, 2)
     state = attend(queries, two, state)
-    three, state, core = tie((three, state, core))
-    up_late = half_of(up_weight, core, 0, up_most, d_model // 2)
-    down_late = half_of(down_weight, core, 1, down_most, d_model // 2)
+    three, state = tie((three, state))
     four = around(three[0][:cut], three[1][cut:])
     state = attend(queries, three, state)
     four, state = tie((four, state))
@@ -451,13 +481,14 @@
     parts = lax.all_to_all(
         part.reshape(8, 2 * row_block, width + HD), ("yl", "x"), split_axis=0, concat_axis=0, tiled=True
     )
-    parts, out_mate, up_b, down_b = tie((parts, out_mate, up_b, down_b))
+    parts, out_mate = tie((parts, out_mate))
     proj_own, proj_away = join_project(parts, out_weight, out_mine, out_mate, order, place)
+    proj_away, up_b, down_b = tie((proj_away, up_b, down_b))
     proj_other = shift(proj_away, "yh", 2, 1)
     up_far = [up_a, up_b, shift(up_a, "dp", 2, 1), shift(up_b, "dp", 2, 1)]
     down_far = [down_a, down_b, shift(down_a, "dp", 2, 1), shift(down_b, "dp", 2, 1)]
     bias_far = cross(up_bias)
-    proj_other, up_far, down_far, bias_far = tie((proj_other, up_far, down_far, bias_far))
+    proj_other, up_far, down_far = tie((proj_other, up_far, down_far))
     stream, normed = stream_norm(proj_own, proj_other, residual_in, vectors)
     everyone = jnp.concatenate(gather_x(normed), axis=0)
     out = mlp(everyone, up_weight, down_weight, up_bias, bias_far, up_far, down_far, order)

time: 203 us -> 374 us (1.84)
  Pallas kernels: 57.3 us -> 233 us
  waiting for transfers between devices: 64.4 us -> 77.4 us
  local copies, waits for them, and re-layouts: 17.5 us -> 5.01 us
  starting transfers between devices: 57.5 us -> 53.1 us
    pallas_call x0 -> x1, Pallas kernels: none -> 180 us  [halves(): pl.pallas_call(halves_body, grid_spec=pltpu.PrefetchScalarGridSpec(num_sc...]
    all_to_all x1, waiting for transfers between devices: 0.01 us -> 12.4 us  [shards(): lax.all_to_all(part.reshape(8, 2 * row_block, width + HD), ('yl', 'x'), s...]
    dynamic_slice x5 -> x0, local copies, waits for them, and re-layouts: 11.1 us -> none  [the longest x4 9.93 us: half_of(): lax.dynamic_slice_in_dim(array, index * n + start, stop - start, axis)]
  transfers between devices with their start and end apart: 33 -> 33, of which waited for: 11 -> 11; matrix products, arithmetic and copies ran while one was open for 6% -> 0% of each run, Pallas kernels for 22% -> 60%
where the time goes in v3:
time: 374 us; the launch traced here: 373 us
  Pallas kernels  233 us (62%)
  waiting for transfers between devices  77.4 us (21%)
  starting transfers between devices  53.1 us (14%)
  local copies, waits for them, and re-layouts  5.01 us (1%)
  other arithmetic  3.82 us (1%)
    pallas_call x1, Pallas kernels, halves(): pl.pallas_call(halves_body, grid_spec=pltpu.PrefetchScalarGridSpec(num_sc...  180 us
    ppermute x27, waiting for transfers between devices, shift(): lax.ppermute(array, axis, [(i, (i + by) % size) for i in range(size)])  43.6 us
    ppermute x27, starting transfers between devices, shift(): lax.ppermute(array, axis, [(i, (i + by) % size) for i in range(size)])  39 us
    pallas_call x5, Pallas kernels, attend(): pl.pallas_call(functools.partial(attend_body, len(ks), first, bool(last))...  38.2 us
    ppermute x5, waiting for transfers between devices, cross(): return lax.ppermute(array, ('yl', 'yh'), [(0, 3), (3, 0), (1, 2), (2, 1)])  21.3 us
    all_to_all x1, waiting for transfers between devices, shards(): lax.all_to_all(part.reshape(8, 2 * row_block, width + HD), ('yl', 'x'), s...  12.4 us
    pallas_call x1, Pallas kernels, mlp(): pl.pallas_call(mlp_body, grid_spec=pltpu.PrefetchScalarGridSpec(num_scala...  9.45 us
  transfers between devices with their start and end apart: 33, of which 11 were waited for; matrix products, arithmetic and copies ran while one was open for 0% of the time, Pallas kernels for 60%

profile of v3, /device:TPU:8, one launch (start us, length us, event | category | flops | bytes accessed | tf_op | source)
XLA Modules:
  0.0 372.7 jit_solution(16802712525029176112)
XLA Ops:
  0.0 1.3 maximum_maximum_fusion.refs_1_.refs_2_
  1.3 2.0 collective-permute-start
  3.3 4.0 %collective-permute-start.1 = (bf16[528,768]{1,0:T(8,128)(2,1)S(1)}, bf16[528,768]{1,0:T(8,128)(2,1)}, u32[]{:S(2)}, u32[]{:S(2)}) collective-permute-start(bf16[528,768]{1,0:T(8,128)(2,1)S(1)} %maximum_maximum_fusion.refs_1_.refs_2_), channel_id=1, source_target_pairs={{0,112},{16,0},{32,16},{48,32},{64,48},{80,64},{96,80},{112,96},{1... | collective-permute-start | bytes 2433032 | tf_op jit(solution)/shard_map/ppermute | solution.py:343
  7.3 0.4 collective-permute-start.2
  7.7 179.8 %shard_map.165 = (bf16[896,768]{1,0:T(8,128)(2,1)}, bf16[640,768]{1,0:T(8,128)(2,1)}, bf16[768,1152]{1,0:T(8,128)(2,1)}, bf16[768,384]{1,0:T(8,128)(2,1)}, bf16[384,1536]{1,0:T(8,128)(2,1)}) custom-call(s32[1]{0:T(128)} %bitcast.1.core, bf16[3072,768]{1,0:T(8,128)(2,1)} %up_ref.1, bf16[768,3072]{1,0:T(8,128)(2,1)} %down_ref.1, bf16[384,3072]{1,0:T(8,128)(2,1)} %own_w.1), custom_call_target="tpu_custom_call" | custom-call | tf_op jit(solution)/shard_map/pallas_call | solution.py:378
  187.6 2.5 collective-permute-start.5
  190.1 1.5 collective-permute-start.6
  191.6 1.7 collective-permute-start.7
  193.3 3.2 collective-permute-start.4
  196.6 1.4 maximum_select_fusion.refs_0_
  197.9 5.1 %shard_map.163 = (f32[3,1,1024]{2,1,0:T(1,128)S(1)}, f32[3,1,1024]{2,1,0:T(1,128)S(1)}, f32[384,1024]{1,0:T(8,128)S(1)}) custom-call(bf16[1024,384]{1,0:T(8,128)(2,1)S(1)} %maximum_select_fusion.refs_0_, bf16[528,768]{1,0:T(8,128)(2,1)S(1)} %maximum_maximum_fusion.refs_1_.refs_2_, bf16[528,768]{1,0:T(8,128)(2,1)S(1)} %maximum_maximum_fusion.refs_1_.refs_2_), custom_call_target="tpu_custom_call" | custom-call | flops 830472192 | bytes 1597440 | tf_op jit(solution)/shard_map/pallas_call | solution.py:111
  203.1 9.0 %shard_map.164 = (f32[3,1,1024]{2,1,0:T(1,128)S(1)}, f32[3,1,1024]{2,1,0:T(1,128)S(1)}, f32[384,1024]{1,0:T(8,128)S(1)}) custom-call(bf16[1024,384]{1,0:T(8,128)(2,1)S(1)} %maximum_select_fusion.refs_0_, bf16[528,768]{1,0:T(8,128)(2,1)S(1)} %collective-permute-done.refs_1_.refs_3_, bf16[528,768]{1,0:T(8,128)(2,1)} %collective-permute-done.1.refs_2_.refs_4_, ...), custom_call_target="tpu_custom_call" | custom-call | flops 1660944384 | bytes 2408448 | tf_op jit(solution)/shard_map/pallas_call | solution.py:111
  212.0 6.4 %collective-permute-done.6.refs_0_ = bf16[384,1536]{1,0:T(8,128)(2,1)} collective-permute-done((bf16[384,1536]{1,0:T(8,128)(2,1)}, bf16[384,1536]{1,0:T(8,128)(2,1)}, u32[]{:S(2)}, u32[]{:S(2)}) %collective-permute-start.6) | collective-permute-done | bytes 1179680 | tf_op jit(solution)/shard_map/ppermute | solution.py:343
  218.5 1.4 collective-permute-done.5.refs_0_
  219.9 1.8 collective-permute-start.12
  221.8 3.2 collective-permute-start.9
  225.0 3.0 collective-permute-start.13
  228.0 8.9 %shard_map.166 = (f32[3,1,1024]{2,1,0:T(1,128)S(1)}, f32[3,1,1024]{2,1,0:T(1,128)S(1)}, f32[384,1024]{1,0:T(8,128)S(1)}) custom-call(bf16[1024,384]{1,0:T(8,128)(2,1)S(1)} %maximum_select_fusion.refs_0_, bf16[528,768]{1,0:T(8,128)(2,1)} %collective-permute-done.3.refs_1_.refs_3_, bf16[528,768]{1,0:T(8,128)(2,1)} %collective-permute-done.4.refs_2_.refs_4_, ...), custom_call_target="tpu_custom_call" | custom-call | flops 1660944384 | bytes 2408448 | tf_op jit(solution)/shard_map/pallas_call | solution.py:111
  236.9 4.3 %collective-permute-done.8.refs_1_.refs_3_ = bf16[528,768]{1,0:T(8,128)(2,1)S(1)} collective-permute-done((bf16[528,768]{1,0:T(8,128)(2,1)}, bf16[528,768]{1,0:T(8,128)(2,1)S(1)}, u32[]{:S(2)}, u32[]{:S(2)}) %collective-permute-start.8) | collective-permute-done | bytes 811040 | tf_op jit(solution)/shard_map/ppermute | solution.py:343
  241.6 3.3 collective-permute-start.11
  244.8 8.0 %shard_map.167 = (f32[3,1,1024]{2,1,0:T(1,128)S(1)}, f32[3,1,1024]{2,1,0:T(1,128)S(1)}, f32[384,1024]{1,0:T(8,128)S(1)}) custom-call(bf16[1024,384]{1,0:T(8,128)(2,1)S(1)} %maximum_select_fusion.refs_0_, bf16[528,768]{1,0:T(8,128)(2,1)S(1)} %collective-permute-done.8.refs_1_.refs_3_, bf16[528,768]{1,0:T(8,128)(2,1)S(1)} %collective-permute-done.9.refs_2_.refs_4_, ...), custom_call_target="tpu_custom_call" | custom-call | flops 1660944384 | bytes 2408448 | tf_op jit(solution)/shard_map/pallas_call | solution.py:111
  252.9 7.3 %shard_map.168 = bf16[2,4,2,64,512]{4,3,2,1,0:T(8,128)(2,1)} custom-call(bf16[1024,384]{1,0:T(8,128)(2,1)S(1)} %maximum_select_fusion.refs_0_, bf16[272,768]{1,0:T(8,128)(2,1)S(1)} %collective-permute-done.10.refs_1_.refs_3_, bf16[256,768]{1,0:T(8,128)(2,1)S(1)} %collective-permute-done.11.refs_2_.refs_4_, ...), custom_call_target="tpu_custom_call" | custom-call | flops 830472192 | bytes 1597440 | tf_op jit(solution)/shard_map/pallas_call | solution.py:111
  260.2 0.5 collective-permute-start.15
  260.8 6.9 %all-to-all-start = ((bf16[8,128,512]{2,1,0:T(8,128)(2,1)}), bf16[8,128,512]{2,1,0:T(8,128)(2,1)S(1)}, u32[]{:S(2)}, u32[]{:S(2)}) async-start(bf16[8,128,512]{2,1,0:T(8,128)(2,1)} %bitcast.2), calls=%async_computation | async-start | bytes 2097152 | tf_op jit(solution)/shard_map/all_to_all | solution.py:481
  267.7 0.5 collective-permute-start.17
  268.1 1.6 collective-permute-start.18
  270.1 12.4 %all-to-all-done.part_ref = bf16[8,128,512]{2,1,0:T(8,128)(2,1)S(1)} async-done(((bf16[8,128,512]{2,1,0:T(8,128)(2,1)}), bf16[8,128,512]{2,1,0:T(8,128)(2,1)S(1)}, u32[]{:S(2)}, u32[]{:S(2)}) %all-to-all-start) | async-done | bytes 1048608 | tf_op jit(solution)/shard_map/all_to_all | solution.py:481
  282.5 4.5 %shard_map.169 = (f32[64,3072]{1,0:T(8,128)S(1)}, bf16[64,3072]{1,0:T(8,128)(2,1)S(1)}) custom-call(s32[4]{0:T(128)S(1)} %iota_xor_fusion.order, s32[5]{0:T(128)S(1)} %pad_add_fusion.place, bf16[8,128,512]{2,1,0:T(8,128)(2,1)S(1)} %all-to-all-done.part_ref, bf16[384,3072]{1,0:T(8,128)(2,1)S(1)} %copy-done.2, ...), custom_call_target="tpu_custom_call" | custom-call | flops 1207959552 | bytes 9437184 | tf_op jit(solution)/shard_map/pallas_call | solution.py:185
  287.1 17.1 %collective-permute-done.18.refs_5_ = bf16[768,384]{1,0:T(8,128)(2,1)} collective-permute-done((bf16[768,384]{1,0:T(8,128)(2,1)}, bf16[768,384]{1,0:T(8,128)(2,1)}, u32[]{:S(2)}, u32[]{:S(2)}) %collective-permute-start.18) | collective-permute-done | bytes 589856 | tf_op jit(solution)/shard_map/ppermute | solution.py:347
  304.2 0.5 collective-permute-start.23
  304.7 3.2 collective-permute-start.19
  308.0 9.2 %collective-permute-done.19.other_ref = bf16[64,3072]{1,0:T(8,128)(2,1)S(1)} collective-permute-done((bf16[64,3072]{1,0:T(8,128)(2,1)S(1)}, bf16[64,3072]{1,0:T(8,128)(2,1)S(1)}, u32[]{:S(2)}, u32[]{:S(2)}) %collective-permute-start.19) | collective-permute-done | bytes 393248 | tf_op jit(solution)/shard_map/ppermute | solution.py:343
  317.2 1.1 shard_map.170
  318.4 1.5 collective-permute-start.24
  319.9 1.8 collective-permute-start.25
  321.7 0.8 collective-permute-start.28
  322.5 2.8 collective-permute-done.28
  325.3 4.5 %collective-permute-done.24 = bf16[64,3072]{1,0:T(8,128)(2,1)S(1)} collective-permute-done((bf16[64,3072]{1,0:T(8,128)(2,1)S(1)}, bf16[64,3072]{1,0:T(8,128)(2,1)S(1)}, u32[]{:S(2)}, u32[]{:S(2)}) %collective-permute-start.24) | collective-permute-done | bytes 393248 | tf_op jit(solution)/shard_map/ppermute | solution.py:343
  330.2 3.1 collective-permute-start.27
  333.3 3.5 collective-permute-done.26
  336.9 2.3 copy-done
  339.2 2.3 copy-done.1
  341.5 9.4 %shard_map.171 = bf16[256,3072]{1,0:T(8,128)(2,1)S(1)} custom-call(s32[4]{0:T(128)S(1)} %iota_xor_fusion.order, bf16[256,3072]{1,0:T(8,128)(2,1)S(1)} %constant_dynamic-update-slice_fusion.x_ref, bf16[3072,768]{1,0:T(8,128)(2,1)S(1)} %copy-done, bf16[768,3072]{1,0:T(8,128)(2,1)S(1)} %copy-done.1, f32[1,768]{1,0:T(1,128)S(1)} %reshape.29.bias_ref, ...), custom_call_target="tpu_custom_call" | custom-call | flops 4831838208 | bytes 18874368 | tf_op jit(solution)/shard_map/pallas_call | solution.py:308
  351.1 3.4 collective-permute-start.29
  354.5 1.6 collective-permute-start.31
  356.0 12.2 %collective-permute-done.29 = bf16[64,3072]{1,0:T(8,128)(2,1)S(1)} collective-permute-done((bf16[64,3072]{1,0:T(8,128)(2,1)S(1)}, bf16[64,3072]{1,0:T(8,128)(2,1)S(1)}, u32[]{:S(2)}, u32[]{:S(2)}) %collective-permute-start.29) | collective-permute-done | bytes 393248 | tf_op jit(solution)/shard_map/ppermute | solution.py:343
  368.3 3.4 collective-permute-done.30
  371.7 1.0 add_convert_fusion
  (80 shorter events, 1.6 us)
Async XLA Ops:
  0.0 7.3 %copy-start.6 = (bf16[512,384]{1,0:T(8,128)(2,1)S(1)}, bf16[512,384]{1,0:T(8,128)(2,1)}, u32[]{:S(2)}) copy-start(bf16[512,384]{1,0:T(8,128)(2,1)} %param.17) | copy-start | bytes 1179652
  1.3 192.0 %collective-permute-start = (bf16[528,768]{1,0:T(8,128)(2,1)S(1)}, bf16[528,768]{1,0:T(8,128)(2,1)S(1)}, u32[]{:S(2)}, u32[]{:S(2)}) collective-permute-start(bf16[528,768]{1,0:T(8,128)(2,1)S(1)} %maximum_maximum_fusion.refs_1_.refs_2_), channel_id=1, source_target_pairs={{0,16},{16,32},{32,48},{48,64},{64,80},{80,96},{96,112},{112,0},{1... | collective-permute-start | bytes 2433032 | tf_op jit(solution)/shard_map/ppermute | solution.py:343
  3.3 190.0 %collective-permute-start.1 = (bf16[528,768]{1,0:T(8,128)(2,1)S(1)}, bf16[528,768]{1,0:T(8,128)(2,1)}, u32[]{:S(2)}, u32[]{:S(2)}) collective-permute-start(bf16[528,768]{1,0:T(8,128)(2,1)S(1)} %maximum_maximum_fusion.refs_1_.refs_2_), channel_id=1, source_target_pairs={{0,112},{16,0},{32,16},{48,32},{64,48},{80,64},{96,80},{112,96},{1... | collective-permute-start | bytes 2433032 | tf_op jit(solution)/shard_map/ppermute | solution.py:343
  7.3 184.3 %collective-permute-start.2 = (bf16[512,384]{1,0:T(8,128)(2,1)S(1)}, bf16[512,384]{1,0:T(8,128)(2,1)}, u32[]{:S(2)}, u32[]{:S(2)}) collective-permute-start(bf16[512,384]{1,0:T(8,128)(2,1)S(1)} %copy-done.6), channel_id=1, source_target_pairs={{0,128},{128,0},{1,129},{129,1},{2,130},{130,2},{3,131},{131,3},{4... | collective-permute-start | bytes 1179656 | tf_op jit(solution)/shard_map/ppermute | solution.py:343
  187.6 32.3 %collective-permute-start.5 = (bf16[896,768]{1,0:T(8,128)(2,1)}, bf16[896,768]{1,0:T(8,128)(2,1)S(1)}, u32[]{:S(2)}, u32[]{:S(2)}) collective-permute-start(bf16[896,768]{1,0:T(8,128)(2,1)} %get-tuple-element.82), channel_id=1, source_target_pairs={{0,136},{136,0},{8,128},{128,8},{1,137},{137,1},{9,129},{129,9},{2... | collective-permute-start | bytes 4128776 | tf_op jit(solution)/shard_map/ppermute | solution.py:347
  190.1 28.4 %collective-permute-start.6 = (bf16[384,1536]{1,0:T(8,128)(2,1)}, bf16[384,1536]{1,0:T(8,128)(2,1)}, u32[]{:S(2)}, u32[]{:S(2)}) collective-permute-start(bf16[384,1536]{1,0:T(8,128)(2,1)} %get-tuple-element.110), channel_id=1, source_target_pairs={{0,2},{2,4},{4,6},{6,0},{1,3},{3,5},{5,7},{7,1},{8,10},{10,12},{12... | collective-permute-start | bytes 3538952 | tf_op jit(solution)/shard_map/ppermute | solution.py:343
  191.6 26.9 %collective-permute-start.7 = (bf16[384,1536]{1,0:T(8,128)(2,1)}, bf16[384,1536]{1,0:T(8,128)(2,1)}, u32[]{:S(2)}, u32[]{:S(2)}) collective-permute-start(bf16[384,1536]{1,0:T(8,128)(2,1)} %get-tuple-element.110), channel_id=1, source_target_pairs={{0,6},{2,0},{4,2},{6,4},{1,7},{3,1},{5,3},{7,5},{8,14},{10,8},{12,... | collective-permute-start | bytes 3538952 | tf_op jit(solution)/shard_map/ppermute | solution.py:343
  193.3 26.6 %collective-permute-start.3 = (bf16[528,768]{1,0:T(8,128)(2,1)S(1)}, bf16[528,768]{1,0:T(8,128)(2,1)}, u32[]{:S(2)}, u32[]{:S(2)}) collective-permute-start(bf16[528,768]{1,0:T(8,128)(2,1)S(1)} %collective-permute-done.refs_1_.refs_3_), channel_id=1, source_target_pairs={{0,16},{16,32},{32,48},{48,64},{64,80},{80,96},{96,112},{112,0},{1... | collective-permute-start | bytes 2433032 | tf_op jit(solution)/shard_map/ppermute | solution.py:343
  193.3 26.6 %collective-permute-start.4 = (bf16[528,768]{1,0:T(8,128)(2,1)}, bf16[528,768]{1,0:T(8,128)(2,1)}, u32[]{:S(2)}, u32[]{:S(2)}) collective-permute-start(bf16[528,768]{1,0:T(8,128)(2,1)} %collective-permute-done.1.refs_2_.refs_4_), channel_id=1, source_target_pairs={{0,112},{16,0},{32,16},{48,32},{64,48},{80,64},{96,80},{112,96},{1... | collective-permute-start | bytes 2433032 | tf_op jit(solution)/shard_map/ppermute | solution.py:343
  203.1 16.9 %copy-start.14 = (bf16[768,1152]{1,0:T(8,128)(2,1)S(1)}, bf16[768,1152]{1,0:T(8,128)(2,1)}, u32[]{:S(2)}) copy-start(bf16[768,1152]{1,0:T(8,128)(2,1)} %get-tuple-element.106) | copy-start | bytes 5308420
  203.1 21.9 %copy-start.15 = (bf16[384,1536]{1,0:T(8,128)(2,1)S(1)}, bf16[384,1536]{1,0:T(8,128)(2,1)}, u32[]{:S(2)}) copy-start(bf16[384,1536]{1,0:T(8,128)(2,1)} %get-tuple-element.110) | copy-start | bytes 3538948
  219.9 17.0 %copy-start.3 = (bf16[896,768]{1,0:T(8,128)(2,1)}, bf16[896,768]{1,0:T(8,128)(2,1)S(1)}, u32[]{:S(2)}) copy-start(bf16[896,768]{1,0:T(8,128)(2,1)S(1)} %collective-permute-done.5.refs_0_) | copy-start | bytes 4128772
  219.9 40.2 %collective-permute-start.12 = (bf16[768,1152]{1,0:T(8,128)(2,1)S(1)}, bf16[768,1152]{1,0:T(8,128)(2,1)}, u32[]{:S(2)}, u32[]{:S(2)}) collective-permute-start(bf16[768,1152]{1,0:T(8,128)(2,1)S(1)} %copy-done.14), channel_id=1, source_target_pairs={{0,136},{136,0},{8,128},{128,8},{1,137},{137,1},{9,129},{129,9},{2... | collective-permute-start | bytes 5308424 | tf_op jit(solution)/shard_map/ppermute | solution.py:347
  221.7 19.5 %collective-permute-start.8 = (bf16[528,768]{1,0:T(8,128)(2,1)}, bf16[528,768]{1,0:T(8,128)(2,1)S(1)}, u32[]{:S(2)}, u32[]{:S(2)}) collective-permute-start(bf16[528,768]{1,0:T(8,128)(2,1)} %collective-permute-done.3.refs_1_.refs_3_), channel_id=1, source_target_pairs={{0,16},{16,32},{32,48},{48,64},{64,80},{80,96},{96,112},{112,0},{1... | collective-permute-start | bytes 2433032 | tf_op jit(solution)/shard_map/ppermute | solution.py:343
  221.8 19.5 %collective-permute-start.9 = (bf16[528,768]{1,0:T(8,128)(2,1)}, bf16[528,768]{1,0:T(8,128)(2,1)S(1)}, u32[]{:S(2)}, u32[]{:S(2)}) collective-permute-start(bf16[528,768]{1,0:T(8,128)(2,1)} %collective-permute-done.4.refs_2_.refs_4_), channel_id=1, source_target_pairs={{0,112},{16,0},{32,16},{48,32},{64,48},{80,64},{96,80},{112,96},{1... | collective-permute-start | bytes 2433032 | tf_op jit(solution)/shard_map/ppermute | solution.py:343
  225.0 35.1 %collective-permute-start.13 = (bf16[384,1536]{1,0:T(8,128)(2,1)S(1)}, bf16[384,1536]{1,0:T(8,128)(2,1)}, u32[]{:S(2)}, u32[]{:S(2)}) collective-permute-start(bf16[384,1536]{1,0:T(8,128)(2,1)S(1)} %copy-done.15), channel_id=1, source_target_pairs={{0,4},{2,6},{4,0},{6,2},{1,5},{3,7},{5,1},{7,3},{8,12},{10,14},{12... | collective-permute-start | bytes 3538952 | tf_op jit(solution)/shard_map/ppermute | solution.py:343
  241.2 11.6 %collective-permute-start.10 = (bf16[272,768]{1,0:T(8,128)(2,1)S(1)}, bf16[272,768]{1,0:T(8,128)(2,1)S(1)}, u32[]{:S(2)}, u32[]{:S(2)}) collective-permute-start(bf16[272,768]{1,0:T(8,128)(2,1)S(1)} %slice.28), channel_id=1, source_target_pairs={{0,16},{16,32},{32,48},{48,64},{64,80},{80,96},{96,112},{112,0},{1... | collective-permute-start | bytes 1253384 | tf_op jit(solution)/shard_map/ppermute | solution.py:343
  241.6 11.3 %collective-permute-start.11 = (bf16[256,768]{1,0:T(8,128)(2,1)S(1)}, bf16[256,768]{1,0:T(8,128)(2,1)S(1)}, u32[]{:S(2)}, u32[]{:S(2)}) collective-permute-start(bf16[256,768]{1,0:T(8,128)(2,1)S(1)} %slice.29), channel_id=1, source_target_pairs={{0,112},{16,0},{32,16},{48,32},{64,48},{80,64},{96,80},{112,96},{1... | collective-permute-start | bytes 1179656 | tf_op jit(solution)/shard_map/ppermute | solution.py:343
  252.8 29.7 %copy-start.2 = (bf16[384,3072]{1,0:T(8,128)(2,1)S(1)}, bf16[384,3072]{1,0:T(8,128)(2,1)}, u32[]{:S(2)}) copy-start(bf16[384,3072]{1,0:T(8,128)(2,1)} %own_w.1) | copy-start | bytes 7077892
  260.1 9.8 %copy-start.16 = (s32[4]{0:T(128)S(1)}, s32[4]{0:T(128)}, u32[]{:S(2)}) copy-start(s32[4]{0:T(128)} %constant.35.clone) | copy-start | bytes 52
  260.1 8.0 %collective-permute-start.14 = (bf16[384,1536]{1,0:T(8,128)(2,1)}, bf16[384,1536]{1,0:T(8,128)(2,1)}, u32[]{:S(2)}, u32[]{:S(2)}) collective-permute-start(bf16[384,1536]{1,0:T(8,128)(2,1)} %collective-permute-done.6.refs_0_), channel_id=1, source_target_pairs={{0,1},{1,0},{2,3},{3,2},{4,5},{5,4},{6,7},{7,6},{8,9},{9,8},{10,11... | collective-permute-start | bytes 3538952 | tf_op jit(solution)/shard_map/ppermute | solution.py:343
  260.2 9.5 %collective-permute-start.15 = (bf16[384,1536]{1,0:T(8,128)(2,1)}, bf16[384,1536]{1,0:T(8,128)(2,1)}, u32[]{:S(2)}, u32[]{:S(2)}) collective-permute-start(bf16[384,1536]{1,0:T(8,128)(2,1)} %collective-permute-done.7.refs_1_), channel_id=1, source_target_pairs={{0,1},{1,0},{2,3},{3,2},{4,5},{5,4},{6,7},{7,6},{8,9},{9,8},{10,11... | collective-permute-start | bytes 3538952 | tf_op jit(solution)/shard_map/ppermute | solution.py:343
  260.7 21.8 %collective-permute-start.16 = (bf16[384,1536]{1,0:T(8,128)(2,1)}, bf16[384,1536]{1,0:T(8,128)(2,1)}, u32[]{:S(2)}, u32[]{:S(2)}) collective-permute-start(bf16[384,1536]{1,0:T(8,128)(2,1)} %collective-permute-done.13.refs_2_), channel_id=1, source_target_pairs={{0,1},{1,0},{2,3},{3,2},{4,5},{5,4},{6,7},{7,6},{8,9},{9,8},{10,11... | collective-permute-start | bytes 3538952 | tf_op jit(solution)/shard_map/ppermute | solution.py:343
  260.8 21.7 %all-to-all-start = ((bf16[8,128,512]{2,1,0:T(8,128)(2,1)}), bf16[8,128,512]{2,1,0:T(8,128)(2,1)S(1)}, u32[]{:S(2)}, u32[]{:S(2)}) async-start(bf16[8,128,512]{2,1,0:T(8,128)(2,1)} %bitcast.2), calls=%async_computation | async-start | bytes 2097152 | tf_op jit(solution)/shard_map/all_to_all | solution.py:481
  267.7 36.5 %collective-permute-start.17 = (bf16[640,768]{1,0:T(8,128)(2,1)}, bf16[640,768]{1,0:T(8,128)(2,1)}, u32[]{:S(2)}, u32[]{:S(2)}) collective-permute-start(bf16[640,768]{1,0:T(8,128)(2,1)} %get-tuple-element.123), channel_id=1, source_target_pairs={{0,136},{136,0},{8,128},{128,8},{1,137},{137,1},{9,129},{129,9},{2... | collective-permute-start | bytes 2949128 | tf_op jit(solution)/shard_map/ppermute | solution.py:347
  268.1 49.1 %collective-permute-start.22 = (bf16[768,1152]{1,0:T(8,128)(2,1)}, bf16[768,1152]{1,0:T(8,128)(2,1)}, u32[]{:S(2)}, u32[]{:S(2)}) collective-permute-start(bf16[768,1152]{1,0:T(8,128)(2,1)} %collective-permute-done.12.refs_4_), channel_id=1, source_target_pairs={{0,1},{1,0},{2,3},{3,2},{4,5},{5,4},{6,7},{7,6},{8,9},{9,8},{10,11... | collective-permute-start | bytes 5308424 | tf_op jit(solution)/shard_map/ppermute | solution.py:343
  268.1 36.0 %collective-permute-start.18 = (bf16[768,384]{1,0:T(8,128)(2,1)}, bf16[768,384]{1,0:T(8,128)(2,1)}, u32[]{:S(2)}, u32[]{:S(2)}) collective-permute-start(bf16[768,384]{1,0:T(8,128)(2,1)} %get-tuple-element.124), channel_id=1, source_target_pairs={{0,136},{136,0},{8,128},{128,8},{1,137},{137,1},{9,129},{129,9},{2... | collective-permute-start | bytes 1769480 | tf_op jit(solution)/shard_map/ppermute | solution.py:347
  269.7 38.2 %collective-permute-start.20 = (bf16[896,768]{1,0:T(8,128)(2,1)}, bf16[896,768]{1,0:T(8,128)(2,1)}, u32[]{:S(2)}, u32[]{:S(2)}) collective-permute-start(bf16[896,768]{1,0:T(8,128)(2,1)} %copy-done.3), channel_id=1, source_target_pairs={{0,1},{1,0},{2,3},{3,2},{4,5},{5,4},{6,7},{7,6},{8,9},{9,8},{10,11... | collective-permute-start | bytes 4128776 | tf_op jit(solution)/shard_map/ppermute | solution.py:343
  270.0 37.8 %copy-start.9 = (f32[3072]{0:T(1024)S(1)}, f32[3072]{0:T(1024)}, u32[]{:S(2)}) copy-start(f32[3072]{0:T(1024)} %param.23) | copy-start | bytes 36868
  270.1 37.8 %copy-start.10 = (f32[3072]{0:T(1024)S(1)}, f32[3072]{0:T(1024)}, u32[]{:S(2)}) copy-start(f32[3072]{0:T(1024)} %param.24) | copy-start | bytes 36868
  270.1 37.8 %copy-start.11 = (f32[3072]{0:T(1024)S(1)}, f32[3072]{0:T(1024)}, u32[]{:S(2)}) copy-start(f32[3072]{0:T(1024)} %param.28) | copy-start | bytes 36868
  270.1 37.8 %copy-start.12 = (f32[3072]{0:T(1024)S(1)}, f32[3072]{0:T(1024)}, u32[]{:S(2)}) copy-start(f32[3072]{0:T(1024)} %param.25) | copy-start | bytes 36868
  282.5 34.7 %copy-start.5 = (bf16[64,3072]{1,0:T(8,128)(2,1)S(1)}, bf16[64,3072]{1,0:T(8,128)(2,1)}, u32[]{:S(2)}) copy-start(bf16[64,3072]{1,0:T(8,128)(2,1)} %residual_ref.1) | copy-start | bytes 1179652
  287.1 34.6 %copy-start.13 = (f32[768]{0:T(1024)S(1)}, f32[768]{0:T(1024)}, u32[]{:S(2)}) copy-start(f32[768]{0:T(1024)} %param.30) | copy-start | bytes 9220
  304.2 13.0 %collective-permute-start.21 = (bf16[640,768]{1,0:T(8,128)(2,1)}, bf16[640,768]{1,0:T(8,128)(2,1)S(1)}, u32[]{:S(2)}, u32[]{:S(2)}) collective-permute-start(bf16[640,768]{1,0:T(8,128)(2,1)} %collective-permute-done.17.refs_1_), channel_id=1, source_target_pairs={{0,1},{1,0},{2,3},{3,2},{4,5},{5,4},{6,7},{7,6},{8,9},{9,8},{10,11... | collective-permute-start | bytes 2949128 | tf_op jit(solution)/shard_map/ppermute | solution.py:343
  304.2 13.0 %collective-permute-start.23 = (bf16[768,384]{1,0:T(8,128)(2,1)}, bf16[768,384]{1,0:T(8,128)(2,1)S(1)}, u32[]{:S(2)}, u32[]{:S(2)}) collective-permute-start(bf16[768,384]{1,0:T(8,128)(2,1)} %collective-permute-done.18.refs_5_), channel_id=1, source_target_pairs={{0,1},{1,0},{2,3},{3,2},{4,5},{5,4},{6,7},{7,6},{8,9},{9,8},{10,11... | collective-permute-start | bytes 1769480 | tf_op jit(solution)/shard_map/ppermute | solution.py:343
  304.7 12.5 %collective-permute-start.19 = (bf16[64,3072]{1,0:T(8,128)(2,1)S(1)}, bf16[64,3072]{1,0:T(8,128)(2,1)S(1)}, u32[]{:S(2)}, u32[]{:S(2)}) collective-permute-start(bf16[64,3072]{1,0:T(8,128)(2,1)S(1)} %get-tuple-element.125), channel_id=1, source_target_pairs={{0,8},{8,0},{1,9},{9,1},{2,10},{10,2},{3,11},{11,3},{4,12},{12,4},... | collective-permute-start | bytes 1179656 | tf_op jit(solution)/shard_map/ppermute | solution.py:343
  318.4 11.5 %collective-permute-start.24 = (bf16[64,3072]{1,0:T(8,128)(2,1)S(1)}, bf16[64,3072]{1,0:T(8,128)(2,1)S(1)}, u32[]{:S(2)}, u32[]{:S(2)}) collective-permute-start(bf16[64,3072]{1,0:T(8,128)(2,1)S(1)} %get-tuple-element.132), channel_id=1, source_target_pairs={{0,2},{2,4},{4,6},{6,0},{1,3},{3,5},{5,7},{7,1},{8,10},{10,12},{12... | collective-permute-start | bytes 1179656 | tf_op jit(solution)/shard_map/ppermute | solution.py:343
  319.9 10.3 %collective-permute-start.25 = (bf16[64,3072]{1,0:T(8,128)(2,1)S(1)}, bf16[64,3072]{1,0:T(8,128)(2,1)S(1)}, u32[]{:S(2)}, u32[]{:S(2)}) collective-permute-start(bf16[64,3072]{1,0:T(8,128)(2,1)S(1)} %get-tuple-element.132), channel_id=1, source_target_pairs={{0,6},{2,0},{4,2},{6,4},{1,7},{3,1},{5,3},{7,5},{8,14},{10,8},{12,... | collective-permute-start | bytes 1179656 | tf_op jit(solution)/shard_map/ppermute | solution.py:343
  321.7 3.6 collective-permute-start.28
  325.3 11.5 %copy-start.4 = (bf16[896,768]{1,0:T(8,128)(2,1)S(1)}, bf16[896,768]{1,0:T(8,128)(2,1)}, u32[]{:S(2)}) copy-start(bf16[896,768]{1,0:T(8,128)(2,1)} %copy-done.3) | copy-start | bytes 4128772
  329.8 7.0 %collective-permute-start.26 = (bf16[32,3072]{1,0:T(8,128)(2,1)S(1)}, bf16[32,3072]{1,0:T(8,128)(2,1)S(1)}, u32[]{:S(2)}, u32[]{:S(2)}) collective-permute-start(bf16[32,3072]{1,0:T(8,128)(2,1)S(1)} %slice.36), channel_id=1, source_target_pairs={{0,2},{2,4},{4,6},{6,0},{1,3},{3,5},{5,7},{7,1},{8,10},{10,12},{12... | collective-permute-start | bytes 589832 | tf_op jit(solution)/shard_map/ppermute | solution.py:343
  330.2 6.6 %collective-permute-start.27 = (bf16[32,3072]{1,0:T(8,128)(2,1)S(1)}, bf16[32,3072]{1,0:T(8,128)(2,1)S(1)}, u32[]{:S(2)}, u32[]{:S(2)}) collective-permute-start(bf16[32,3072]{1,0:T(8,128)(2,1)S(1)} %slice.37), channel_id=1, source_target_pairs={{0,6},{2,0},{4,2},{6,4},{1,7},{3,1},{5,3},{7,5},{8,14},{10,8},{12,... | collective-permute-start | bytes 589832 | tf_op jit(solution)/shard_map/ppermute | solution.py:343
  351.0 20.7 %copy-start.7 = (f32[3072]{0:T(1024)S(1)}, f32[3072]{0:T(1024)}, u32[]{:S(2)}) copy-start(f32[3072]{0:T(1024)} %param.32) | copy-start | bytes 36868
  351.0 20.7 %copy-start.8 = (f32[3072]{0:T(1024)S(1)}, f32[3072]{0:T(1024)}, u32[]{:S(2)}) copy-start(f32[3072]{0:T(1024)} %param.26) | copy-start | bytes 36868
  351.1 17.1 %collective-permute-start.29 = (bf16[64,3072]{1,0:T(8,128)(2,1)S(1)}, bf16[64,3072]{1,0:T(8,128)(2,1)S(1)}, u32[]{:S(2)}, u32[]{:S(2)}) collective-permute-start(bf16[64,3072]{1,0:T(8,128)(2,1)S(1)} %get-tuple-element.141), channel_id=1, source_target_pairs={{0,6},{2,0},{4,2},{6,4},{1,7},{3,1},{5,3},{7,5},{8,14},{10,8},{12,... | collective-permute-start | bytes 1179656 | tf_op jit(solution)/shard_map/ppermute | solution.py:343
  354.5 17.2 %collective-permute-start.30 = (bf16[64,3072]{1,0:T(8,128)(2,1)S(1)}, bf16[64,3072]{1,0:T(8,128)(2,1)S(1)}, u32[]{:S(2)}, u32[]{:S(2)}) collective-permute-start(bf16[64,3072]{1,0:T(8,128)(2,1)S(1)} %get-tuple-element.143), channel_id=1, source_target_pairs={{0,2},{2,4},{4,6},{6,0},{1,3},{3,5},{5,7},{7,1},{8,10},{10,12},{12... | collective-permute-start | bytes 1179656 | tf_op jit(solution)/shard_map/ppermute | solution.py:343
  354.5 17.2 %collective-permute-start.31 = (bf16[64,3072]{1,0:T(8,128)(2,1)S(1)}, bf16[64,3072]{1,0:T(8,128)(2,1)S(1)}, u32[]{:S(2)}, u32[]{:S(2)}) collective-permute-start(bf16[64,3072]{1,0:T(8,128)(2,1)S(1)} %get-tuple-element.142), channel_id=1, source_target_pairs={{0,4},{2,6},{4,0},{6,2},{1,5},{3,7},{5,1},{7,3},{8,12},{10,14},{12... | collective-permute-start | bytes 1179656 | tf_op jit(solution)/shard_map/ppermute | solution.py:343
  (2 other events, 4.7 us)

commit v4 on v3

--- a/solution.py
+++ b/solution.py
@@ -242,25 +242,25 @@
 
 def mlp_body(order, x_ref, up_ref, down_ref, bias_ref, bias_far_ref, *refs):
     n = 4
-    up_far, down_far, out_ref = refs[:n], refs[n : 2 * n], refs[2 * n]
-    near, far, hid_near, hid_far, up_buf, down_buf, sems = refs[2 * n + 1 :]
+    up_far, down_far, out_ref = refs[:n], refs[n : n + 4], refs[n + 4]
+    near, far, hid_near, hid_far, up_buf, down_buf, sems = refs[n + 5 :]
     i = pl.program_id(0)
     quarter = up_ref.shape[0]
 
+    first = down_far[0].shape[1] - quarter
+
     def copies(j):
-        down = j >= n
-        a, b = (down_far if down else up_far)[j % n // 2 * 2 : j % n // 2 * 2 + 2]
-        to = (down_buf if down else up_buf).at[j % n]
-
-        def part(ref, start, size):
-            return ref.at[:, pl.ds(start, size)] if down else ref.at[pl.ds(start, size)]
-
+        sem = sems.at[j, 0]
+        if j < n:
+            yield pltpu.make_async_copy(up_far[j], up_buf.at[j], sem)
+            return
+        a, b = down_far[(j - n) // 2 * 2 : (j - n) // 2 * 2 + 2]
+        to = down_buf.at[j - n]
         if j % 2 == 0:
-            yield pltpu.make_async_copy(part(a, 0, quarter), to, sems.at[j, 0])
-            return
-        rest = a.shape[1 if down else 0] - quarter
-        yield pltpu.make_async_copy(part(a, quarter, rest), part(to, 0, rest), sems.at[j, 0])
-        yield pltpu.make_async_copy(b, part(to, rest, quarter - rest), sems.at[j, 1])
+            yield pltpu.make_async_copy(a.at[:, pl.ds(0, quarter)], to, sem)
+        else:
+            yield pltpu.make_async_copy(a.at[:, pl.ds(quarter, first)], to.at[:, pl.ds(0, first)], sem)
+            yield pltpu.make_async_copy(b, to.at[:, pl.ds(first, quarter - first)], sems.at[j, 1])
 
     @pl.when(i == 0)
     def _():
@@ -279,10 +279,14 @@
 
     @pl.when(i < n)
     def _():
+        at = pl.multiple_of(i * quarter, quarter)
+        near[...] += jnp.dot(
+            x_ref[:, pl.ds(at, quarter)], up_ref[...], preferred_element_type=jnp.float32
+        )
         at = pl.multiple_of(order[i] * quarter, quarter)
-        x = x_ref[:, pl.ds(at, quarter)]
-        near[...] += jnp.dot(x, up_ref[...], preferred_element_type=jnp.float32)
-        far[...] += jnp.dot(x, up_buf[i], preferred_element_type=jnp.float32)
+        far[...] += jnp.dot(
+            x_ref[:, pl.ds(at, quarter)], up_buf[i], preferred_element_type=jnp.float32
+        )
 
     @pl.when(i == n - 1)
     def _():
@@ -300,10 +304,10 @@
 def mlp(x, up, down, bias, bias_far, up_far, down_far, order):
     rows, d_model = x.shape
     hidden = up.shape[1]
-    n = 4
+    n = len(up_far)
     quarter = d_model // n
     whole = lambda i, order: (0, 0)
-    column = lambda i, order: (0, order[jnp.maximum(i - n, 0)])
+    column = lambda i, order: (0, order[jnp.maximum(i, n)])
     far_spec = pl.BlockSpec(memory_space=pltpu.MemorySpace.HBM)
     return pl.pallas_call(
         mlp_body,
@@ -312,11 +316,11 @@
             grid=(2 * n,),
             in_specs=[
                 pl.BlockSpec((rows, d_model), whole),
-                pl.BlockSpec((quarter, hidden), lambda i, order: (order[jnp.minimum(i, n - 1)], 0)),
+                pl.BlockSpec((quarter, hidden), lambda i, order: (jnp.minimum(i, n - 1), 0)),
                 pl.BlockSpec((hidden, quarter), column),
                 pl.BlockSpec((1, hidden), whole),
                 pl.BlockSpec((1, hidden), whole),
-                *[far_spec] * (2 * n),
+                *[far_spec] * (n + 4),
             ],
             out_specs=pl.BlockSpec((rows, quarter), column),
             scratch_shapes=[
@@ -347,45 +351,54 @@
     return lax.ppermute(array, ("yl", "yh"), [(0, 3), (3, 0), (1, 2), (2, 1)])
 
 
-def halves_body(core, up, down, out, up_a, up_b, down_a, down_b, out_half, sems):
-    n = up_a.shape[0] + up_b.shape[0]
-    start = pl.multiple_of(core[0] * n, n)
-    copies = (
-        (up.at[pl.ds(start, up_a.shape[0])], up_a),
-        (up.at[pl.ds(start + up_a.shape[0], up_b.shape[0])], up_b),
-        (down.at[:, pl.ds(start, down_a.shape[1])], down_a),
-        (down.at[:, pl.ds(start + down_a.shape[1], down_b.shape[1])], down_b),
-        (out.at[:, pl.ds(start, n)], out_half),
-    )
-    copies = [pltpu.make_async_copy(a, b, sems.at[i]) for i, (a, b) in enumerate(copies)]
-    for copy in copies:
+def pieces_body(place, up, down, out, *refs):
+    dests, bufs, sems = refs[:4], refs[4:8], refs[8]
+    half = out.shape[1] // 2
+    start = pl.multiple_of(place[0] * half, half)
+    rows = dests[0].shape[0]
+    first = dests[1].shape[1]
+    sources = (
+        up.at[pl.ds(pl.multiple_of(place[1] * rows, rows), rows)],
+        down.at[:, pl.ds(start, first)],
+        down.at[:, pl.ds(start + first, half - first)],
+        out.at[:, pl.ds(start, half)],
+    )
+    reads = [pltpu.make_async_copy(a, b, sems.at[0, i]) for i, (a, b) in enumerate(zip(sources, bufs))]
+    writes = [pltpu.make_async_copy(a, b, sems.at[1, i]) for i, (a, b) in enumerate(zip(bufs, dests))]
+    for copy in reads:
         copy.start()
-    for copy in copies:
+    for read, write in zip(reads, writes):
+        read.wait()
+        write.start()
+    for copy in writes:
         copy.wait()
 
 
-def halves(core, up, down, out, up_most, down_most):
+def pieces_of(place, up, down, out, down_most):
     d_model, hidden = up.shape
     half = d_model // 2
     hbm = pl.BlockSpec(memory_space=pltpu.MemorySpace.HBM)
     shapes = (
-        (up_most, hidden),
-        (half - up_most, hidden),
+        (d_model // 4, hidden),
         (hidden, down_most),
         (hidden, half - down_most),
         (out.shape[0], half),
     )
     return pl.pallas_call(
-        halves_body,
+        pieces_body,
         grid_spec=pltpu.PrefetchScalarGridSpec(
             num_scalar_prefetch=1,
             grid=(1,),
             in_specs=[hbm] * 3,
-            out_specs=[hbm] * 5,
-            scratch_shapes=[pltpu.SemaphoreType.DMA((5,))],
+            out_specs=[hbm] * 4,
+            scratch_shapes=[
+                *[pltpu.VMEM(shape, up.dtype) for shape in shapes],
+                pltpu.SemaphoreType.DMA((2, 4)),
+            ],
         ),
         out_shape=[jax.ShapeDtypeStruct(shape, up.dtype) for shape in shapes],
-    )(core.reshape(1), up, down, out)
+        compiler_params=pltpu.CompilerParams(vmem_limit_bytes=8 << 20),
+    )(place, up, down, out)
 
 
 tie = lax.optimization_barrier
@@ -422,13 +435,17 @@
     row_block, d_model = residual_in.shape
 
     vectors = jnp.stack([gate_attn, out_bias, mod_scale, mod_shift])
-    order = jnp.bitwise_xor(2 * core, jnp.arange(4, dtype=jnp.int32))
+    order = jnp.bitwise_xor(
+        jnp.array([2, 2, 2, 2, 0, 0, 0, 0], jnp.int32) * (1 - yl_at)
+        + core * jnp.array([1, 1, 1, 1, 2, 2, 2, 2], jnp.int32),
+        jnp.array([0, 2, 1, 3, 0, 1, 2, 3], jnp.int32),
+    )
     x_at = lax.axis_index("x")
     place = jnp.concatenate(
         [(x_at + jnp.array([0, 3, 1, 2], jnp.int32)) % 4, yh_at.reshape(1).astype(jnp.int32)]
     )
-    up_first, up_late, down_first, down_late, out_half = halves(
-        core, up_weight, down_weight, out_weight, d_model // 24 * 7, d_model // 8 * 3
+    up_first, down_first, down_late, out_half = pieces_of(
+        jnp.stack([core, 2 * yl_at + core]), up_weight, down_weight, out_weight, d_model // 8 * 3
     )
 
     q_other = shift(img_query, "yl", 2, 1)
@@ -462,6 +479,7 @@
     )
     three = around(*two)
     down_a = cross(down_first)
+    up_b = shift(up_a, "yl", 2, 1)
     out_f = shift(out_half, "x", 4, 2)
     state = attend(queries, two, state)
     three, state = tie((three, state))
@@ -471,19 +489,18 @@
     shape = (2, 4, 2, row_block, width + HD)
     (part,) = attend(queries, four, state, shape)
     out_mine = [out_l, out_r, out_f]
-    part, down_a, up_a, out_mine, up_late, down_late = tie(
-        (part, down_a, up_a, out_mine, up_late, down_late)
+    part, down_a, up_a, up_b, out_mine, down_late = tie(
+        (part, down_a, up_a, up_b, out_mine, down_late)
     )
     out_mate = [shift(piece, "dp", 2, 1) for piece in out_mine]
-    up_b = cross(up_late)
     down_b = cross(down_late)
 
     parts = lax.all_to_all(
         part.reshape(8, 2 * row_block, width + HD), ("yl", "x"), split_axis=0, concat_axis=0, tiled=True
     )
     parts, out_mate = tie((parts, out_mate))
-    proj_own, proj_away = join_project(parts, out_weight, out_mine, out_mate, order, place)
-    proj_away, up_b, down_b = tie((proj_away, up_b, down_b))
+    proj_own, proj_away = join_project(parts, out_weight, out_mine, out_mate, order[4:], place)
+    proj_away, down_b = tie((proj_away, down_b))
     proj_other = shift(proj_away, "yh", 2, 1)
     up_far = [up_a, up_b, shift(up_a, "dp", 2, 1), shift(up_b, "dp", 2, 1)]
     down_far = [down_a, down_b, shift(down_a, "dp", 2, 1), shift(down_b, "dp", 2, 1)]

time: 374 us -> 187 us (0.50)
  Pallas kernels: 233 us -> 56 us
  waiting for transfers between devices: 77.4 us -> 61.3 us
  local copies, waits for them, and re-layouts: 5.01 us -> 15.3 us
  starting transfers between devices: 53.1 us -> 49.1 us
    pallas_call x1, Pallas kernels: 180 us -> 3.02 us  [pieces_of(): pl.pallas_call(pieces_body, grid_spec=pltpu.PrefetchScalarGridSpec(num_sc...]
    ppermute x5 -> x4, waiting for transfers between devices: 21.3 us -> 5.48 us  [cross(): return lax.ppermute(array, ('yl', 'yh'), [(0, 3), (3, 0), (1, 2), (2, 1)])]
    unnamed x38 -> x58, local copies, waits for them, and re-layouts: 4.83 us -> 15 us
    ppermute x27 -> x28, waiting for transfers between devices: 43.6 us -> 41.8 us  [shift(): lax.ppermute(array, axis, [(i, (i + by) % size) for i in range(size)])]
    ppermute x27 -> x28, starting transfers between devices: 39 us -> 38.2 us  [shift(): lax.ppermute(array, axis, [(i, (i + by) % size) for i in range(size)])]
  transfers between devices with their start and end apart: 33 -> 33, of which waited for: 11 -> 10; matrix products, arithmetic and copies ran while one was open for 0% -> 1% of each run, Pallas kernels for 60% -> 25%
where the time goes in v4:
time: 187 us; the launch traced here: 186 us
  waiting for transfers between devices  61.3 us (33%)
  Pallas kernels  56 us (30%)
  starting transfers between devices  49.1 us (26%)
  local copies, waits for them, and re-layouts  15.3 us (8%)
  other arithmetic  4.11 us (2%)
    ppermute x28, waiting for transfers between devices, shift(): lax.ppermute(array, axis, [(i, (i + by) % size) for i in range(size)])  41.8 us
    ppermute x28, starting transfers between devices, shift(): lax.ppermute(array, axis, [(i, (i + by) % size) for i in range(size)])  38.2 us
    pallas_call x5, Pallas kernels, attend(): pl.pallas_call(functools.partial(attend_body, len(ks), first, bool(last))...  38.2 us
    unnamed x58, local copies, waits for them, and re-layouts  15 us
    all_to_all x1, waiting for transfers between devices, shards(): lax.all_to_all(part.reshape(8, 2 * row_block, width + HD), ('yl', 'x'), s...  14 us
    pallas_call x1, Pallas kernels, mlp(): pl.pallas_call(mlp_body, grid_spec=pltpu.PrefetchScalarGridSpec(num_scala...  9.13 us
    all_to_all x1, starting transfers between devices, shards(): lax.all_to_all(part.reshape(8, 2 * row_block, width + HD), ('yl', 'x'), s...  5.93 us
    ppermute x4, waiting for transfers between devices, cross(): return lax.ppermute(array, ('yl', 'yh'), [(0, 3), (3, 0), (1, 2), (2, 1)])  5.48 us
  transfers between devices with their start and end apart: 33, of which 10 were waited for; matrix products, arithmetic and copies ran while one was open for 1% of the time, Pallas kernels for 25%

profile of v4, /device:TPU:8, one launch (start us, length us, event | category | flops | bytes accessed | tf_op | source)
XLA Modules:
  0.0 186.2 jit_solution(17318487664536522578)
XLA Ops:
  0.0 1.3 maximum_maximum_fusion.refs_1_.refs_2_
  1.3 2.0 %collective-permute-start = (bf16[528,768]{1,0:T(8,128)(2,1)S(1)}, bf16[528,768]{1,0:T(8,128)(2,1)}, u32[]{:S(2)}, u32[]{:S(2)}) collective-permute-start(bf16[528,768]{1,0:T(8,128)(2,1)S(1)} %maximum_maximum_fusion.refs_1_.refs_2_), channel_id=1, source_target_pairs={{0,16},{16,32},{32,48},{48,64},{64,80},{80,96},{96,112},{112,0},{1... | collective-permute-start | bytes 2433032 | tf_op jit(solution)/shard_map/ppermute | solution.py:347
  3.3 4.0 %collective-permute-start.1 = (bf16[528,768]{1,0:T(8,128)(2,1)S(1)}, bf16[528,768]{1,0:T(8,128)(2,1)}, u32[]{:S(2)}, u32[]{:S(2)}) collective-permute-start(bf16[528,768]{1,0:T(8,128)(2,1)S(1)} %maximum_maximum_fusion.refs_1_.refs_2_), channel_id=1, source_target_pairs={{0,112},{16,0},{32,16},{48,32},{64,48},{80,64},{96,80},{112,96},{1... | collective-permute-start | bytes 2433032 | tf_op jit(solution)/shard_map/ppermute | solution.py:347
  7.8 2.3 %copy-done = bf16[3072,768]{1,0:T(8,128)(2,1)S(1)} copy-done((bf16[3072,768]{1,0:T(8,128)(2,1)S(1)}, bf16[3072,768]{1,0:T(8,128)(2,1)}, u32[]{:S(2)}) %copy-start) | copy-done | bytes 4718616
  10.2 2.3 %copy-done.2 = bf16[768,3072]{1,0:T(8,128)(2,1)S(1)} copy-done((bf16[768,3072]{1,0:T(8,128)(2,1)S(1)}, bf16[768,3072]{1,0:T(8,128)(2,1)}, u32[]{:S(2)}) %copy-start.2) | copy-done | bytes 4718616
  12.5 1.7 copy-done.4
  14.2 3.0 %shard_map.192 = (bf16[768,768]{1,0:T(8,128)(2,1)S(1)}, bf16[768,1152]{1,0:T(8,128)(2,1)S(1)}, bf16[768,384]{1,0:T(8,128)(2,1)S(1)}, bf16[384,1536]{1,0:T(8,128)(2,1)}) custom-call(s32[2]{0:T(128)S(1)} %pad_add_fusion.1.place, bf16[3072,768]{1,0:T(8,128)(2,1)S(1)} %copy-done, bf16[768,3072]{1,0:T(8,128)(2,1)S(1)} %copy-done.2, bf16[384,3072]{1,0:T(8,128)(2,1)S(1)} %copy-done.4), custom_call_target="tpu_custom_call" | custom-call | tf_op jit(solution)/shard_map/pallas_call | solution.py:387
  17.2 1.2 copy-done.11
  18.4 0.8 copy-done.13
  19.2 1.5 collective-permute-start.6
  20.7 1.7 collective-permute-start.7
  23.2 2.4 %collective-permute-start.5 = (bf16[768,768]{1,0:T(8,128)(2,1)S(1)}, bf16[768,768]{1,0:T(8,128)(2,1)S(1)}, u32[]{:S(2)}, u32[]{:S(2)}) collective-permute-start(bf16[768,768]{1,0:T(8,128)(2,1)S(1)} %get-tuple-element.80), channel_id=1, source_target_pairs={{0,136},{136,0},{8,128},{128,8},{1,137},{137,1},{9,129},{129,9},{2... | collective-permute-start | bytes 3538952 | tf_op jit(solution)/shard_map/ppermute | solution.py:351
  25.6 3.2 %collective-permute-start.4 = (bf16[528,768]{1,0:T(8,128)(2,1)}, bf16[528,768]{1,0:T(8,128)(2,1)}, u32[]{:S(2)}, u32[]{:S(2)}) collective-permute-start(bf16[528,768]{1,0:T(8,128)(2,1)} %collective-permute-done.1.refs_2_.refs_4_), channel_id=1, source_target_pairs={{0,112},{16,0},{32,16},{48,32},{64,48},{80,64},{96,80},{112,96},{1... | collective-permute-start | bytes 2433032 | tf_op jit(solution)/shard_map/ppermute | solution.py:347
  28.9 1.6 maximum_select_fusion.refs_0_
  30.5 5.1 %shard_map.190 = (f32[3,1,1024]{2,1,0:T(1,128)S(1)}, f32[3,1,1024]{2,1,0:T(1,128)S(1)}, f32[384,1024]{1,0:T(8,128)S(1)}) custom-call(bf16[1024,384]{1,0:T(8,128)(2,1)S(1)} %maximum_select_fusion.refs_0_, bf16[528,768]{1,0:T(8,128)(2,1)S(1)} %maximum_maximum_fusion.refs_1_.refs_2_, bf16[528,768]{1,0:T(8,128)(2,1)S(1)} %maximum_maximum_fusion.refs_1_.refs_2_), custom_call_target="tpu_custom_call" | custom-call | flops 830472192 | bytes 1597440 | tf_op jit(solution)/shard_map/pallas_call | solution.py:111
  35.6 9.0 %shard_map.191 = (f32[3,1,1024]{2,1,0:T(1,128)S(1)}, f32[3,1,1024]{2,1,0:T(1,128)S(1)}, f32[384,1024]{1,0:T(8,128)S(1)}) custom-call(bf16[1024,384]{1,0:T(8,128)(2,1)S(1)} %maximum_select_fusion.refs_0_, bf16[528,768]{1,0:T(8,128)(2,1)} %collective-permute-done.refs_1_.refs_3_, bf16[528,768]{1,0:T(8,128)(2,1)} %collective-permute-done.1.refs_2_.refs_4_, ...), custom_call_target="tpu_custom_call" | custom-call | flops 1660944384 | bytes 2408448 | tf_op jit(solution)/shard_map/pallas_call | solution.py:111
  44.6 3.3 %collective-permute-done.6.refs_0_ = bf16[384,1536]{1,0:T(8,128)(2,1)} collective-permute-done((bf16[384,1536]{1,0:T(8,128)(2,1)}, bf16[384,1536]{1,0:T(8,128)(2,1)}, u32[]{:S(2)}, u32[]{:S(2)}) %collective-permute-start.6) | collective-permute-done | bytes 1179680 | tf_op jit(solution)/shard_map/ppermute | solution.py:347
  47.9 2.6 %collective-permute-done.5.refs_0_ = bf16[768,768]{1,0:T(8,128)(2,1)S(1)} collective-permute-done((bf16[768,768]{1,0:T(8,128)(2,1)S(1)}, bf16[768,768]{1,0:T(8,128)(2,1)S(1)}, u32[]{:S(2)}, u32[]{:S(2)}) %collective-permute-start.5) | collective-permute-done | bytes 1179680 | tf_op jit(solution)/shard_map/ppermute | solution.py:351
  50.5 1.8 collective-permute-start.12
  52.3 3.2 %collective-permute-start.9 = (bf16[528,768]{1,0:T(8,128)(2,1)}, bf16[528,768]{1,0:T(8,128)(2,1)S(1)}, u32[]{:S(2)}, u32[]{:S(2)}) collective-permute-start(bf16[528,768]{1,0:T(8,128)(2,1)} %collective-permute-done.4.refs_2_.refs_4_), channel_id=1, source_target_pairs={{0,112},{16,0},{32,16},{48,32},{64,48},{80,64},{96,80},{112,96},{1... | collective-permute-start | bytes 2433032 | tf_op jit(solution)/shard_map/ppermute | solution.py:347
  55.6 2.6 %collective-permute-start.13 = (bf16[768,768]{1,0:T(8,128)(2,1)S(1)}, bf16[768,768]{1,0:T(8,128)(2,1)S(1)}, u32[]{:S(2)}, u32[]{:S(2)}) collective-permute-start(bf16[768,768]{1,0:T(8,128)(2,1)S(1)} %collective-permute-done.5.refs_0_), channel_id=1, source_target_pairs={{0,128},{128,0},{1,129},{129,1},{2,130},{130,2},{3,131},{131,3},{4... | collective-permute-start | bytes 3538952 | tf_op jit(solution)/shard_map/ppermute | solution.py:347
  58.1 1.8 collective-permute-start.14
  59.9 8.9 %shard_map.193 = (f32[3,1,1024]{2,1,0:T(1,128)S(1)}, f32[3,1,1024]{2,1,0:T(1,128)S(1)}, f32[384,1024]{1,0:T(8,128)S(1)}) custom-call(bf16[1024,384]{1,0:T(8,128)(2,1)S(1)} %maximum_select_fusion.refs_0_, bf16[528,768]{1,0:T(8,128)(2,1)} %collective-permute-done.3.refs_1_.refs_3_, bf16[528,768]{1,0:T(8,128)(2,1)} %collective-permute-done.4.refs_2_.refs_4_, ...), custom_call_target="tpu_custom_call" | custom-call | flops 1660944384 | bytes 2408448 | tf_op jit(solution)/shard_map/pallas_call | solution.py:111
  68.8 2.5 %collective-permute-done.8.refs_1_.refs_3_ = bf16[528,768]{1,0:T(8,128)(2,1)S(1)} collective-permute-done((bf16[528,768]{1,0:T(8,128)(2,1)}, bf16[528,768]{1,0:T(8,128)(2,1)S(1)}, u32[]{:S(2)}, u32[]{:S(2)}) %collective-permute-start.8) | collective-permute-done | bytes 811040 | tf_op jit(solution)/shard_map/ppermute | solution.py:347
  71.5 3.3 %collective-permute-start.11 = (bf16[256,768]{1,0:T(8,128)(2,1)S(1)}, bf16[256,768]{1,0:T(8,128)(2,1)S(1)}, u32[]{:S(2)}, u32[]{:S(2)}) collective-permute-start(bf16[256,768]{1,0:T(8,128)(2,1)S(1)} %slice.33), channel_id=1, source_target_pairs={{0,112},{16,0},{32,16},{48,32},{64,48},{80,64},{96,80},{112,96},{1... | collective-permute-start | bytes 1179656 | tf_op jit(solution)/shard_map/ppermute | solution.py:347
  74.8 8.0 %shard_map.194 = (f32[3,1,1024]{2,1,0:T(1,128)S(1)}, f32[3,1,1024]{2,1,0:T(1,128)S(1)}, f32[384,1024]{1,0:T(8,128)S(1)}) custom-call(bf16[1024,384]{1,0:T(8,128)(2,1)S(1)} %maximum_select_fusion.refs_0_, bf16[528,768]{1,0:T(8,128)(2,1)S(1)} %collective-permute-done.8.refs_1_.refs_3_, bf16[528,768]{1,0:T(8,128)(2,1)S(1)} %collective-permute-done.9.refs_2_.refs_4_, ...), custom_call_target="tpu_custom_call" | custom-call | flops 1660944384 | bytes 2408448 | tf_op jit(solution)/shard_map/pallas_call | solution.py:111
  82.8 7.3 %shard_map.195 = bf16[2,4,2,64,512]{4,3,2,1,0:T(8,128)(2,1)} custom-call(bf16[1024,384]{1,0:T(8,128)(2,1)S(1)} %maximum_select_fusion.refs_0_, bf16[272,768]{1,0:T(8,128)(2,1)S(1)} %collective-permute-done.10.refs_1_.refs_3_, bf16[256,768]{1,0:T(8,128)(2,1)S(1)} %collective-permute-done.11.refs_2_.refs_4_, ...), custom_call_target="tpu_custom_call" | custom-call | flops 830472192 | bytes 1597440 | tf_op jit(solution)/shard_map/pallas_call | solution.py:111
  90.1 1.1 copy-done.8
  92.2 5.9 %all-to-all-start = ((bf16[8,128,512]{2,1,0:T(8,128)(2,1)}), bf16[8,128,512]{2,1,0:T(8,128)(2,1)S(1)}, u32[]{:S(2)}, u32[]{:S(2)}) async-start(bf16[8,128,512]{2,1,0:T(8,128)(2,1)} %bitcast.3), calls=%async_computation | async-start | bytes 2097152 | tf_op jit(solution)/shard_map/all_to_all | solution.py:498
  98.9 14.0 %all-to-all-done.part_ref = bf16[8,128,512]{2,1,0:T(8,128)(2,1)S(1)} async-done(((bf16[8,128,512]{2,1,0:T(8,128)(2,1)}), bf16[8,128,512]{2,1,0:T(8,128)(2,1)S(1)}, u32[]{:S(2)}, u32[]{:S(2)}) %all-to-all-start) | async-done | bytes 1048608 | tf_op jit(solution)/shard_map/all_to_all | solution.py:498
  112.9 4.5 %shard_map.196 = (f32[64,3072]{1,0:T(8,128)S(1)}, bf16[64,3072]{1,0:T(8,128)(2,1)S(1)}) custom-call(s32[4]{0:T(128)S(1)} %slice.31.order, s32[5]{0:T(128)S(1)} %pad_add_fusion.place, bf16[8,128,512]{2,1,0:T(8,128)(2,1)S(1)} %all-to-all-done.part_ref, bf16[384,3072]{1,0:T(8,128)(2,1)S(1)} %copy-done.5, bf16[384,1536]{1,0:T(8,128)(2,1)} %collective-permute-done.6.refs_0_, ...), custom_call_target="tpu_custom_call" | custom-call | flops 1207959552 | bytes 9437184 | tf_op jit(solution)/shard_map/pallas_call | solution.py:185
  117.6 1.0 collective-permute-start.19
  118.7 11.9 %collective-permute-done.19.other_ref = bf16[64,3072]{1,0:T(8,128)(2,1)S(1)} collective-permute-done((bf16[64,3072]{1,0:T(8,128)(2,1)S(1)}, bf16[64,3072]{1,0:T(8,128)(2,1)S(1)}, u32[]{:S(2)}, u32[]{:S(2)}) %collective-permute-start.19) | collective-permute-done | bytes 393248 | tf_op jit(solution)/shard_map/ppermute | solution.py:347
  130.6 1.1 shard_map.197
  131.7 0.9 collective-permute-start.24
  132.7 2.4 %collective-permute-start.25 = (bf16[64,3072]{1,0:T(8,128)(2,1)S(1)}, bf16[64,3072]{1,0:T(8,128)(2,1)S(1)}, u32[]{:S(2)}, u32[]{:S(2)}) collective-permute-start(bf16[64,3072]{1,0:T(8,128)(2,1)S(1)} %get-tuple-element.128), channel_id=1, source_target_pairs={{0,6},{2,0},{4,2},{6,4},{1,7},{3,1},{5,3},{7,5},{8,14},{10,8},{12,... | collective-permute-start | bytes 1179656 | tf_op jit(solution)/shard_map/ppermute | solution.py:347
  135.8 2.9 %collective-permute-done.28 = f32[768]{0:T(1024)S(1)} collective-permute-done((f32[768]{0:T(1024)S(1)}, f32[768]{0:T(1024)S(1)}, u32[]{:S(2)}, u32[]{:S(2)}) %collective-permute-start.28) | collective-permute-done | bytes 3104 | tf_op jit(solution)/shard_map/ppermute | solution.py:351
  138.7 4.7 %collective-permute-done.24 = bf16[64,3072]{1,0:T(8,128)(2,1)S(1)} collective-permute-done((bf16[64,3072]{1,0:T(8,128)(2,1)S(1)}, bf16[64,3072]{1,0:T(8,128)(2,1)S(1)}, u32[]{:S(2)}, u32[]{:S(2)}) %collective-permute-start.24) | collective-permute-done | bytes 393248 | tf_op jit(solution)/shard_map/ppermute | solution.py:347
  143.6 3.3 %collective-permute-start.27 = (bf16[32,3072]{1,0:T(8,128)(2,1)S(1)}, bf16[32,3072]{1,0:T(8,128)(2,1)S(1)}, u32[]{:S(2)}, u32[]{:S(2)}) collective-permute-start(bf16[32,3072]{1,0:T(8,128)(2,1)S(1)} %slice.41), channel_id=1, source_target_pairs={{0,6},{2,0},{4,2},{6,4},{1,7},{3,1},{5,3},{7,5},{8,14},{10,8},{12,... | collective-permute-start | bytes 589832 | tf_op jit(solution)/shard_map/ppermute | solution.py:347
  146.9 3.5 %collective-permute-done.26 = bf16[32,3072]{1,0:T(8,128)(2,1)S(1)} collective-permute-done((bf16[32,3072]{1,0:T(8,128)(2,1)S(1)}, bf16[32,3072]{1,0:T(8,128)(2,1)S(1)}, u32[]{:S(2)}, u32[]{:S(2)}) %collective-permute-start.26) | collective-permute-done | bytes 196640 | tf_op jit(solution)/shard_map/ppermute | solution.py:347
  150.5 2.3 %copy-done.1 = bf16[3072,768]{1,0:T(8,128)(2,1)S(1)} copy-done((bf16[3072,768]{1,0:T(8,128)(2,1)S(1)}, bf16[3072,768]{1,0:T(8,128)(2,1)}, u32[]{:S(2)}) %copy-start.1) | copy-done | bytes 4718616
  152.8 2.3 %copy-done.3 = bf16[768,3072]{1,0:T(8,128)(2,1)S(1)} copy-done((bf16[768,3072]{1,0:T(8,128)(2,1)S(1)}, bf16[768,3072]{1,0:T(8,128)(2,1)}, u32[]{:S(2)}) %copy-start.3) | copy-done | bytes 4718616
  155.1 9.1 %shard_map.198 = bf16[256,3072]{1,0:T(8,128)(2,1)S(1)} custom-call(s32[8]{0:T(128)S(1)} %add_xor_fusion.order, bf16[256,3072]{1,0:T(8,128)(2,1)S(1)} %constant_dynamic-update-slice_fusion.x_ref, bf16[3072,768]{1,0:T(8,128)(2,1)S(1)} %copy-done.1, bf16[768,3072]{1,0:T(8,128)(2,1)S(1)} %copy-done.3, f32[1,768]{1,0:T(1,128)S(1)} %reshape.25.bias_ref, ...), custom_call_target="tpu_custom_call" | custom-call | flops 4831838208 | bytes 18874368 | tf_op jit(solution)/shard_map/pallas_call | solution.py:312
  164.4 3.4 %collective-permute-start.29 = (bf16[64,3072]{1,0:T(8,128)(2,1)S(1)}, bf16[64,3072]{1,0:T(8,128)(2,1)S(1)}, u32[]{:S(2)}, u32[]{:S(2)}) collective-permute-start(bf16[64,3072]{1,0:T(8,128)(2,1)S(1)} %get-tuple-element.137), channel_id=1, source_target_pairs={{0,6},{2,0},{4,2},{6,4},{1,7},{3,1},{5,3},{7,5},{8,14},{10,8},{12,... | collective-permute-start | bytes 1179656 | tf_op jit(solution)/shard_map/ppermute | solution.py:347
  167.8 1.6 collective-permute-start.31
  169.3 12.4 %collective-permute-done.29 = bf16[64,3072]{1,0:T(8,128)(2,1)S(1)} collective-permute-done((bf16[64,3072]{1,0:T(8,128)(2,1)S(1)}, bf16[64,3072]{1,0:T(8,128)(2,1)S(1)}, u32[]{:S(2)}, u32[]{:S(2)}) %collective-permute-start.29) | collective-permute-done | bytes 393248 | tf_op jit(solution)/shard_map/ppermute | solution.py:347
  181.7 3.4 %collective-permute-done.30 = bf16[64,3072]{1,0:T(8,128)(2,1)S(1)} collective-permute-done((bf16[64,3072]{1,0:T(8,128)(2,1)S(1)}, bf16[64,3072]{1,0:T(8,128)(2,1)S(1)}, u32[]{:S(2)}, u32[]{:S(2)}) %collective-permute-start.30) | collective-permute-done | bytes 393248 | tf_op jit(solution)/shard_map/ppermute | solution.py:347
  185.2 1.0 add_convert_fusion
  (102 shorter events, 4.5 us)
Async XLA Ops:
  1.3 24.4 %collective-permute-start = (bf16[528,768]{1,0:T(8,128)(2,1)S(1)}, bf16[528,768]{1,0:T(8,128)(2,1)}, u32[]{:S(2)}, u32[]{:S(2)}) collective-permute-start(bf16[528,768]{1,0:T(8,128)(2,1)S(1)} %maximum_maximum_fusion.refs_1_.refs_2_), channel_id=1, source_target_pairs={{0,16},{16,32},{32,48},{48,64},{64,80},{80,96},{96,112},{112,0},{1... | collective-permute-start | bytes 2433032 | tf_op jit(solution)/shard_map/ppermute | solution.py:347
  3.3 22.4 %collective-permute-start.1 = (bf16[528,768]{1,0:T(8,128)(2,1)S(1)}, bf16[528,768]{1,0:T(8,128)(2,1)}, u32[]{:S(2)}, u32[]{:S(2)}) collective-permute-start(bf16[528,768]{1,0:T(8,128)(2,1)S(1)} %maximum_maximum_fusion.refs_1_.refs_2_), channel_id=1, source_target_pairs={{0,112},{16,0},{32,16},{48,32},{64,48},{80,64},{96,80},{112,96},{1... | collective-permute-start | bytes 2433032 | tf_op jit(solution)/shard_map/ppermute | solution.py:347
  7.3 15.2 %collective-permute-start.2 = (bf16[512,384]{1,0:T(8,128)(2,1)S(1)}, bf16[512,384]{1,0:T(8,128)(2,1)S(1)}, u32[]{:S(2)}, u32[]{:S(2)}) collective-permute-start(bf16[512,384]{1,0:T(8,128)(2,1)S(1)} %copy-done.14), channel_id=1, source_target_pairs={{0,128},{128,0},{1,129},{129,1},{2,130},{130,2},{3,131},{131,3},{4... | collective-permute-start | bytes 1179656 | tf_op jit(solution)/shard_map/ppermute | solution.py:347
  19.2 28.7 %collective-permute-start.6 = (bf16[384,1536]{1,0:T(8,128)(2,1)}, bf16[384,1536]{1,0:T(8,128)(2,1)}, u32[]{:S(2)}, u32[]{:S(2)}) collective-permute-start(bf16[384,1536]{1,0:T(8,128)(2,1)} %get-tuple-element.108), channel_id=1, source_target_pairs={{0,2},{2,4},{4,6},{6,0},{1,3},{3,5},{5,7},{7,1},{8,10},{10,12},{12... | collective-permute-start | bytes 3538952 | tf_op jit(solution)/shard_map/ppermute | solution.py:347
  20.7 27.2 %collective-permute-start.7 = (bf16[384,1536]{1,0:T(8,128)(2,1)}, bf16[384,1536]{1,0:T(8,128)(2,1)}, u32[]{:S(2)}, u32[]{:S(2)}) collective-permute-start(bf16[384,1536]{1,0:T(8,128)(2,1)} %get-tuple-element.108), channel_id=1, source_target_pairs={{0,6},{2,0},{4,2},{6,4},{1,7},{3,1},{5,3},{7,5},{8,14},{10,8},{12,... | collective-permute-start | bytes 3538952 | tf_op jit(solution)/shard_map/ppermute | solution.py:347
  23.2 27.3 %collective-permute-start.5 = (bf16[768,768]{1,0:T(8,128)(2,1)S(1)}, bf16[768,768]{1,0:T(8,128)(2,1)S(1)}, u32[]{:S(2)}, u32[]{:S(2)}) collective-permute-start(bf16[768,768]{1,0:T(8,128)(2,1)S(1)} %get-tuple-element.80), channel_id=1, source_target_pairs={{0,136},{136,0},{8,128},{128,8},{1,137},{137,1},{9,129},{129,9},{2... | collective-permute-start | bytes 3538952 | tf_op jit(solution)/shard_map/ppermute | solution.py:351
  25.6 24.8 %collective-permute-start.3 = (bf16[528,768]{1,0:T(8,128)(2,1)}, bf16[528,768]{1,0:T(8,128)(2,1)}, u32[]{:S(2)}, u32[]{:S(2)}) collective-permute-start(bf16[528,768]{1,0:T(8,128)(2,1)} %collective-permute-done.refs_1_.refs_3_), channel_id=1, source_target_pairs={{0,16},{16,32},{32,48},{48,64},{64,80},{80,96},{96,112},{112,0},{1... | collective-permute-start | bytes 2433032 | tf_op jit(solution)/shard_map/ppermute | solution.py:347
  25.6 24.8 %collective-permute-start.4 = (bf16[528,768]{1,0:T(8,128)(2,1)}, bf16[528,768]{1,0:T(8,128)(2,1)}, u32[]{:S(2)}, u32[]{:S(2)}) collective-permute-start(bf16[528,768]{1,0:T(8,128)(2,1)} %collective-permute-done.1.refs_2_.refs_4_), channel_id=1, source_target_pairs={{0,112},{16,0},{32,16},{48,32},{64,48},{80,64},{96,80},{112,96},{1... | collective-permute-start | bytes 2433032 | tf_op jit(solution)/shard_map/ppermute | solution.py:347
  35.6 14.9 %copy-start.12 = (bf16[768,1152]{1,0:T(8,128)(2,1)S(1)}, bf16[768,1152]{1,0:T(8,128)(2,1)}, u32[]{:S(2)}) copy-start(bf16[768,1152]{1,0:T(8,128)(2,1)} %copy-done.11) | copy-start | bytes 5308420
  50.5 18.3 %copy-start.6 = (bf16[768,768]{1,0:T(8,128)(2,1)}, bf16[768,768]{1,0:T(8,128)(2,1)S(1)}, u32[]{:S(2)}) copy-start(bf16[768,768]{1,0:T(8,128)(2,1)S(1)} %collective-permute-done.5.refs_0_) | copy-start | bytes 3538948
  50.5 40.7 %collective-permute-start.12 = (bf16[768,1152]{1,0:T(8,128)(2,1)S(1)}, bf16[768,1152]{1,0:T(8,128)(2,1)}, u32[]{:S(2)}, u32[]{:S(2)}) collective-permute-start(bf16[768,1152]{1,0:T(8,128)(2,1)S(1)} %copy-done.12), channel_id=1, source_target_pairs={{0,136},{136,0},{8,128},{128,8},{1,137},{137,1},{9,129},{129,9},{2... | collective-permute-start | bytes 5308424 | tf_op jit(solution)/shard_map/ppermute | solution.py:351
  52.3 19.0 %collective-permute-start.8 = (bf16[528,768]{1,0:T(8,128)(2,1)}, bf16[528,768]{1,0:T(8,128)(2,1)S(1)}, u32[]{:S(2)}, u32[]{:S(2)}) collective-permute-start(bf16[528,768]{1,0:T(8,128)(2,1)} %collective-permute-done.3.refs_1_.refs_3_), channel_id=1, source_target_pairs={{0,16},{16,32},{32,48},{48,64},{64,80},{80,96},{96,112},{112,0},{1... | collective-permute-start | bytes 2433032 | tf_op jit(solution)/shard_map/ppermute | solution.py:347
  52.3 19.0 %collective-permute-start.9 = (bf16[528,768]{1,0:T(8,128)(2,1)}, bf16[528,768]{1,0:T(8,128)(2,1)S(1)}, u32[]{:S(2)}, u32[]{:S(2)}) collective-permute-start(bf16[528,768]{1,0:T(8,128)(2,1)} %collective-permute-done.4.refs_2_.refs_4_), channel_id=1, source_target_pairs={{0,112},{16,0},{32,16},{48,32},{64,48},{80,64},{96,80},{112,96},{1... | collective-permute-start | bytes 2433032 | tf_op jit(solution)/shard_map/ppermute | solution.py:347
  55.6 34.5 %collective-permute-start.13 = (bf16[768,768]{1,0:T(8,128)(2,1)S(1)}, bf16[768,768]{1,0:T(8,128)(2,1)S(1)}, u32[]{:S(2)}, u32[]{:S(2)}) collective-permute-start(bf16[768,768]{1,0:T(8,128)(2,1)S(1)} %collective-permute-done.5.refs_0_), channel_id=1, source_target_pairs={{0,128},{128,0},{1,129},{129,1},{2,130},{130,2},{3,131},{131,3},{4... | collective-permute-start | bytes 3538952 | tf_op jit(solution)/shard_map/ppermute | solution.py:347
  58.1 33.1 %collective-permute-start.14 = (bf16[384,1536]{1,0:T(8,128)(2,1)}, bf16[384,1536]{1,0:T(8,128)(2,1)}, u32[]{:S(2)}, u32[]{:S(2)}) collective-permute-start(bf16[384,1536]{1,0:T(8,128)(2,1)} %get-tuple-element.108), channel_id=1, source_target_pairs={{0,4},{2,6},{4,0},{6,2},{1,5},{3,7},{5,1},{7,3},{8,12},{10,14},{12... | collective-permute-start | bytes 3538952 | tf_op jit(solution)/shard_map/ppermute | solution.py:347
  71.4 11.4 %collective-permute-start.10 = (bf16[272,768]{1,0:T(8,128)(2,1)S(1)}, bf16[272,768]{1,0:T(8,128)(2,1)S(1)}, u32[]{:S(2)}, u32[]{:S(2)}) collective-permute-start(bf16[272,768]{1,0:T(8,128)(2,1)S(1)} %slice.32), channel_id=1, source_target_pairs={{0,16},{16,32},{32,48},{48,64},{64,80},{80,96},{96,112},{112,0},{1... | collective-permute-start | bytes 1253384 | tf_op jit(solution)/shard_map/ppermute | solution.py:347
  71.5 11.3 %collective-permute-start.11 = (bf16[256,768]{1,0:T(8,128)(2,1)S(1)}, bf16[256,768]{1,0:T(8,128)(2,1)S(1)}, u32[]{:S(2)}, u32[]{:S(2)}) collective-permute-start(bf16[256,768]{1,0:T(8,128)(2,1)S(1)} %slice.33), channel_id=1, source_target_pairs={{0,112},{16,0},{32,16},{48,32},{64,48},{80,64},{96,80},{112,96},{1... | collective-permute-start | bytes 1179656 | tf_op jit(solution)/shard_map/ppermute | solution.py:347
  82.8 30.1 %copy-start.5 = (bf16[384,3072]{1,0:T(8,128)(2,1)S(1)}, bf16[384,3072]{1,0:T(8,128)(2,1)}, u32[]{:S(2)}) copy-start(bf16[384,3072]{1,0:T(8,128)(2,1)} %own_w.1) | copy-start | bytes 7077892
  90.1 8.7 %copy-start.25 = (s32[8]{0:T(128)S(1)}, s32[8]{0:T(128)}, u32[]{:S(2)}) copy-start(s32[8]{0:T(128)} %constant.45.clone) | copy-start | bytes 100
  90.1 8.8 %copy-start.26 = (s32[4]{0:T(128)S(1)}, s32[4]{0:T(128)}, u32[]{:S(2)}) copy-start(s32[4]{0:T(128)} %constant.46.clone) | copy-start | bytes 52
  91.2 7.0 %collective-permute-start.15 = (bf16[384,1536]{1,0:T(8,128)(2,1)}, bf16[384,1536]{1,0:T(8,128)(2,1)}, u32[]{:S(2)}, u32[]{:S(2)}) collective-permute-start(bf16[384,1536]{1,0:T(8,128)(2,1)} %collective-permute-done.6.refs_0_), channel_id=1, source_target_pairs={{0,1},{1,0},{2,3},{3,2},{4,5},{5,4},{6,7},{7,6},{8,9},{9,8},{10,11... | collective-permute-start | bytes 3538952 | tf_op jit(solution)/shard_map/ppermute | solution.py:347
  91.2 7.1 %collective-permute-start.16 = (bf16[384,1536]{1,0:T(8,128)(2,1)}, bf16[384,1536]{1,0:T(8,128)(2,1)}, u32[]{:S(2)}, u32[]{:S(2)}) collective-permute-start(bf16[384,1536]{1,0:T(8,128)(2,1)} %collective-permute-done.7.refs_1_), channel_id=1, source_target_pairs={{0,1},{1,0},{2,3},{3,2},{4,5},{5,4},{6,7},{7,6},{8,9},{9,8},{10,11... | collective-permute-start | bytes 3538952 | tf_op jit(solution)/shard_map/ppermute | solution.py:347
  91.7 21.2 %collective-permute-start.17 = (bf16[384,1536]{1,0:T(8,128)(2,1)}, bf16[384,1536]{1,0:T(8,128)(2,1)}, u32[]{:S(2)}, u32[]{:S(2)}) collective-permute-start(bf16[384,1536]{1,0:T(8,128)(2,1)} %collective-permute-done.14.refs_2_), channel_id=1, source_target_pairs={{0,1},{1,0},{2,3},{3,2},{4,5},{5,4},{6,7},{7,6},{8,9},{9,8},{10,11... | collective-permute-start | bytes 3538952 | tf_op jit(solution)/shard_map/ppermute | solution.py:347
  91.8 38.8 %collective-permute-start.22 = (bf16[768,1152]{1,0:T(8,128)(2,1)}, bf16[768,1152]{1,0:T(8,128)(2,1)}, u32[]{:S(2)}, u32[]{:S(2)}) collective-permute-start(bf16[768,1152]{1,0:T(8,128)(2,1)} %collective-permute-done.12.refs_4_), channel_id=1, source_target_pairs={{0,1},{1,0},{2,3},{3,2},{4,5},{5,4},{6,7},{7,6},{8,9},{9,8},{10,11... | collective-permute-start | bytes 5308424 | tf_op jit(solution)/shard_map/ppermute | solution.py:347
  92.2 20.7 %all-to-all-start = ((bf16[8,128,512]{2,1,0:T(8,128)(2,1)}), bf16[8,128,512]{2,1,0:T(8,128)(2,1)S(1)}, u32[]{:S(2)}, u32[]{:S(2)}) async-start(bf16[8,128,512]{2,1,0:T(8,128)(2,1)} %bitcast.3), calls=%async_computation | async-start | bytes 2097152 | tf_op jit(solution)/shard_map/all_to_all | solution.py:498
  98.1 19.3 %collective-permute-start.18 = (bf16[768,384]{1,0:T(8,128)(2,1)}, bf16[768,384]{1,0:T(8,128)(2,1)}, u32[]{:S(2)}, u32[]{:S(2)}) collective-permute-start(bf16[768,384]{1,0:T(8,128)(2,1)} %copy-done.13), channel_id=1, source_target_pairs={{0,136},{136,0},{8,128},{128,8},{1,137},{137,1},{9,129},{129,9},{2... | collective-permute-start | bytes 1769480 | tf_op jit(solution)/shard_map/ppermute | solution.py:351
  98.1 20.5 %collective-permute-start.20 = (bf16[768,768]{1,0:T(8,128)(2,1)}, bf16[768,768]{1,0:T(8,128)(2,1)}, u32[]{:S(2)}, u32[]{:S(2)}) collective-permute-start(bf16[768,768]{1,0:T(8,128)(2,1)} %copy-done.6), channel_id=1, source_target_pairs={{0,1},{1,0},{2,3},{3,2},{4,5},{5,4},{6,7},{7,6},{8,9},{9,8},{10,11... | collective-permute-start | bytes 3538952 | tf_op jit(solution)/shard_map/ppermute | solution.py:347
  98.3 20.4 %collective-permute-start.21 = (bf16[768,768]{1,0:T(8,128)(2,1)}, bf16[768,768]{1,0:T(8,128)(2,1)}, u32[]{:S(2)}, u32[]{:S(2)}) collective-permute-start(bf16[768,768]{1,0:T(8,128)(2,1)} %copy-done.8), channel_id=1, source_target_pairs={{0,1},{1,0},{2,3},{3,2},{4,5},{5,4},{6,7},{7,6},{8,9},{9,8},{10,11... | collective-permute-start | bytes 3538952 | tf_op jit(solution)/shard_map/ppermute | solution.py:347
  98.9 19.6 %copy-start.18 = (f32[3072]{0:T(1024)S(1)}, f32[3072]{0:T(1024)}, u32[]{:S(2)}) copy-start(f32[3072]{0:T(1024)} %param.26) | copy-start | bytes 36868
  98.9 19.6 %copy-start.19 = (f32[3072]{0:T(1024)S(1)}, f32[3072]{0:T(1024)}, u32[]{:S(2)}) copy-start(f32[3072]{0:T(1024)} %param.27) | copy-start | bytes 36868
  98.9 19.6 %copy-start.20 = (f32[3072]{0:T(1024)S(1)}, f32[3072]{0:T(1024)}, u32[]{:S(2)}) copy-start(f32[3072]{0:T(1024)} %param.31) | copy-start | bytes 36868
  98.9 19.6 %copy-start.21 = (f32[3072]{0:T(1024)S(1)}, f32[3072]{0:T(1024)}, u32[]{:S(2)}) copy-start(f32[3072]{0:T(1024)} %param.28) | copy-start | bytes 36868
  112.9 17.7 %copy-start.10 = (bf16[64,3072]{1,0:T(8,128)(2,1)S(1)}, bf16[64,3072]{1,0:T(8,128)(2,1)}, u32[]{:S(2)}) copy-start(bf16[64,3072]{1,0:T(8,128)(2,1)} %residual_ref.1) | copy-start | bytes 1179652
  117.5 17.6 %copy-start.22 = (f32[768]{0:T(1024)S(1)}, f32[768]{0:T(1024)}, u32[]{:S(2)}) copy-start(f32[768]{0:T(1024)} %param.33) | copy-start | bytes 9220
  117.5 13.1 %collective-permute-start.23 = (bf16[768,384]{1,0:T(8,128)(2,1)}, bf16[768,384]{1,0:T(8,128)(2,1)S(1)}, u32[]{:S(2)}, u32[]{:S(2)}) collective-permute-start(bf16[768,384]{1,0:T(8,128)(2,1)} %collective-permute-done.18.refs_5_), channel_id=1, source_target_pairs={{0,1},{1,0},{2,3},{3,2},{4,5},{5,4},{6,7},{7,6},{8,9},{9,8},{10,11... | collective-permute-start | bytes 1769480 | tf_op jit(solution)/shard_map/ppermute | solution.py:347
  117.6 13.0 %collective-permute-start.19 = (bf16[64,3072]{1,0:T(8,128)(2,1)S(1)}, bf16[64,3072]{1,0:T(8,128)(2,1)S(1)}, u32[]{:S(2)}, u32[]{:S(2)}) collective-permute-start(bf16[64,3072]{1,0:T(8,128)(2,1)S(1)} %get-tuple-element.121), channel_id=1, source_target_pairs={{0,8},{8,0},{1,9},{9,1},{2,10},{10,2},{3,11},{11,3},{4,12},{12,4},... | collective-permute-start | bytes 1179656 | tf_op jit(solution)/shard_map/ppermute | solution.py:347
  131.7 11.7 %collective-permute-start.24 = (bf16[64,3072]{1,0:T(8,128)(2,1)S(1)}, bf16[64,3072]{1,0:T(8,128)(2,1)S(1)}, u32[]{:S(2)}, u32[]{:S(2)}) collective-permute-start(bf16[64,3072]{1,0:T(8,128)(2,1)S(1)} %get-tuple-element.128), channel_id=1, source_target_pairs={{0,2},{2,4},{4,6},{6,0},{1,3},{3,5},{5,7},{7,1},{8,10},{10,12},{12... | collective-permute-start | bytes 1179656 | tf_op jit(solution)/shard_map/ppermute | solution.py:347
  132.7 10.9 %collective-permute-start.25 = (bf16[64,3072]{1,0:T(8,128)(2,1)S(1)}, bf16[64,3072]{1,0:T(8,128)(2,1)S(1)}, u32[]{:S(2)}, u32[]{:S(2)}) collective-permute-start(bf16[64,3072]{1,0:T(8,128)(2,1)S(1)} %get-tuple-element.128), channel_id=1, source_target_pairs={{0,6},{2,0},{4,2},{6,4},{1,7},{3,1},{5,3},{7,5},{8,14},{10,8},{12,... | collective-permute-start | bytes 1179656 | tf_op jit(solution)/shard_map/ppermute | solution.py:347
  135.1 3.6 %collective-permute-start.28 = (f32[768]{0:T(1024)S(1)}, f32[768]{0:T(1024)S(1)}, u32[]{:S(2)}, u32[]{:S(2)}) collective-permute-start(f32[768]{0:T(1024)S(1)} %copy-done.22), channel_id=1, source_target_pairs={{0,136},{136,0},{8,128},{128,8},{1,137},{137,1},{9,129},{129,9},{2... | collective-permute-start | bytes 9224 | tf_op jit(solution)/shard_map/ppermute | solution.py:351
  138.7 11.7 %copy-start.7 = (bf16[768,768]{1,0:T(8,128)(2,1)S(1)}, bf16[768,768]{1,0:T(8,128)(2,1)}, u32[]{:S(2)}) copy-start(bf16[768,768]{1,0:T(8,128)(2,1)} %copy-done.6) | copy-start | bytes 3538948
  138.7 11.7 %copy-start.9 = (bf16[768,768]{1,0:T(8,128)(2,1)S(1)}, bf16[768,768]{1,0:T(8,128)(2,1)}, u32[]{:S(2)}) copy-start(bf16[768,768]{1,0:T(8,128)(2,1)} %copy-done.8) | copy-start | bytes 3538948
  143.4 7.0 %collective-permute-start.26 = (bf16[32,3072]{1,0:T(8,128)(2,1)S(1)}, bf16[32,3072]{1,0:T(8,128)(2,1)S(1)}, u32[]{:S(2)}, u32[]{:S(2)}) collective-permute-start(bf16[32,3072]{1,0:T(8,128)(2,1)S(1)} %slice.40), channel_id=1, source_target_pairs={{0,2},{2,4},{4,6},{6,0},{1,3},{3,5},{5,7},{7,1},{8,10},{10,12},{12... | collective-permute-start | bytes 589832 | tf_op jit(solution)/shard_map/ppermute | solution.py:347
  143.6 6.9 %collective-permute-start.27 = (bf16[32,3072]{1,0:T(8,128)(2,1)S(1)}, bf16[32,3072]{1,0:T(8,128)(2,1)S(1)}, u32[]{:S(2)}, u32[]{:S(2)}) collective-permute-start(bf16[32,3072]{1,0:T(8,128)(2,1)S(1)} %slice.41), channel_id=1, source_target_pairs={{0,6},{2,0},{4,2},{6,4},{1,7},{3,1},{5,3},{7,5},{8,14},{10,8},{12,... | collective-permute-start | bytes 589832 | tf_op jit(solution)/shard_map/ppermute | solution.py:347
  164.3 20.9 %copy-start.16 = (f32[3072]{0:T(1024)S(1)}, f32[3072]{0:T(1024)}, u32[]{:S(2)}) copy-start(f32[3072]{0:T(1024)} %param.35) | copy-start | bytes 36868
  164.3 20.9 %copy-start.17 = (f32[3072]{0:T(1024)S(1)}, f32[3072]{0:T(1024)}, u32[]{:S(2)}) copy-start(f32[3072]{0:T(1024)} %param.29) | copy-start | bytes 36868
  164.4 17.4 %collective-permute-start.29 = (bf16[64,3072]{1,0:T(8,128)(2,1)S(1)}, bf16[64,3072]{1,0:T(8,128)(2,1)S(1)}, u32[]{:S(2)}, u32[]{:S(2)}) collective-permute-start(bf16[64,3072]{1,0:T(8,128)(2,1)S(1)} %get-tuple-element.137), channel_id=1, source_target_pairs={{0,6},{2,0},{4,2},{6,4},{1,7},{3,1},{5,3},{7,5},{8,14},{10,8},{12,... | collective-permute-start | bytes 1179656 | tf_op jit(solution)/shard_map/ppermute | solution.py:347
  167.8 17.4 %collective-permute-start.30 = (bf16[64,3072]{1,0:T(8,128)(2,1)S(1)}, bf16[64,3072]{1,0:T(8,128)(2,1)S(1)}, u32[]{:S(2)}, u32[]{:S(2)}) collective-permute-start(bf16[64,3072]{1,0:T(8,128)(2,1)S(1)} %get-tuple-element.139), channel_id=1, source_target_pairs={{0,2},{2,4},{4,6},{6,0},{1,3},{3,5},{5,7},{7,1},{8,10},{10,12},{12... | collective-permute-start | bytes 1179656 | tf_op jit(solution)/shard_map/ppermute | solution.py:347
  167.8 17.4 %collective-permute-start.31 = (bf16[64,3072]{1,0:T(8,128)(2,1)S(1)}, bf16[64,3072]{1,0:T(8,128)(2,1)S(1)}, u32[]{:S(2)}, u32[]{:S(2)}) collective-permute-start(bf16[64,3072]{1,0:T(8,128)(2,1)S(1)} %get-tuple-element.138), channel_id=1, source_target_pairs={{0,4},{2,6},{4,0},{6,2},{1,5},{3,7},{5,1},{7,3},{8,12},{10,14},{12... | collective-permute-start | bytes 1179656 | tf_op jit(solution)/shard_map/ppermute | solution.py:347
  (12 other events, 39.6 us)

commit v5 on v4

--- a/solution.py
+++ b/solution.py
@@ -262,11 +262,15 @@
             yield pltpu.make_async_copy(a.at[:, pl.ds(quarter, first)], to.at[:, pl.ds(0, first)], sem)
             yield pltpu.make_async_copy(b, to.at[:, pl.ds(first, quarter - first)], sems.at[j, 1])
 
+    for j in range(2 * n):
+
+        @pl.when(i == max(j - 2, 0))
+        def _(j=j):
+            for copy in copies(j):
+                copy.start()
+
     @pl.when(i == 0)
     def _():
-        for j in range(2 * n):
-            for copy in copies(j):
-                copy.start()
         near[...] = jnp.broadcast_to(bias_ref[...], near.shape)
         far[...] = jnp.broadcast_to(bias_far_ref[...], far.shape)
 
@@ -339,7 +343,7 @@
             transcendentals=rows * hidden * 2,
             bytes_accessed=8 * d_model * hidden,
         ),
-        compiler_params=pltpu.CompilerParams(vmem_limit_bytes=30 << 20),
+        compiler_params=pltpu.CompilerParams(vmem_limit_bytes=46 << 20),
     )(order, x, up, down, bias.reshape(1, -1), bias_far.reshape(1, -1), *up_far, *down_far)
 
 
@@ -351,54 +355,14 @@
     return lax.ppermute(array, ("yl", "yh"), [(0, 3), (3, 0), (1, 2), (2, 1)])
 
 
-def pieces_body(place, up, down, out, *refs):
-    dests, bufs, sems = refs[:4], refs[4:8], refs[8]
-    half = out.shape[1] // 2
-    start = pl.multiple_of(place[0] * half, half)
-    rows = dests[0].shape[0]
-    first = dests[1].shape[1]
-    sources = (
-        up.at[pl.ds(pl.multiple_of(place[1] * rows, rows), rows)],
-        down.at[:, pl.ds(start, first)],
-        down.at[:, pl.ds(start + first, half - first)],
-        out.at[:, pl.ds(start, half)],
-    )
-    reads = [pltpu.make_async_copy(a, b, sems.at[0, i]) for i, (a, b) in enumerate(zip(sources, bufs))]
-    writes = [pltpu.make_async_copy(a, b, sems.at[1, i]) for i, (a, b) in enumerate(zip(bufs, dests))]
-    for copy in reads:
-        copy.start()
-    for read, write in zip(reads, writes):
-        read.wait()
-        write.start()
-    for copy in writes:
-        copy.wait()
-
-
-def pieces_of(place, up, down, out, down_most):
-    d_model, hidden = up.shape
-    half = d_model // 2
-    hbm = pl.BlockSpec(memory_space=pltpu.MemorySpace.HBM)
-    shapes = (
-        (d_model // 4, hidden),
-        (hidden, down_most),
-        (hidden, half - down_most),
-        (out.shape[0], half),
-    )
-    return pl.pallas_call(
-        pieces_body,
-        grid_spec=pltpu.PrefetchScalarGridSpec(
-            num_scalar_prefetch=1,
-            grid=(1,),
-            in_specs=[hbm] * 3,
-            out_specs=[hbm] * 4,
-            scratch_shapes=[
-                *[pltpu.VMEM(shape, up.dtype) for shape in shapes],
-                pltpu.SemaphoreType.DMA((2, 4)),
-            ],
-        ),
-        out_shape=[jax.ShapeDtypeStruct(shape, up.dtype) for shape in shapes],
-        compiler_params=pltpu.CompilerParams(vmem_limit_bytes=8 << 20),
-    )(place, up, down, out)
+def part_of(array, parts, index, axis):
+    n = array.shape[axis] // parts
+    return lax.dynamic_slice_in_dim(array, index * n, n, axis)
+
+
+def half_of(array, index, axis, start, stop):
+    n = array.shape[axis] // 2
+    return lax.dynamic_slice_in_dim(array, index * n + start, stop - start, axis)
 
 
 tie = lax.optimization_barrier
@@ -444,9 +408,8 @@
     place = jnp.concatenate(
         [(x_at + jnp.array([0, 3, 1, 2], jnp.int32)) % 4, yh_at.reshape(1).astype(jnp.int32)]
     )
-    up_first, down_first, down_late, out_half = pieces_of(
-        jnp.stack([core, 2 * yl_at + core]), up_weight, down_weight, out_weight, d_model // 8 * 3
-    )
+    down_most = d_model // 8 * 3
+    out_half = part_of(out_weight, 2, core, 1)
 
     q_other = shift(img_query, "yl", 2, 1)
     own = jnp.concatenate(
@@ -462,10 +425,12 @@
         return [shift(up, "z", 8, 1), shift(down, "z", 8, 7)]
 
     one = around(own, own)
-    up_a = cross(up_first)
+    up_a = cross(part_of(up_weight, 4, 2 * yl_at + core, 0))
     out_l = shift(out_half, "x", 4, 1)
     out_r = shift(out_half, "x", 4, 3)
-    one, q_other = tie((one, q_other))
+    down_first = half_of(down_weight, core, 1, 0, down_most)
+    down_late = half_of(down_weight, core, 1, down_most, d_model // 2)
+    one, q_other, down_first, down_late = tie((one, q_other, down_first, down_late))
     queries = jnp.where(
         yl_at == 0,
         jnp.concatenate([img_query, q_other], axis=0),

time: 187 us -> 182 us (0.973)
  local copies, waits for them, and re-layouts: 15.3 us -> 12.3 us
  waiting for transfers between devices: 61.3 us -> 59.4 us
    unnamed x58 -> x44, local copies, waits for them, and re-layouts: 15 us -> 2.45 us
    dynamic_slice x0 -> x4, local copies, waits for them, and re-layouts: none -> 9.55 us  [the longest x2 4.8 us: half_of(): lax.dynamic_slice_in_dim(array, index * n + start, stop - start, axis)]
    pallas_call x1, Pallas kernels: 9.13 us -> 12.4 us  [mlp(): pl.pallas_call(mlp_body, grid_spec=pltpu.PrefetchScalarGridSpec(num_scala...]
    pallas_call x1 -> x0, Pallas kernels: 3.02 us -> none  [pieces_of(): pl.pallas_call(pieces_body, grid_spec=pltpu.PrefetchScalarGridSpec(num_sc...]
    ppermute x4, waiting for transfers between devices: 5.48 us -> 3.29 us  [cross(): return lax.ppermute(array, ('yl', 'yh'), [(0, 3), (3, 0), (1, 2), (2, 1)])]
  transfers between devices with their start and end apart: 33 -> 33, of which waited for: 10 -> 12; matrix products, arithmetic and copies ran while one was open for 1% -> 6% of each run, Pallas kernels for 25% -> 23%
where the time goes in v5:
time: 182 us
  waiting for transfers between devices  59.4 us (33%)
  Pallas kernels  56.1 us (31%)
  starting transfers between devices  49.5 us (27%)
  local copies, waits for them, and re-layouts  12.3 us (7%)
  other arithmetic  3.83 us (2%)
    ppermute x28, waiting for transfers between devices, shift(): lax.ppermute(array, axis, [(i, (i + by) % size) for i in range(size)])  42.5 us
    ppermute x28, starting transfers between devices, shift(): lax.ppermute(array, axis, [(i, (i + by) % size) for i in range(size)])  39.3 us
    pallas_call x5, Pallas kernels, attend(): pl.pallas_call(functools.partial(attend_body, len(ks), first, bool(last))...  38.1 us
    all_to_all x1, waiting for transfers between devices, shards(): lax.all_to_all(part.reshape(8, 2 * row_block, width + HD), ('yl', 'x'), s...  13.7 us
    pallas_call x1, Pallas kernels, mlp(): pl.pallas_call(mlp_body, grid_spec=pltpu.PrefetchScalarGridSpec(num_scala...  12.4 us
    all_to_all x1, starting transfers between devices, shards(): lax.all_to_all(part.reshape(8, 2 * row_block, width + HD), ('yl', 'x'), s...  5.99 us
    dynamic_slice x2, local copies, waits for them, and re-layouts, half_of(): lax.dynamic_slice_in_dim(array, index * n + start, stop - start, axis)  4.8 us
    dynamic_slice x2, local copies, waits for them, and re-layouts, part_of(): return lax.dynamic_slice_in_dim(array, index * n, n, axis)  4.75 us
  transfers between devices with their start and end apart: 33, of which 12 were waited for; matrix products, arithmetic and copies ran while one was open for 6% of the time, Pallas kernels for 23%

profile of v5, /device:TPU:8, one launch (start us, length us, event | category | flops | bytes accessed | tf_op | source)
XLA Modules:
  0.0 181.5 jit_solution(11003815550684045383)
XLA Ops:
  0.0 1.3 maximum_maximum_fusion.refs_1_.refs_2_
  1.3 2.0 %collective-permute-start = (bf16[528,768]{1,0:T(8,128)(2,1)S(1)}, bf16[528,768]{1,0:T(8,128)(2,1)S(1)}, u32[]{:S(2)}, u32[]{:S(2)}) collective-permute-start(bf16[528,768]{1,0:T(8,128)(2,1)S(1)} %maximum_maximum_fusion.refs_1_.refs_2_), channel_id=1, source_target_pairs={{0,16},{16,32},{32,48},{48,64},{64,80},{80,96},{96,112},{112,0},{1... | collective-permute-start | bytes 2433032 | tf_op jit(solution)/shard_map/ppermute | solution.py:351
  3.3 4.0 %collective-permute-start.1 = (bf16[528,768]{1,0:T(8,128)(2,1)S(1)}, bf16[528,768]{1,0:T(8,128)(2,1)}, u32[]{:S(2)}, u32[]{:S(2)}) collective-permute-start(bf16[528,768]{1,0:T(8,128)(2,1)S(1)} %maximum_maximum_fusion.refs_1_.refs_2_), channel_id=1, source_target_pairs={{0,112},{16,0},{32,16},{48,32},{64,48},{80,64},{96,80},{112,96},{1... | collective-permute-start | bytes 2433032 | tf_op jit(solution)/shard_map/ppermute | solution.py:351
  7.7 2.4 %constant_dynamic-slice_fusion = bf16[384,1536]{1,0:T(8,128)(2,1)} fusion(bf16[384,3072]{1,0:T(8,128)(2,1)} %own_w.1, s32[]{:T(128)S(6)} %select_n.27), kind=kLoop, calls=%fused_computation.12 | loop fusion | bytes 2359300 | tf_op jit(solution)/shard_map/dynamic_slice | solution.py:360
  10.1 1.5 collective-permute-start.6
  11.6 1.7 collective-permute-start.7
  13.4 2.4 %constant_dynamic-slice_fusion.1 = bf16[768,768]{1,0:T(8,128)(2,1)} fusion(bf16[3072,768]{1,0:T(8,128)(2,1)} %up_ref.1, s32[]{:T(128)S(6)} %select_n.30), kind=kLoop, calls=%fused_computation.13 | loop fusion | bytes 2359300 | tf_op jit(solution)/shard_map/dynamic_slice | solution.py:360
  15.7 2.2 %collective-permute-done.2 = bf16[512,384]{1,0:T(8,128)(2,1)} collective-permute-done((bf16[512,384]{1,0:T(8,128)(2,1)S(1)}, bf16[512,384]{1,0:T(8,128)(2,1)}, u32[]{:S(2)}, u32[]{:S(2)}) %collective-permute-start.2) | collective-permute-done | bytes 393248 | tf_op jit(solution)/shard_map/ppermute | solution.py:351
  18.0 1.6 collective-permute-start.5
  19.6 1.9 %constant_dynamic-slice_fusion.2 = bf16[768,384]{1,0:T(8,128)(2,1)} fusion(bf16[768,3072]{1,0:T(8,128)(2,1)} %down_ref.1, s32[]{:T(128)S(6)} %select_n.28), kind=kLoop, calls=%fused_computation.14 | loop fusion | bytes 1179652 | tf_op jit(solution)/shard_map/dynamic_slice | solution.py:365
  21.5 2.9 %constant_dynamic-slice_fusion.3 = bf16[768,1152]{1,0:T(8,128)(2,1)} fusion(bf16[768,3072]{1,0:T(8,128)(2,1)} %down_ref.1, s32[]{:T(128)S(6)} %select_n.27), kind=kLoop, calls=%fused_computation.15 | loop fusion | bytes 3538948 | tf_op jit(solution)/shard_map/dynamic_slice | solution.py:365
  25.3 3.2 %collective-permute-start.4 = (bf16[528,768]{1,0:T(8,128)(2,1)}, bf16[528,768]{1,0:T(8,128)(2,1)}, u32[]{:S(2)}, u32[]{:S(2)}) collective-permute-start(bf16[528,768]{1,0:T(8,128)(2,1)} %collective-permute-done.1.refs_2_.refs_4_), channel_id=1, source_target_pairs={{0,112},{16,0},{32,16},{48,32},{64,48},{80,64},{96,80},{112,96},{1... | collective-permute-start | bytes 2433032 | tf_op jit(solution)/shard_map/ppermute | solution.py:351
  28.5 1.4 maximum_select_fusion.refs_0_
  29.9 5.1 %shard_map.190 = (f32[3,1,1024]{2,1,0:T(1,128)S(1)}, f32[3,1,1024]{2,1,0:T(1,128)S(1)}, f32[384,1024]{1,0:T(8,128)S(1)}) custom-call(bf16[1024,384]{1,0:T(8,128)(2,1)S(1)} %maximum_select_fusion.refs_0_, bf16[528,768]{1,0:T(8,128)(2,1)S(1)} %maximum_maximum_fusion.refs_1_.refs_2_, bf16[528,768]{1,0:T(8,128)(2,1)S(1)} %maximum_maximum_fusion.refs_1_.refs_2_), custom_call_target="tpu_custom_call" | custom-call | flops 830472192 | bytes 1597440 | tf_op jit(solution)/shard_map/pallas_call | solution.py:111
  35.0 8.9 %shard_map.191 = (f32[3,1,1024]{2,1,0:T(1,128)S(1)}, f32[3,1,1024]{2,1,0:T(1,128)S(1)}, f32[384,1024]{1,0:T(8,128)S(1)}) custom-call(bf16[1024,384]{1,0:T(8,128)(2,1)S(1)} %maximum_select_fusion.refs_0_, bf16[528,768]{1,0:T(8,128)(2,1)S(1)} %collective-permute-done.refs_1_.refs_3_, bf16[528,768]{1,0:T(8,128)(2,1)} %collective-permute-done.1.refs_2_.refs_4_, ...), custom_call_target="tpu_custom_call" | custom-call | flops 1660944384 | bytes 2408448 | tf_op jit(solution)/shard_map/pallas_call | solution.py:111
  44.7 1.2 collective-permute-done.3.refs_1_.refs_3_
  46.0 1.6 collective-permute-start.12
  47.5 2.0 %collective-permute-start.8 = (bf16[528,768]{1,0:T(8,128)(2,1)}, bf16[528,768]{1,0:T(8,128)(2,1)S(1)}, u32[]{:S(2)}, u32[]{:S(2)}) collective-permute-start(bf16[528,768]{1,0:T(8,128)(2,1)} %collective-permute-done.3.refs_1_.refs_3_), channel_id=1, source_target_pairs={{0,16},{16,32},{32,48},{48,64},{64,80},{80,96},{96,112},{112,0},{1... | collective-permute-start | bytes 2433032 | tf_op jit(solution)/shard_map/ppermute | solution.py:351
  49.6 1.2 collective-permute-start.9
  50.8 2.0 %collective-permute-start.13 = (bf16[768,768]{1,0:T(8,128)(2,1)S(1)}, bf16[768,768]{1,0:T(8,128)(2,1)S(1)}, u32[]{:S(2)}, u32[]{:S(2)}) collective-permute-start(bf16[768,768]{1,0:T(8,128)(2,1)S(1)} %collective-permute-done.5.refs_0_), channel_id=1, source_target_pairs={{0,128},{128,0},{1,129},{129,1},{2,130},{130,2},{3,131},{131,3},{4... | collective-permute-start | bytes 3538952 | tf_op jit(solution)/shard_map/ppermute | solution.py:351
  52.7 3.0 %collective-permute-start.14 = (bf16[384,1536]{1,0:T(8,128)(2,1)}, bf16[384,1536]{1,0:T(8,128)(2,1)}, u32[]{:S(2)}, u32[]{:S(2)}) collective-permute-start(bf16[384,1536]{1,0:T(8,128)(2,1)} %constant_dynamic-slice_fusion), channel_id=1, source_target_pairs={{0,4},{2,6},{4,0},{6,2},{1,5},{3,7},{5,1},{7,3},{8,12},{10,14},{12... | collective-permute-start | bytes 3538952 | tf_op jit(solution)/shard_map/ppermute | solution.py:351
  55.8 8.9 %shard_map.192 = (f32[3,1,1024]{2,1,0:T(1,128)S(1)}, f32[3,1,1024]{2,1,0:T(1,128)S(1)}, f32[384,1024]{1,0:T(8,128)S(1)}) custom-call(bf16[1024,384]{1,0:T(8,128)(2,1)S(1)} %maximum_select_fusion.refs_0_, bf16[528,768]{1,0:T(8,128)(2,1)} %collective-permute-done.3.refs_1_.refs_3_, bf16[528,768]{1,0:T(8,128)(2,1)} %collective-permute-done.4.refs_2_.refs_4_, ...), custom_call_target="tpu_custom_call" | custom-call | flops 1660944384 | bytes 2408448 | tf_op jit(solution)/shard_map/pallas_call | solution.py:111
  64.7 2.5 %collective-permute-done.8.refs_1_.refs_3_ = bf16[528,768]{1,0:T(8,128)(2,1)S(1)} collective-permute-done((bf16[528,768]{1,0:T(8,128)(2,1)}, bf16[528,768]{1,0:T(8,128)(2,1)S(1)}, u32[]{:S(2)}, u32[]{:S(2)}) %collective-permute-start.8) | collective-permute-done | bytes 811040 | tf_op jit(solution)/shard_map/ppermute | solution.py:351
  67.2 1.8 %collective-permute-start.10 = (bf16[272,768]{1,0:T(8,128)(2,1)S(1)}, bf16[272,768]{1,0:T(8,128)(2,1)S(1)}, u32[]{:S(2)}, u32[]{:S(2)}) collective-permute-start(bf16[272,768]{1,0:T(8,128)(2,1)S(1)} %slice.32), channel_id=1, source_target_pairs={{0,16},{16,32},{32,48},{48,64},{64,80},{80,96},{96,112},{112,0},{1... | collective-permute-start | bytes 1253384 | tf_op jit(solution)/shard_map/ppermute | solution.py:351
  69.0 1.6 collective-permute-start.11
  70.6 8.0 %shard_map.193 = (f32[3,1,1024]{2,1,0:T(1,128)S(1)}, f32[3,1,1024]{2,1,0:T(1,128)S(1)}, f32[384,1024]{1,0:T(8,128)S(1)}) custom-call(bf16[1024,384]{1,0:T(8,128)(2,1)S(1)} %maximum_select_fusion.refs_0_, bf16[528,768]{1,0:T(8,128)(2,1)S(1)} %collective-permute-done.8.refs_1_.refs_3_, bf16[528,768]{1,0:T(8,128)(2,1)S(1)} %collective-permute-done.9.refs_2_.refs_4_, ...), custom_call_target="tpu_custom_call" | custom-call | flops 1660944384 | bytes 2408448 | tf_op jit(solution)/shard_map/pallas_call | solution.py:111
  78.6 7.3 %shard_map.194 = bf16[2,4,2,64,512]{4,3,2,1,0:T(8,128)(2,1)} custom-call(bf16[1024,384]{1,0:T(8,128)(2,1)S(1)} %maximum_select_fusion.refs_0_, bf16[272,768]{1,0:T(8,128)(2,1)S(1)} %collective-permute-done.10.refs_1_.refs_3_, bf16[256,768]{1,0:T(8,128)(2,1)S(1)} %collective-permute-done.11.refs_2_.refs_4_, ...), custom_call_target="tpu_custom_call" | custom-call | flops 830472192 | bytes 1597440 | tf_op jit(solution)/shard_map/pallas_call | solution.py:111
  85.8 1.1 copy-done.3
  88.0 6.0 %all-to-all-start = ((bf16[8,128,512]{2,1,0:T(8,128)(2,1)}), bf16[8,128,512]{2,1,0:T(8,128)(2,1)S(1)}, u32[]{:S(2)}, u32[]{:S(2)}) async-start(bf16[8,128,512]{2,1,0:T(8,128)(2,1)} %bitcast.1), calls=%async_computation | async-start | bytes 2097152 | tf_op jit(solution)/shard_map/all_to_all | solution.py:463
  94.8 13.7 %all-to-all-done.part_ref = bf16[8,128,512]{2,1,0:T(8,128)(2,1)S(1)} async-done(((bf16[8,128,512]{2,1,0:T(8,128)(2,1)}), bf16[8,128,512]{2,1,0:T(8,128)(2,1)S(1)}, u32[]{:S(2)}, u32[]{:S(2)}) %all-to-all-start) | async-done | bytes 1048608 | tf_op jit(solution)/shard_map/all_to_all | solution.py:463
  108.5 4.5 %shard_map.195 = (f32[64,3072]{1,0:T(8,128)S(1)}, bf16[64,3072]{1,0:T(8,128)(2,1)S(1)}) custom-call(s32[4]{0:T(128)S(1)} %slice.31.order, s32[5]{0:T(128)S(1)} %pad_add_fusion.place, bf16[8,128,512]{2,1,0:T(8,128)(2,1)S(1)} %all-to-all-done.part_ref, bf16[384,3072]{1,0:T(8,128)(2,1)S(1)} %copy-done, bf16[384,1536]{1,0:T(8,128)(2,1)} %collective-permute-done.6.refs_0_, ...), custom_call_target="tpu_custom_call" | custom-call | flops 1207959552 | bytes 9437184 | tf_op jit(solution)/shard_map/pallas_call | solution.py:185
  113.1 1.4 collective-permute-start.19
  114.6 11.5 %collective-permute-done.19.other_ref = bf16[64,3072]{1,0:T(8,128)(2,1)S(1)} collective-permute-done((bf16[64,3072]{1,0:T(8,128)(2,1)S(1)}, bf16[64,3072]{1,0:T(8,128)(2,1)S(1)}, u32[]{:S(2)}, u32[]{:S(2)}) %collective-permute-start.19) | collective-permute-done | bytes 393248 | tf_op jit(solution)/shard_map/ppermute | solution.py:351
  126.2 1.1 shard_map.196
  127.3 0.9 collective-permute-start.24
  128.2 2.4 %collective-permute-start.25 = (bf16[64,3072]{1,0:T(8,128)(2,1)S(1)}, bf16[64,3072]{1,0:T(8,128)(2,1)S(1)}, u32[]{:S(2)}, u32[]{:S(2)}) collective-permute-start(bf16[64,3072]{1,0:T(8,128)(2,1)S(1)} %get-tuple-element.124), channel_id=1, source_target_pairs={{0,6},{2,0},{4,2},{6,4},{1,7},{3,1},{5,3},{7,5},{8,14},{10,8},{12,... | collective-permute-start | bytes 1179656 | tf_op jit(solution)/shard_map/ppermute | solution.py:351
  130.6 1.1 collective-permute-start.28
  131.7 2.5 %collective-permute-done.28 = f32[768]{0:T(1024)S(1)} collective-permute-done((f32[768]{0:T(1024)S(1)}, f32[768]{0:T(1024)S(1)}, u32[]{:S(2)}, u32[]{:S(2)}) %collective-permute-start.28) | collective-permute-done | bytes 3104 | tf_op jit(solution)/shard_map/ppermute | solution.py:355
  134.3 4.7 %collective-permute-done.24 = bf16[64,3072]{1,0:T(8,128)(2,1)S(1)} collective-permute-done((bf16[64,3072]{1,0:T(8,128)(2,1)S(1)}, bf16[64,3072]{1,0:T(8,128)(2,1)S(1)}, u32[]{:S(2)}, u32[]{:S(2)}) %collective-permute-start.24) | collective-permute-done | bytes 393248 | tf_op jit(solution)/shard_map/ppermute | solution.py:351
  139.1 3.3 %collective-permute-start.27 = (bf16[32,3072]{1,0:T(8,128)(2,1)S(1)}, bf16[32,3072]{1,0:T(8,128)(2,1)S(1)}, u32[]{:S(2)}, u32[]{:S(2)}) collective-permute-start(bf16[32,3072]{1,0:T(8,128)(2,1)S(1)} %slice.41), channel_id=1, source_target_pairs={{0,6},{2,0},{4,2},{6,4},{1,7},{3,1},{5,3},{7,5},{8,14},{10,8},{12,... | collective-permute-start | bytes 589832 | tf_op jit(solution)/shard_map/ppermute | solution.py:351
  142.5 3.5 %collective-permute-done.26 = bf16[32,3072]{1,0:T(8,128)(2,1)S(1)} collective-permute-done((bf16[32,3072]{1,0:T(8,128)(2,1)S(1)}, bf16[32,3072]{1,0:T(8,128)(2,1)S(1)}, u32[]{:S(2)}, u32[]{:S(2)}) %collective-permute-start.26) | collective-permute-done | bytes 196640 | tf_op jit(solution)/shard_map/ppermute | solution.py:351
  146.0 1.2 copy-done.6
  147.2 12.4 %shard_map.197 = bf16[256,3072]{1,0:T(8,128)(2,1)S(1)} custom-call(s32[8]{0:T(128)S(1)} %add_xor_fusion.order, bf16[256,3072]{1,0:T(8,128)(2,1)} %copy-done.6, bf16[3072,768]{1,0:T(8,128)(2,1)} %up_ref.1, bf16[768,3072]{1,0:T(8,128)(2,1)} %down_ref.1, f32[1,768]{1,0:T(1,128)S(1)} %reshape.25.bias_ref, f32[1,768]{1,0:T(1,128)S(1)} %reshape.26.bias_far_ref, ...), custom_call_target="tpu_custom_call" | custom-call | flops 4831838208 | bytes 18874368 | tf_op jit(solution)/shard_map/pallas_call | solution.py:316
  159.7 3.4 %collective-permute-start.29 = (bf16[64,3072]{1,0:T(8,128)(2,1)S(1)}, bf16[64,3072]{1,0:T(8,128)(2,1)S(1)}, u32[]{:S(2)}, u32[]{:S(2)}) collective-permute-start(bf16[64,3072]{1,0:T(8,128)(2,1)S(1)} %get-tuple-element.133), channel_id=1, source_target_pairs={{0,6},{2,0},{4,2},{6,4},{1,7},{3,1},{5,3},{7,5},{8,14},{10,8},{12,... | collective-permute-start | bytes 1179656 | tf_op jit(solution)/shard_map/ppermute | solution.py:351
  163.1 1.6 collective-permute-start.31
  164.6 12.4 %collective-permute-done.29 = bf16[64,3072]{1,0:T(8,128)(2,1)S(1)} collective-permute-done((bf16[64,3072]{1,0:T(8,128)(2,1)S(1)}, bf16[64,3072]{1,0:T(8,128)(2,1)S(1)}, u32[]{:S(2)}, u32[]{:S(2)}) %collective-permute-start.29) | collective-permute-done | bytes 393248 | tf_op jit(solution)/shard_map/ppermute | solution.py:351
  177.0 3.4 %collective-permute-done.30 = bf16[64,3072]{1,0:T(8,128)(2,1)S(1)} collective-permute-done((bf16[64,3072]{1,0:T(8,128)(2,1)S(1)}, bf16[64,3072]{1,0:T(8,128)(2,1)S(1)}, u32[]{:S(2)}, u32[]{:S(2)}) %collective-permute-start.30) | collective-permute-done | bytes 393248 | tf_op jit(solution)/shard_map/ppermute | solution.py:351
  180.5 1.0 add_convert_fusion
  (90 shorter events, 4.5 us)
Async XLA Ops:
  1.3 24.0 %collective-permute-start = (bf16[528,768]{1,0:T(8,128)(2,1)S(1)}, bf16[528,768]{1,0:T(8,128)(2,1)S(1)}, u32[]{:S(2)}, u32[]{:S(2)}) collective-permute-start(bf16[528,768]{1,0:T(8,128)(2,1)S(1)} %maximum_maximum_fusion.refs_1_.refs_2_), channel_id=1, source_target_pairs={{0,16},{16,32},{32,48},{48,64},{64,80},{80,96},{96,112},{112,0},{1... | collective-permute-start | bytes 2433032 | tf_op jit(solution)/shard_map/ppermute | solution.py:351
  3.3 22.0 %collective-permute-start.1 = (bf16[528,768]{1,0:T(8,128)(2,1)S(1)}, bf16[528,768]{1,0:T(8,128)(2,1)}, u32[]{:S(2)}, u32[]{:S(2)}) collective-permute-start(bf16[528,768]{1,0:T(8,128)(2,1)S(1)} %maximum_maximum_fusion.refs_1_.refs_2_), channel_id=1, source_target_pairs={{0,112},{16,0},{32,16},{48,32},{64,48},{80,64},{96,80},{112,96},{1... | collective-permute-start | bytes 2433032 | tf_op jit(solution)/shard_map/ppermute | solution.py:351
  7.3 10.7 %collective-permute-start.2 = (bf16[512,384]{1,0:T(8,128)(2,1)S(1)}, bf16[512,384]{1,0:T(8,128)(2,1)}, u32[]{:S(2)}, u32[]{:S(2)}) collective-permute-start(bf16[512,384]{1,0:T(8,128)(2,1)S(1)} %copy-done.8), channel_id=1, source_target_pairs={{0,128},{128,0},{1,129},{129,1},{2,130},{130,2},{3,131},{131,3},{4... | collective-permute-start | bytes 1179656 | tf_op jit(solution)/shard_map/ppermute | solution.py:351
  10.1 34.6 %collective-permute-start.6 = (bf16[384,1536]{1,0:T(8,128)(2,1)}, bf16[384,1536]{1,0:T(8,128)(2,1)}, u32[]{:S(2)}, u32[]{:S(2)}) collective-permute-start(bf16[384,1536]{1,0:T(8,128)(2,1)} %constant_dynamic-slice_fusion), channel_id=1, source_target_pairs={{0,2},{2,4},{4,6},{6,0},{1,3},{3,5},{5,7},{7,1},{8,10},{10,12},{12... | collective-permute-start | bytes 3538952 | tf_op jit(solution)/shard_map/ppermute | solution.py:351
  11.6 33.1 %collective-permute-start.7 = (bf16[384,1536]{1,0:T(8,128)(2,1)}, bf16[384,1536]{1,0:T(8,128)(2,1)}, u32[]{:S(2)}, u32[]{:S(2)}) collective-permute-start(bf16[384,1536]{1,0:T(8,128)(2,1)} %constant_dynamic-slice_fusion), channel_id=1, source_target_pairs={{0,6},{2,0},{4,2},{6,4},{1,7},{3,1},{5,3},{7,5},{8,14},{10,8},{12,... | collective-permute-start | bytes 3538952 | tf_op jit(solution)/shard_map/ppermute | solution.py:351
  18.0 26.7 %collective-permute-start.5 = (bf16[768,768]{1,0:T(8,128)(2,1)}, bf16[768,768]{1,0:T(8,128)(2,1)S(1)}, u32[]{:S(2)}, u32[]{:S(2)}) collective-permute-start(bf16[768,768]{1,0:T(8,128)(2,1)} %constant_dynamic-slice_fusion.1), channel_id=1, source_target_pairs={{0,136},{136,0},{8,128},{128,8},{1,137},{137,1},{9,129},{129,9},{2... | collective-permute-start | bytes 3538952 | tf_op jit(solution)/shard_map/ppermute | solution.py:355
  25.3 20.7 %collective-permute-start.3 = (bf16[528,768]{1,0:T(8,128)(2,1)S(1)}, bf16[528,768]{1,0:T(8,128)(2,1)}, u32[]{:S(2)}, u32[]{:S(2)}) collective-permute-start(bf16[528,768]{1,0:T(8,128)(2,1)S(1)} %collective-permute-done.refs_1_.refs_3_), channel_id=1, source_target_pairs={{0,16},{16,32},{32,48},{48,64},{64,80},{80,96},{96,112},{112,0},{1... | collective-permute-start | bytes 2433032 | tf_op jit(solution)/shard_map/ppermute | solution.py:351
  25.3 20.7 %collective-permute-start.4 = (bf16[528,768]{1,0:T(8,128)(2,1)}, bf16[528,768]{1,0:T(8,128)(2,1)}, u32[]{:S(2)}, u32[]{:S(2)}) collective-permute-start(bf16[528,768]{1,0:T(8,128)(2,1)} %collective-permute-done.1.refs_2_.refs_4_), channel_id=1, source_target_pairs={{0,112},{16,0},{32,16},{48,32},{64,48},{80,64},{96,80},{112,96},{1... | collective-permute-start | bytes 2433032 | tf_op jit(solution)/shard_map/ppermute | solution.py:351
  35.0 11.0 %copy-start.7 = (bf16[768,1152]{1,0:T(8,128)(2,1)S(1)}, bf16[768,1152]{1,0:T(8,128)(2,1)}, u32[]{:S(2)}) copy-start(bf16[768,1152]{1,0:T(8,128)(2,1)} %constant_dynamic-slice_fusion.3) | copy-start | bytes 5308420
  44.7 19.9 %copy-start.1 = (bf16[768,768]{1,0:T(8,128)(2,1)}, bf16[768,768]{1,0:T(8,128)(2,1)S(1)}, u32[]{:S(2)}) copy-start(bf16[768,768]{1,0:T(8,128)(2,1)S(1)} %collective-permute-done.5.refs_0_) | copy-start | bytes 3538948
  46.0 41.0 %collective-permute-start.12 = (bf16[768,1152]{1,0:T(8,128)(2,1)S(1)}, bf16[768,1152]{1,0:T(8,128)(2,1)}, u32[]{:S(2)}, u32[]{:S(2)}) collective-permute-start(bf16[768,1152]{1,0:T(8,128)(2,1)S(1)} %copy-done.7), channel_id=1, source_target_pairs={{0,136},{136,0},{8,128},{128,8},{1,137},{137,1},{9,129},{129,9},{2... | collective-permute-start | bytes 5308424 | tf_op jit(solution)/shard_map/ppermute | solution.py:355
  47.5 19.6 %collective-permute-start.8 = (bf16[528,768]{1,0:T(8,128)(2,1)}, bf16[528,768]{1,0:T(8,128)(2,1)S(1)}, u32[]{:S(2)}, u32[]{:S(2)}) collective-permute-start(bf16[528,768]{1,0:T(8,128)(2,1)} %collective-permute-done.3.refs_1_.refs_3_), channel_id=1, source_target_pairs={{0,16},{16,32},{32,48},{48,64},{64,80},{80,96},{96,112},{112,0},{1... | collective-permute-start | bytes 2433032 | tf_op jit(solution)/shard_map/ppermute | solution.py:351
  49.6 17.6 %collective-permute-start.9 = (bf16[528,768]{1,0:T(8,128)(2,1)}, bf16[528,768]{1,0:T(8,128)(2,1)S(1)}, u32[]{:S(2)}, u32[]{:S(2)}) collective-permute-start(bf16[528,768]{1,0:T(8,128)(2,1)} %collective-permute-done.4.refs_2_.refs_4_), channel_id=1, source_target_pairs={{0,112},{16,0},{32,16},{48,32},{64,48},{80,64},{96,80},{112,96},{1... | collective-permute-start | bytes 2433032 | tf_op jit(solution)/shard_map/ppermute | solution.py:351
  50.8 35.1 %collective-permute-start.13 = (bf16[768,768]{1,0:T(8,128)(2,1)S(1)}, bf16[768,768]{1,0:T(8,128)(2,1)S(1)}, u32[]{:S(2)}, u32[]{:S(2)}) collective-permute-start(bf16[768,768]{1,0:T(8,128)(2,1)S(1)} %collective-permute-done.5.refs_0_), channel_id=1, source_target_pairs={{0,128},{128,0},{1,129},{129,1},{2,130},{130,2},{3,131},{131,3},{4... | collective-permute-start | bytes 3538952 | tf_op jit(solution)/shard_map/ppermute | solution.py:351
  52.7 34.2 %collective-permute-start.14 = (bf16[384,1536]{1,0:T(8,128)(2,1)}, bf16[384,1536]{1,0:T(8,128)(2,1)}, u32[]{:S(2)}, u32[]{:S(2)}) collective-permute-start(bf16[384,1536]{1,0:T(8,128)(2,1)} %constant_dynamic-slice_fusion), channel_id=1, source_target_pairs={{0,4},{2,6},{4,0},{6,2},{1,5},{3,7},{5,1},{7,3},{8,12},{10,14},{12... | collective-permute-start | bytes 3538952 | tf_op jit(solution)/shard_map/ppermute | solution.py:351
  67.2 11.4 %collective-permute-start.10 = (bf16[272,768]{1,0:T(8,128)(2,1)S(1)}, bf16[272,768]{1,0:T(8,128)(2,1)S(1)}, u32[]{:S(2)}, u32[]{:S(2)}) collective-permute-start(bf16[272,768]{1,0:T(8,128)(2,1)S(1)} %slice.32), channel_id=1, source_target_pairs={{0,16},{16,32},{32,48},{48,64},{64,80},{80,96},{96,112},{112,0},{1... | collective-permute-start | bytes 1253384 | tf_op jit(solution)/shard_map/ppermute | solution.py:351
  69.0 9.5 %collective-permute-start.11 = (bf16[256,768]{1,0:T(8,128)(2,1)S(1)}, bf16[256,768]{1,0:T(8,128)(2,1)S(1)}, u32[]{:S(2)}, u32[]{:S(2)}) collective-permute-start(bf16[256,768]{1,0:T(8,128)(2,1)S(1)} %slice.33), channel_id=1, source_target_pairs={{0,112},{16,0},{32,16},{48,32},{64,48},{80,64},{96,80},{112,96},{1... | collective-permute-start | bytes 1179656 | tf_op jit(solution)/shard_map/ppermute | solution.py:351
  78.6 29.9 %copy-start = (bf16[384,3072]{1,0:T(8,128)(2,1)S(1)}, bf16[384,3072]{1,0:T(8,128)(2,1)}, u32[]{:S(2)}) copy-start(bf16[384,3072]{1,0:T(8,128)(2,1)} %own_w.1) | copy-start | bytes 7077892
  85.8 8.7 %copy-start.18 = (s32[8]{0:T(128)S(1)}, s32[8]{0:T(128)}, u32[]{:S(2)}) copy-start(s32[8]{0:T(128)} %constant.55.clone) | copy-start | bytes 100
  85.8 8.8 %copy-start.19 = (s32[4]{0:T(128)S(1)}, s32[4]{0:T(128)}, u32[]{:S(2)}) copy-start(s32[4]{0:T(128)} %constant.56.clone) | copy-start | bytes 52
  86.9 7.0 %collective-permute-start.15 = (bf16[384,1536]{1,0:T(8,128)(2,1)}, bf16[384,1536]{1,0:T(8,128)(2,1)}, u32[]{:S(2)}, u32[]{:S(2)}) collective-permute-start(bf16[384,1536]{1,0:T(8,128)(2,1)} %collective-permute-done.6.refs_0_), channel_id=1, source_target_pairs={{0,1},{1,0},{2,3},{3,2},{4,5},{5,4},{6,7},{7,6},{8,9},{9,8},{10,11... | collective-permute-start | bytes 3538952 | tf_op jit(solution)/shard_map/ppermute | solution.py:351
  86.9 7.1 %collective-permute-start.16 = (bf16[384,1536]{1,0:T(8,128)(2,1)}, bf16[384,1536]{1,0:T(8,128)(2,1)}, u32[]{:S(2)}, u32[]{:S(2)}) collective-permute-start(bf16[384,1536]{1,0:T(8,128)(2,1)} %collective-permute-done.7.refs_1_), channel_id=1, source_target_pairs={{0,1},{1,0},{2,3},{3,2},{4,5},{5,4},{6,7},{7,6},{8,9},{9,8},{10,11... | collective-permute-start | bytes 3538952 | tf_op jit(solution)/shard_map/ppermute | solution.py:351
  87.5 21.0 %collective-permute-start.17 = (bf16[384,1536]{1,0:T(8,128)(2,1)}, bf16[384,1536]{1,0:T(8,128)(2,1)}, u32[]{:S(2)}, u32[]{:S(2)}) collective-permute-start(bf16[384,1536]{1,0:T(8,128)(2,1)} %collective-permute-done.14.refs_2_), channel_id=1, source_target_pairs={{0,1},{1,0},{2,3},{3,2},{4,5},{5,4},{6,7},{7,6},{8,9},{9,8},{10,11... | collective-permute-start | bytes 3538952 | tf_op jit(solution)/shard_map/ppermute | solution.py:351
  87.5 38.6 %collective-permute-start.22 = (bf16[768,1152]{1,0:T(8,128)(2,1)}, bf16[768,1152]{1,0:T(8,128)(2,1)}, u32[]{:S(2)}, u32[]{:S(2)}) collective-permute-start(bf16[768,1152]{1,0:T(8,128)(2,1)} %collective-permute-done.12.refs_4_), channel_id=1, source_target_pairs={{0,1},{1,0},{2,3},{3,2},{4,5},{5,4},{6,7},{7,6},{8,9},{9,8},{10,11... | collective-permute-start | bytes 5308424 | tf_op jit(solution)/shard_map/ppermute | solution.py:351
  88.0 20.5 %all-to-all-start = ((bf16[8,128,512]{2,1,0:T(8,128)(2,1)}), bf16[8,128,512]{2,1,0:T(8,128)(2,1)S(1)}, u32[]{:S(2)}, u32[]{:S(2)}) async-start(bf16[8,128,512]{2,1,0:T(8,128)(2,1)} %bitcast.1), calls=%async_computation | async-start | bytes 2097152 | tf_op jit(solution)/shard_map/all_to_all | solution.py:463
  93.9 19.1 %collective-permute-start.18 = (bf16[768,384]{1,0:T(8,128)(2,1)}, bf16[768,384]{1,0:T(8,128)(2,1)}, u32[]{:S(2)}, u32[]{:S(2)}) collective-permute-start(bf16[768,384]{1,0:T(8,128)(2,1)} %constant_dynamic-slice_fusion.2), channel_id=1, source_target_pairs={{0,136},{136,0},{8,128},{128,8},{1,137},{137,1},{9,129},{129,9},{2... | collective-permute-start | bytes 1769480 | tf_op jit(solution)/shard_map/ppermute | solution.py:355
  94.0 20.6 %collective-permute-start.20 = (bf16[768,768]{1,0:T(8,128)(2,1)}, bf16[768,768]{1,0:T(8,128)(2,1)}, u32[]{:S(2)}, u32[]{:S(2)}) collective-permute-start(bf16[768,768]{1,0:T(8,128)(2,1)} %copy-done.1), channel_id=1, source_target_pairs={{0,1},{1,0},{2,3},{3,2},{4,5},{5,4},{6,7},{7,6},{8,9},{9,8},{10,11... | collective-permute-start | bytes 3538952 | tf_op jit(solution)/shard_map/ppermute | solution.py:351
  94.1 20.5 %collective-permute-start.21 = (bf16[768,768]{1,0:T(8,128)(2,1)}, bf16[768,768]{1,0:T(8,128)(2,1)}, u32[]{:S(2)}, u32[]{:S(2)}) collective-permute-start(bf16[768,768]{1,0:T(8,128)(2,1)} %copy-done.3), channel_id=1, source_target_pairs={{0,1},{1,0},{2,3},{3,2},{4,5},{5,4},{6,7},{7,6},{8,9},{9,8},{10,11... | collective-permute-start | bytes 3538952 | tf_op jit(solution)/shard_map/ppermute | solution.py:351
  94.7 19.8 %copy-start.11 = (f32[3072]{0:T(1024)S(1)}, f32[3072]{0:T(1024)}, u32[]{:S(2)}) copy-start(f32[3072]{0:T(1024)} %param.26) | copy-start | bytes 36868
  94.7 19.8 %copy-start.12 = (f32[3072]{0:T(1024)S(1)}, f32[3072]{0:T(1024)}, u32[]{:S(2)}) copy-start(f32[3072]{0:T(1024)} %param.27) | copy-start | bytes 36868
  94.7 19.8 %copy-start.13 = (f32[3072]{0:T(1024)S(1)}, f32[3072]{0:T(1024)}, u32[]{:S(2)}) copy-start(f32[3072]{0:T(1024)} %param.31) | copy-start | bytes 36868
  94.7 19.8 %copy-start.14 = (f32[3072]{0:T(1024)S(1)}, f32[3072]{0:T(1024)}, u32[]{:S(2)}) copy-start(f32[3072]{0:T(1024)} %param.28) | copy-start | bytes 36868
  108.4 17.7 %copy-start.5 = (bf16[64,3072]{1,0:T(8,128)(2,1)S(1)}, bf16[64,3072]{1,0:T(8,128)(2,1)}, u32[]{:S(2)}) copy-start(bf16[64,3072]{1,0:T(8,128)(2,1)} %residual_ref.1) | copy-start | bytes 1179652
  113.0 17.6 %copy-start.15 = (f32[768]{0:T(1024)S(1)}, f32[768]{0:T(1024)}, u32[]{:S(2)}) copy-start(f32[768]{0:T(1024)} %param.33) | copy-start | bytes 9220
  113.0 13.1 %collective-permute-start.23 = (bf16[768,384]{1,0:T(8,128)(2,1)}, bf16[768,384]{1,0:T(8,128)(2,1)S(1)}, u32[]{:S(2)}, u32[]{:S(2)}) collective-permute-start(bf16[768,384]{1,0:T(8,128)(2,1)} %collective-permute-done.18.refs_5_), channel_id=1, source_target_pairs={{0,1},{1,0},{2,3},{3,2},{4,5},{5,4},{6,7},{7,6},{8,9},{9,8},{10,11... | collective-permute-start | bytes 1769480 | tf_op jit(solution)/shard_map/ppermute | solution.py:351
  113.1 13.0 %collective-permute-start.19 = (bf16[64,3072]{1,0:T(8,128)(2,1)S(1)}, bf16[64,3072]{1,0:T(8,128)(2,1)S(1)}, u32[]{:S(2)}, u32[]{:S(2)}) collective-permute-start(bf16[64,3072]{1,0:T(8,128)(2,1)S(1)} %get-tuple-element.117), channel_id=1, source_target_pairs={{0,8},{8,0},{1,9},{9,1},{2,10},{10,2},{3,11},{11,3},{4,12},{12,4},... | collective-permute-start | bytes 1179656 | tf_op jit(solution)/shard_map/ppermute | solution.py:351
  127.3 11.7 %collective-permute-start.24 = (bf16[64,3072]{1,0:T(8,128)(2,1)S(1)}, bf16[64,3072]{1,0:T(8,128)(2,1)S(1)}, u32[]{:S(2)}, u32[]{:S(2)}) collective-permute-start(bf16[64,3072]{1,0:T(8,128)(2,1)S(1)} %get-tuple-element.124), channel_id=1, source_target_pairs={{0,2},{2,4},{4,6},{6,0},{1,3},{3,5},{5,7},{7,1},{8,10},{10,12},{12... | collective-permute-start | bytes 1179656 | tf_op jit(solution)/shard_map/ppermute | solution.py:351
  128.2 10.9 %collective-permute-start.25 = (bf16[64,3072]{1,0:T(8,128)(2,1)S(1)}, bf16[64,3072]{1,0:T(8,128)(2,1)S(1)}, u32[]{:S(2)}, u32[]{:S(2)}) collective-permute-start(bf16[64,3072]{1,0:T(8,128)(2,1)S(1)} %get-tuple-element.124), channel_id=1, source_target_pairs={{0,6},{2,0},{4,2},{6,4},{1,7},{3,1},{5,3},{7,5},{8,14},{10,8},{12,... | collective-permute-start | bytes 1179656 | tf_op jit(solution)/shard_map/ppermute | solution.py:351
  130.6 3.6 %collective-permute-start.28 = (f32[768]{0:T(1024)S(1)}, f32[768]{0:T(1024)S(1)}, u32[]{:S(2)}, u32[]{:S(2)}) collective-permute-start(f32[768]{0:T(1024)S(1)} %copy-done.15), channel_id=1, source_target_pairs={{0,136},{136,0},{8,128},{128,8},{1,137},{137,1},{9,129},{129,9},{2... | collective-permute-start | bytes 9224 | tf_op jit(solution)/shard_map/ppermute | solution.py:355
  134.2 12.9 %copy-start.2 = (bf16[768,768]{1,0:T(8,128)(2,1)S(1)}, bf16[768,768]{1,0:T(8,128)(2,1)}, u32[]{:S(2)}) copy-start(bf16[768,768]{1,0:T(8,128)(2,1)} %copy-done.1) | copy-start | bytes 3538948
  134.3 12.9 %copy-start.4 = (bf16[768,768]{1,0:T(8,128)(2,1)S(1)}, bf16[768,768]{1,0:T(8,128)(2,1)}, u32[]{:S(2)}) copy-start(bf16[768,768]{1,0:T(8,128)(2,1)} %copy-done.3) | copy-start | bytes 3538948
  139.0 7.0 %collective-permute-start.26 = (bf16[32,3072]{1,0:T(8,128)(2,1)S(1)}, bf16[32,3072]{1,0:T(8,128)(2,1)S(1)}, u32[]{:S(2)}, u32[]{:S(2)}) collective-permute-start(bf16[32,3072]{1,0:T(8,128)(2,1)S(1)} %slice.40), channel_id=1, source_target_pairs={{0,2},{2,4},{4,6},{6,0},{1,3},{3,5},{5,7},{7,1},{8,10},{10,12},{12... | collective-permute-start | bytes 589832 | tf_op jit(solution)/shard_map/ppermute | solution.py:351
  139.1 6.9 %collective-permute-start.27 = (bf16[32,3072]{1,0:T(8,128)(2,1)S(1)}, bf16[32,3072]{1,0:T(8,128)(2,1)S(1)}, u32[]{:S(2)}, u32[]{:S(2)}) collective-permute-start(bf16[32,3072]{1,0:T(8,128)(2,1)S(1)} %slice.41), channel_id=1, source_target_pairs={{0,6},{2,0},{4,2},{6,4},{1,7},{3,1},{5,3},{7,5},{8,14},{10,8},{12,... | collective-permute-start | bytes 589832 | tf_op jit(solution)/shard_map/ppermute | solution.py:351
  159.6 20.9 %copy-start.9 = (f32[3072]{0:T(1024)S(1)}, f32[3072]{0:T(1024)}, u32[]{:S(2)}) copy-start(f32[3072]{0:T(1024)} %param.35) | copy-start | bytes 36868
  159.6 20.9 %copy-start.10 = (f32[3072]{0:T(1024)S(1)}, f32[3072]{0:T(1024)}, u32[]{:S(2)}) copy-start(f32[3072]{0:T(1024)} %param.29) | copy-start | bytes 36868
  159.7 17.4 %collective-permute-start.29 = (bf16[64,3072]{1,0:T(8,128)(2,1)S(1)}, bf16[64,3072]{1,0:T(8,128)(2,1)S(1)}, u32[]{:S(2)}, u32[]{:S(2)}) collective-permute-start(bf16[64,3072]{1,0:T(8,128)(2,1)S(1)} %get-tuple-element.133), channel_id=1, source_target_pairs={{0,6},{2,0},{4,2},{6,4},{1,7},{3,1},{5,3},{7,5},{8,14},{10,8},{12,... | collective-permute-start | bytes 1179656 | tf_op jit(solution)/shard_map/ppermute | solution.py:351
  163.1 17.4 %collective-permute-start.30 = (bf16[64,3072]{1,0:T(8,128)(2,1)S(1)}, bf16[64,3072]{1,0:T(8,128)(2,1)S(1)}, u32[]{:S(2)}, u32[]{:S(2)}) collective-permute-start(bf16[64,3072]{1,0:T(8,128)(2,1)S(1)} %get-tuple-element.135), channel_id=1, source_target_pairs={{0,2},{2,4},{4,6},{6,0},{1,3},{3,5},{5,7},{7,1},{8,10},{10,12},{12... | collective-permute-start | bytes 1179656 | tf_op jit(solution)/shard_map/ppermute | solution.py:351
  163.1 17.4 %collective-permute-start.31 = (bf16[64,3072]{1,0:T(8,128)(2,1)S(1)}, bf16[64,3072]{1,0:T(8,128)(2,1)S(1)}, u32[]{:S(2)}, u32[]{:S(2)}) collective-permute-start(bf16[64,3072]{1,0:T(8,128)(2,1)S(1)} %get-tuple-element.134), channel_id=1, source_target_pairs={{0,4},{2,6},{4,0},{6,2},{1,5},{3,7},{5,1},{7,3},{8,12},{10,14},{12... | collective-permute-start | bytes 1179656 | tf_op jit(solution)/shard_map/ppermute | solution.py:351
  (5 other events, 27.1 us)

commit v6 on v5

--- a/solution.py
+++ b/solution.py
@@ -240,111 +240,151 @@
     )(own, other, residual, vectors)
 
 
-def mlp_body(order, x_ref, up_ref, down_ref, bias_ref, bias_far_ref, *refs):
-    n = 4
-    up_far, down_far, out_ref = refs[:n], refs[n : n + 4], refs[n + 4]
-    near, far, hid_near, hid_far, up_buf, down_buf, sems = refs[n + 5 :]
-    i = pl.program_id(0)
-    quarter = up_ref.shape[0]
-
-    first = down_far[0].shape[1] - quarter
-
-    def copies(j):
-        sem = sems.at[j, 0]
-        if j < n:
-            yield pltpu.make_async_copy(up_far[j], up_buf.at[j], sem)
-            return
-        a, b = down_far[(j - n) // 2 * 2 : (j - n) // 2 * 2 + 2]
-        to = down_buf.at[j - n]
-        if j % 2 == 0:
-            yield pltpu.make_async_copy(a.at[:, pl.ds(0, quarter)], to, sem)
-        else:
-            yield pltpu.make_async_copy(a.at[:, pl.ds(quarter, first)], to.at[:, pl.ds(0, first)], sem)
-            yield pltpu.make_async_copy(b, to.at[:, pl.ds(first, quarter - first)], sems.at[j, 1])
-
-    for j in range(2 * n):
+def start_ahead(i, copies, n):
+    for j in range(n):
 
         @pl.when(i == max(j - 2, 0))
         def _(j=j):
             for copy in copies(j):
                 copy.start()
 
-    @pl.when(i == 0)
-    def _():
-        near[...] = jnp.broadcast_to(bias_ref[...], near.shape)
-        far[...] = jnp.broadcast_to(bias_far_ref[...], far.shape)
-
-    for j in range(2 * n):
+    for j in range(n):
 
         @pl.when(i == j)
         def _(j=j):
             for copy in copies(j):
                 copy.wait()
 
-    @pl.when(i < n)
+
+def up_body(n_rows, order, up_ref, bias_ref, bias_far_ref, *refs):
+    n = 4
+    row_refs, up_far, out_ref = refs[:n_rows], refs[n_rows : n_rows + n], refs[n_rows + n]
+    x, near, far, up_buf, sems = refs[n_rows + n + 1 :]
+    i = pl.program_id(0)
+    quarter, hidden = up_ref.shape
+
+    start_ahead(i, lambda j: [pltpu.make_async_copy(up_far[j], up_buf.at[j], sems.at[j])], n)
+
+    @pl.when(i == 0)
     def _():
-        at = pl.multiple_of(i * quarter, quarter)
-        near[...] += jnp.dot(
-            x_ref[:, pl.ds(at, quarter)], up_ref[...], preferred_element_type=jnp.float32
-        )
-        at = pl.multiple_of(order[i] * quarter, quarter)
-        far[...] += jnp.dot(
-            x_ref[:, pl.ds(at, quarter)], up_buf[i], preferred_element_type=jnp.float32
-        )
+        at = 0
+        for ref in row_refs:
+            x[at : at + ref.shape[0]] = ref[...]
+            at += ref.shape[0]
+        near[...] = jnp.broadcast_to(bias_ref[...], near.shape)
+        far[...] = jnp.broadcast_to(bias_far_ref[...], far.shape)
+
+    at = pl.multiple_of(i * quarter, quarter)
+    near[...] += jnp.dot(x[:, pl.ds(at, quarter)], up_ref[...], preferred_element_type=jnp.float32)
+    at = pl.multiple_of(order[i] * quarter, quarter)
+    far[...] += jnp.dot(x[:, pl.ds(at, quarter)], up_buf[i], preferred_element_type=jnp.float32)
 
     @pl.when(i == n - 1)
     def _():
-        hid_near[...] = jax.nn.gelu(near[...], approximate=True).astype(jnp.bfloat16)
-        hid_far[...] = jax.nn.gelu(far[...], approximate=True).astype(jnp.bfloat16)
-
-    @pl.when(i >= n)
-    def _():
-        out_ref[...] = (
-            jnp.dot(hid_near[...], down_ref[...], preferred_element_type=jnp.float32)
-            + jnp.dot(hid_far[...], down_buf[i - n], preferred_element_type=jnp.float32)
-        ).astype(jnp.bfloat16)
-
-
-def mlp(x, up, down, bias, bias_far, up_far, down_far, order):
-    rows, d_model = x.shape
-    hidden = up.shape[1]
-    n = len(up_far)
+        out_ref[:, :hidden] = jax.nn.gelu(near[...], approximate=True).astype(jnp.bfloat16)
+        out_ref[:, hidden:] = jax.nn.gelu(far[...], approximate=True).astype(jnp.bfloat16)
+
+
+def up_project(row_pieces, up, bias, bias_far, up_far, order):
+    d_model, hidden = up.shape
+    n = 4
     quarter = d_model // n
+    rows = sum(piece.shape[0] for piece in row_pieces)
     whole = lambda i, order: (0, 0)
-    column = lambda i, order: (0, order[jnp.maximum(i, n)])
-    far_spec = pl.BlockSpec(memory_space=pltpu.MemorySpace.HBM)
     return pl.pallas_call(
-        mlp_body,
+        functools.partial(up_body, len(row_pieces)),
         grid_spec=pltpu.PrefetchScalarGridSpec(
             num_scalar_prefetch=1,
-            grid=(2 * n,),
+            grid=(n,),
             in_specs=[
-                pl.BlockSpec((rows, d_model), whole),
-                pl.BlockSpec((quarter, hidden), lambda i, order: (jnp.minimum(i, n - 1), 0)),
-                pl.BlockSpec((hidden, quarter), column),
+                pl.BlockSpec((quarter, hidden), lambda i, order: (i, 0)),
                 pl.BlockSpec((1, hidden), whole),
                 pl.BlockSpec((1, hidden), whole),
-                *[far_spec] * (n + 4),
+                *[pl.BlockSpec(piece.shape, whole) for piece in row_pieces],
+                *[pl.BlockSpec(memory_space=pltpu.MemorySpace.HBM)] * n,
+            ],
+            out_specs=pl.BlockSpec((rows, 2 * hidden), whole),
+            scratch_shapes=[
+                pltpu.VMEM((rows, d_model), jnp.bfloat16),
+                pltpu.VMEM((rows, hidden), jnp.float32),
+                pltpu.VMEM((rows, hidden), jnp.float32),
+                pltpu.VMEM((n, quarter, hidden), jnp.bfloat16),
+                pltpu.SemaphoreType.DMA((n,)),
+            ],
+        ),
+        out_shape=jax.ShapeDtypeStruct((rows, 2 * hidden), jnp.bfloat16),
+        cost_estimate=pl.CostEstimate(
+            flops=4 * rows * d_model * hidden,
+            transcendentals=rows * hidden * 2,
+            bytes_accessed=4 * d_model * hidden,
+        ),
+        compiler_params=pltpu.CompilerParams(vmem_limit_bytes=40 << 20),
+    )(order, up, bias.reshape(1, -1), bias_far.reshape(1, -1), *row_pieces, *up_far)
+
+
+def down_body(n_rows, order, down_ref, *refs):
+    n = 4
+    row_refs, down_far, out_ref = refs[:n_rows], refs[n_rows : n_rows + n], refs[n_rows + n]
+    x, down_buf, sems = refs[n_rows + n + 1 :]
+    i = pl.program_id(0)
+    hidden, quarter = down_ref.shape
+    first = down_far[0].shape[1] - quarter
+
+    def copies(j):
+        a, b = down_far[j // 2 * 2 : j // 2 * 2 + 2]
+        to = down_buf.at[j]
+        if j % 2 == 0:
+            return [pltpu.make_async_copy(a.at[:, pl.ds(0, quarter)], to, sems.at[j, 0])]
+        return [
+            pltpu.make_async_copy(a.at[:, pl.ds(quarter, first)], to.at[:, pl.ds(0, first)], sems.at[j, 0]),
+            pltpu.make_async_copy(b, to.at[:, pl.ds(first, quarter - first)], sems.at[j, 1]),
+        ]
+
+    start_ahead(i, copies, n)
+
+    @pl.when(i == 0)
+    def _():
+        at = 0
+        for ref in row_refs:
+            x[at : at + ref.shape[0]] = ref[...]
+            at += ref.shape[0]
+
+    out_ref[...] = (
+        jnp.dot(x[:, :hidden], down_ref[...], preferred_element_type=jnp.float32)
+        + jnp.dot(x[:, hidden:], down_buf[i], preferred_element_type=jnp.float32)
+    ).astype(jnp.bfloat16)
+
+
+def down_project(row_pieces, down, down_far, order):
+    hidden, d_model = down.shape
+    n = 4
+    quarter = d_model // n
+    rows = sum(piece.shape[0] for piece in row_pieces)
+    whole = lambda i, order: (0, 0)
+    column = lambda i, order: (0, order[i])
+    return pl.pallas_call(
+        functools.partial(down_body, len(row_pieces)),
+        grid_spec=pltpu.PrefetchScalarGridSpec(
+            num_scalar_prefetch=1,
+            grid=(n,),
+            in_specs=[
+                pl.BlockSpec((hidden, quarter), column),
+                *[pl.BlockSpec(piece.shape, whole) for piece in row_pieces],
+                *[pl.BlockSpec(memory_space=pltpu.MemorySpace.HBM)] * n,
             ],
             out_specs=pl.BlockSpec((rows, quarter), column),
             scratch_shapes=[
-                pltpu.VMEM((rows, hidden), jnp.float32),
-                pltpu.VMEM((rows, hidden), jnp.float32),
-                pltpu.VMEM((rows, hidden), jnp.bfloat16),
-                pltpu.VMEM((rows, hidden), jnp.bfloat16),
-                pltpu.VMEM((n, quarter, hidden), jnp.bfloat16),
+                pltpu.VMEM((rows, 2 * hidden), jnp.bfloat16),
                 pltpu.VMEM((n, hidden, quarter), jnp.bfloat16),
-                pltpu.SemaphoreType.DMA((2 * n, 2)),
+                pltpu.SemaphoreType.DMA((n, 2)),
             ],
         ),
         out_shape=jax.ShapeDtypeStruct((rows, d_model), jnp.bfloat16),
         cost_estimate=pl.CostEstimate(
-            flops=8 * rows * d_model * hidden,
-            transcendentals=rows * hidden * 2,
-            bytes_accessed=8 * d_model * hidden,
-        ),
-        compiler_params=pltpu.CompilerParams(vmem_limit_bytes=46 << 20),
-    )(order, x, up, down, bias.reshape(1, -1), bias_far.reshape(1, -1), *up_far, *down_far)
+            flops=4 * rows * d_model * hidden, transcendentals=0, bytes_accessed=4 * d_model * hidden
+        ),
+        compiler_params=pltpu.CompilerParams(vmem_limit_bytes=40 << 20),
+    )(order, down, *row_pieces, *down_far)
 
 
 def shift(array, axis, size, by):
@@ -372,8 +412,8 @@
     n = rows.shape[0] // 2
     left = shift(rows, "x", 4, 1)
     right = shift(rows, "x", 4, 3)
-    far = jnp.concatenate([shift(left[:n], "x", 4, 1), shift(right[n:], "x", 4, 3)], axis=0)
-    return rows, left, right, far
+    far = [shift(left[:n], "x", 4, 1), shift(right[n:], "x", 4, 3)]
+    return [rows, left, right], far
 
 
 def shards(
@@ -439,10 +479,11 @@
     two = around(*one)
     state = attend(queries, [own], None)
     state = attend(queries, one, state)
-    two, state, up_a, out_l, out_r, down_first, out_half = tie(
-        (two, state, up_a, out_l, out_r, down_first, out_half)
-    )
+    two, state = tie((two, state))
     three = around(*two)
+    state, up_a, out_l, out_r, down_first, out_half = tie(
+        (state, up_a, out_l, out_r, down_first, out_half)
+    )
     down_a = cross(down_first)
     up_b = shift(up_a, "yl", 2, 1)
     out_f = shift(out_half, "x", 4, 2)
@@ -463,17 +504,20 @@
     parts = lax.all_to_all(
         part.reshape(8, 2 * row_block, width + HD), ("yl", "x"), split_axis=0, concat_axis=0, tiled=True
     )
-    parts, out_mate = tie((parts, out_mate))
+    parts, out_mate, bias_far = tie((parts, out_mate, cross(up_bias)))
     proj_own, proj_away = join_project(parts, out_weight, out_mine, out_mate, order[4:], place)
     proj_away, down_b = tie((proj_away, down_b))
     proj_other = shift(proj_away, "yh", 2, 1)
     up_far = [up_a, up_b, shift(up_a, "dp", 2, 1), shift(up_b, "dp", 2, 1)]
     down_far = [down_a, down_b, shift(down_a, "dp", 2, 1), shift(down_b, "dp", 2, 1)]
-    bias_far = cross(up_bias)
     proj_other, up_far, down_far = tie((proj_other, up_far, down_far))
     stream, normed = stream_norm(proj_own, proj_other, residual_in, vectors)
-    everyone = jnp.concatenate(gather_x(normed), axis=0)
-    out = mlp(everyone, up_weight, down_weight, up_bias, bias_far, up_far, down_far, order)
+    near_rows, far_rows = gather_x(normed)
+    units = [
+        up_project(part, up_weight, up_bias, bias_far, up_far, order[:4])
+        for part in (near_rows, far_rows)
+    ]
+    out = down_project(units, down_weight, down_far, order[4:])
     blocks = out.reshape(4, row_block, d_model)
     total = blocks[0].astype(jnp.float32)
     total = total + shift(blocks[1], "x", 4, 3).astype(jnp.float32)

time: 182 us -> 181 us (level)
  waiting for transfers between devices: 59.4 us -> 56.9 us
  starting transfers between devices: 49.5 us -> 47.3 us
  Pallas kernels: 56.1 us -> 58.1 us
  other arithmetic: 3.83 us -> 5.74 us
    all_to_all x1, waiting for transfers between devices: 13.7 us -> 9.22 us  [shards(): lax.all_to_all(part.reshape(8, 2 * row_block, width + HD), ('yl', 'x'), s...]
    ppermute x28, waiting for transfers between devices: 42.5 us -> 44.7 us  [shift(): lax.ppermute(array, axis, [(i, (i + by) % size) for i in range(size)])]
    pallas_call x1 -> x3, Pallas kernels: 12.4 us -> 13.6 us  [the longest x2 7.95 us: up_project(): pl.pallas_call(functools.partial(up_body, len(row_pieces)), grid_spec=plt...]
  transfers between devices with their start and end apart: 33 -> 33, of which waited for: 12 -> 10; matrix products, arithmetic and copies ran while one was open for 6% -> 7% of each run, Pallas kernels for 23% -> 26%
where the time goes in v6:
time: 181 us; the launch traced here: 180 us
  Pallas kernels  58.1 us (32%)
  waiting for transfers between devices  56.9 us (31%)
  starting transfers between devices  47.3 us (26%)
  local copies, waits for them, and re-layouts  11.8 us (7%)
  other arithmetic  5.74 us (3%)
    ppermute x28, waiting for transfers between devices, shift(): lax.ppermute(array, axis, [(i, (i + by) % size) for i in range(size)])  44.7 us
    ppermute x28, starting transfers between devices, shift(): lax.ppermute(array, axis, [(i, (i + by) % size) for i in range(size)])  38 us
    pallas_call x5, Pallas kernels, attend(): pl.pallas_call(functools.partial(attend_body, len(ks), first, bool(last))...  37.2 us
    all_to_all x1, waiting for transfers between devices, shards(): lax.all_to_all(part.reshape(8, 2 * row_block, width + HD), ('yl', 'x'), s...  9.22 us
    pallas_call x2, Pallas kernels, up_project(): pl.pallas_call(functools.partial(up_body, len(row_pieces)), grid_spec=plt...  7.95 us
    pallas_call x1, Pallas kernels, join_project(): pl.pallas_call(join_project_body, grid_spec=pltpu.PrefetchScalarGridSpec(...  6.11 us
    all_to_all x1, starting transfers between devices, shards(): lax.all_to_all(part.reshape(8, 2 * row_block, width + HD), ('yl', 'x'), s...  6.03 us
    pallas_call x1, Pallas kernels, down_project(): pl.pallas_call(functools.partial(down_body, len(row_pieces)), grid_spec=p...  5.64 us
  transfers between devices with their start and end apart: 33, of which 10 were waited for; matrix products, arithmetic and copies ran while one was open for 7% of the time, Pallas kernels for 26%

profile of v6, /device:TPU:8, one launch (start us, length us, event | category | flops | bytes accessed | tf_op | source)
XLA Modules:
  0.0 180.3 jit_solution(1597841175301706305)
XLA Ops:
  0.0 1.3 maximum_maximum_fusion.refs_1_.refs_2_
  1.3 2.0 %collective-permute-start = (bf16[528,768]{1,0:T(8,128)(2,1)S(1)}, bf16[528,768]{1,0:T(8,128)(2,1)S(1)}, u32[]{:S(2)}, u32[]{:S(2)}) collective-permute-start(bf16[528,768]{1,0:T(8,128)(2,1)S(1)} %maximum_maximum_fusion.refs_1_.refs_2_), channel_id=1, source_target_pairs={{0,16},{16,32},{32,48},{48,64},{64,80},{80,96},{96,112},{112,0},{1... | collective-permute-start | bytes 2433032 | tf_op jit(solution)/shard_map/ppermute | solution.py:391
  3.3 4.0 %collective-permute-start.1 = (bf16[528,768]{1,0:T(8,128)(2,1)S(1)}, bf16[528,768]{1,0:T(8,128)(2,1)}, u32[]{:S(2)}, u32[]{:S(2)}) collective-permute-start(bf16[528,768]{1,0:T(8,128)(2,1)S(1)} %maximum_maximum_fusion.refs_1_.refs_2_), channel_id=1, source_target_pairs={{0,112},{16,0},{32,16},{48,32},{64,48},{80,64},{96,80},{112,96},{1... | collective-permute-start | bytes 2433032 | tf_op jit(solution)/shard_map/ppermute | solution.py:391
  7.7 2.4 %constant_dynamic-slice_fusion = bf16[384,1536]{1,0:T(8,128)(2,1)} fusion(bf16[384,3072]{1,0:T(8,128)(2,1)} %own_w.1, s32[]{:T(128)S(6)} %select_n.27), kind=kLoop, calls=%fused_computation.7 | loop fusion | bytes 2359300 | tf_op jit(solution)/shard_map/dynamic_slice | solution.py:400
  10.1 1.5 collective-permute-start.8
  11.6 1.7 collective-permute-start.9
  13.3 2.4 %constant_dynamic-slice_fusion.1 = bf16[768,768]{1,0:T(8,128)(2,1)} fusion(bf16[3072,768]{1,0:T(8,128)(2,1)} %up_ref.3, s32[]{:T(128)S(6)} %select_n.30), kind=kLoop, calls=%fused_computation.8 | loop fusion | bytes 2359300 | tf_op jit(solution)/shard_map/dynamic_slice | solution.py:400
  15.7 2.3 %collective-permute-done.2 = bf16[512,384]{1,0:T(8,128)(2,1)} collective-permute-done((bf16[512,384]{1,0:T(8,128)(2,1)S(1)}, bf16[512,384]{1,0:T(8,128)(2,1)}, u32[]{:S(2)}, u32[]{:S(2)}) %collective-permute-start.2) | collective-permute-done | bytes 393248 | tf_op jit(solution)/shard_map/ppermute | solution.py:391
  18.0 1.6 collective-permute-start.7
  19.6 1.9 %constant_dynamic-slice_fusion.2 = bf16[768,384]{1,0:T(8,128)(2,1)} fusion(bf16[768,3072]{1,0:T(8,128)(2,1)} %down_ref.1, s32[]{:T(128)S(6)} %select_n.28), kind=kLoop, calls=%fused_computation.9 | loop fusion | bytes 1179652 | tf_op jit(solution)/shard_map/dynamic_slice | solution.py:405
  21.5 2.8 %constant_dynamic-slice_fusion.3 = bf16[768,1152]{1,0:T(8,128)(2,1)} fusion(bf16[768,3072]{1,0:T(8,128)(2,1)} %down_ref.1, s32[]{:T(128)S(6)} %select_n.27), kind=kLoop, calls=%fused_computation.10 | loop fusion | bytes 3538948 | tf_op jit(solution)/shard_map/dynamic_slice | solution.py:405
  24.3 1.0 collective-permute-done.refs_1_.refs_3_
  25.3 3.2 %collective-permute-start.4 = (bf16[528,768]{1,0:T(8,128)(2,1)}, bf16[528,768]{1,0:T(8,128)(2,1)}, u32[]{:S(2)}, u32[]{:S(2)}) collective-permute-start(bf16[528,768]{1,0:T(8,128)(2,1)} %collective-permute-done.1.refs_2_.refs_4_), channel_id=1, source_target_pairs={{0,112},{16,0},{32,16},{48,32},{64,48},{80,64},{96,80},{112,96},{1... | collective-permute-start | bytes 2433032 | tf_op jit(solution)/shard_map/ppermute | solution.py:391
  28.5 1.5 maximum_select_fusion.refs_0_
  30.0 5.1 %shard_map.190 = (f32[3,1,1024]{2,1,0:T(1,128)S(1)}, f32[3,1,1024]{2,1,0:T(1,128)S(1)}, f32[384,1024]{1,0:T(8,128)S(1)}) custom-call(bf16[1024,384]{1,0:T(8,128)(2,1)S(1)} %maximum_select_fusion.refs_0_, bf16[528,768]{1,0:T(8,128)(2,1)S(1)} %maximum_maximum_fusion.refs_1_.refs_2_, bf16[528,768]{1,0:T(8,128)(2,1)S(1)} %maximum_maximum_fusion.refs_1_.refs_2_), custom_call_target="tpu_custom_call" | custom-call | flops 830472192 | bytes 1597440 | tf_op jit(solution)/shard_map/pallas_call | solution.py:111
  35.1 8.9 %shard_map.191 = (f32[3,1,1024]{2,1,0:T(1,128)S(1)}, f32[3,1,1024]{2,1,0:T(1,128)S(1)}, f32[384,1024]{1,0:T(8,128)S(1)}) custom-call(bf16[1024,384]{1,0:T(8,128)(2,1)S(1)} %maximum_select_fusion.refs_0_, bf16[528,768]{1,0:T(8,128)(2,1)S(1)} %collective-permute-done.refs_1_.refs_3_, bf16[528,768]{1,0:T(8,128)(2,1)} %collective-permute-done.1.refs_2_.refs_4_, ...), custom_call_target="tpu_custom_call" | custom-call | flops 1660944384 | bytes 2408448 | tf_op jit(solution)/shard_map/pallas_call | solution.py:111
  44.1 1.9 %collective-permute-done.3.refs_1_.refs_3_ = bf16[528,768]{1,0:T(8,128)(2,1)} collective-permute-done((bf16[528,768]{1,0:T(8,128)(2,1)S(1)}, bf16[528,768]{1,0:T(8,128)(2,1)}, u32[]{:S(2)}, u32[]{:S(2)}) %collective-permute-start.3) | collective-permute-done | bytes 811040 | tf_op jit(solution)/shard_map/ppermute | solution.py:391
  46.0 1.7 collective-permute-start.12
  47.6 2.0 %collective-permute-start.5 = (bf16[528,768]{1,0:T(8,128)(2,1)}, bf16[528,768]{1,0:T(8,128)(2,1)S(1)}, u32[]{:S(2)}, u32[]{:S(2)}) collective-permute-start(bf16[528,768]{1,0:T(8,128)(2,1)} %collective-permute-done.3.refs_1_.refs_3_), channel_id=1, source_target_pairs={{0,16},{16,32},{32,48},{48,64},{64,80},{80,96},{96,112},{112,0},{1... | collective-permute-start | bytes 2433032 | tf_op jit(solution)/shard_map/ppermute | solution.py:391
  49.7 1.2 collective-permute-start.6
  50.9 1.9 %collective-permute-start.13 = (bf16[768,768]{1,0:T(8,128)(2,1)S(1)}, bf16[768,768]{1,0:T(8,128)(2,1)S(1)}, u32[]{:S(2)}, u32[]{:S(2)}) collective-permute-start(bf16[768,768]{1,0:T(8,128)(2,1)S(1)} %collective-permute-done.7.refs_3_.refs_2_), channel_id=1, source_target_pairs={{0,128},{128,0},{1,129},{129,1},{2,130},{130,2},{3,131},{131,3},{4... | collective-permute-start | bytes 3538952 | tf_op jit(solution)/shard_map/ppermute | solution.py:391
  52.8 3.0 %collective-permute-start.14 = (bf16[384,1536]{1,0:T(8,128)(2,1)}, bf16[384,1536]{1,0:T(8,128)(2,1)}, u32[]{:S(2)}, u32[]{:S(2)}) collective-permute-start(bf16[384,1536]{1,0:T(8,128)(2,1)} %constant_dynamic-slice_fusion), channel_id=1, source_target_pairs={{0,4},{2,6},{4,0},{6,2},{1,5},{3,7},{5,1},{7,3},{8,12},{10,14},{12... | collective-permute-start | bytes 3538952 | tf_op jit(solution)/shard_map/ppermute | solution.py:391
  55.7 8.9 %shard_map.192 = (f32[3,1,1024]{2,1,0:T(1,128)S(1)}, f32[3,1,1024]{2,1,0:T(1,128)S(1)}, f32[384,1024]{1,0:T(8,128)S(1)}) custom-call(bf16[1024,384]{1,0:T(8,128)(2,1)S(1)} %maximum_select_fusion.refs_0_, bf16[528,768]{1,0:T(8,128)(2,1)} %collective-permute-done.3.refs_1_.refs_3_, bf16[528,768]{1,0:T(8,128)(2,1)} %collective-permute-done.4.refs_2_.refs_4_, ...), custom_call_target="tpu_custom_call" | custom-call | flops 1660944384 | bytes 2408448 | tf_op jit(solution)/shard_map/pallas_call | solution.py:111
  64.6 2.6 %collective-permute-done.5.refs_1_.refs_3_ = bf16[528,768]{1,0:T(8,128)(2,1)S(1)} collective-permute-done((bf16[528,768]{1,0:T(8,128)(2,1)}, bf16[528,768]{1,0:T(8,128)(2,1)S(1)}, u32[]{:S(2)}, u32[]{:S(2)}) %collective-permute-start.5) | collective-permute-done | bytes 811040 | tf_op jit(solution)/shard_map/ppermute | solution.py:391
  67.3 1.8 %collective-permute-start.10 = (bf16[272,768]{1,0:T(8,128)(2,1)S(1)}, bf16[272,768]{1,0:T(8,128)(2,1)S(1)}, u32[]{:S(2)}, u32[]{:S(2)}) collective-permute-start(bf16[272,768]{1,0:T(8,128)(2,1)S(1)} %slice.37), channel_id=1, source_target_pairs={{0,16},{16,32},{32,48},{48,64},{64,80},{80,96},{96,112},{112,0},{1... | collective-permute-start | bytes 1253384 | tf_op jit(solution)/shard_map/ppermute | solution.py:391
  69.1 1.6 collective-permute-start.11
  70.7 8.0 %shard_map.193 = (f32[3,1,1024]{2,1,0:T(1,128)S(1)}, f32[3,1,1024]{2,1,0:T(1,128)S(1)}, f32[384,1024]{1,0:T(8,128)S(1)}) custom-call(bf16[1024,384]{1,0:T(8,128)(2,1)S(1)} %maximum_select_fusion.refs_0_, bf16[528,768]{1,0:T(8,128)(2,1)S(1)} %collective-permute-done.5.refs_1_.refs_3_, bf16[528,768]{1,0:T(8,128)(2,1)S(1)} %collective-permute-done.6.refs_2_.refs_4_, ...), custom_call_target="tpu_custom_call" | custom-call | flops 1660944384 | bytes 2408448 | tf_op jit(solution)/shard_map/pallas_call | solution.py:111
  78.7 6.4 %shard_map.194 = bf16[2,4,2,64,512]{4,3,2,1,0:T(8,128)(2,1)S(1)} custom-call(bf16[1024,384]{1,0:T(8,128)(2,1)S(1)} %maximum_select_fusion.refs_0_, bf16[272,768]{1,0:T(8,128)(2,1)S(1)} %collective-permute-done.10.refs_1_.refs_3_, bf16[256,768]{1,0:T(8,128)(2,1)S(1)} %collective-permute-done.11.refs_2_.refs_4_, ...), custom_call_target="tpu_custom_call" | custom-call | flops 830472192 | bytes 1597440 | tf_op jit(solution)/shard_map/pallas_call | solution.py:111
  85.1 1.0 copy-done.3
  86.1 1.0 copy-done.1
  88.1 6.0 %all-to-all-start = ((bf16[8,128,512]{2,1,0:T(8,128)(2,1)}), bf16[8,128,512]{2,1,0:T(8,128)(2,1)}, u32[]{:S(2)}, u32[]{:S(2)}) async-start(bf16[8,128,512]{2,1,0:T(8,128)(2,1)} %bitcast.10), calls=%async_computation | async-start | bytes 2097152 | tf_op jit(solution)/shard_map/all_to_all | solution.py:504
  94.7 3.1 %collective-permute-done.18 = f32[768]{0:T(1024)S(1)} collective-permute-done((f32[768]{0:T(1024)S(1)}, f32[768]{0:T(1024)S(1)}, u32[]{:S(2)}, u32[]{:S(2)}) %collective-permute-start.18) | collective-permute-done | bytes 3104 | tf_op jit(solution)/shard_map/ppermute | solution.py:395
  99.8 9.2 %all-to-all-done.part_ref = bf16[8,128,512]{2,1,0:T(8,128)(2,1)} async-done(((bf16[8,128,512]{2,1,0:T(8,128)(2,1)}), bf16[8,128,512]{2,1,0:T(8,128)(2,1)}, u32[]{:S(2)}, u32[]{:S(2)}) %all-to-all-start) | async-done | bytes 1048608 | tf_op jit(solution)/shard_map/all_to_all | solution.py:504
  109.1 6.1 %shard_map.195 = (f32[64,3072]{1,0:T(8,128)S(1)}, bf16[64,3072]{1,0:T(8,128)(2,1)S(1)}) custom-call(s32[4]{0:T(128)S(1)} %get-tuple-element.145.order, s32[5]{0:T(128)S(1)} %pad_add_fusion.place, bf16[8,128,512]{2,1,0:T(8,128)(2,1)} %all-to-all-done.part_ref, bf16[384,3072]{1,0:T(8,128)(2,1)S(1)} %copy-done, ...), custom_call_target="tpu_custom_call" | custom-call | flops 1207959552 | bytes 9437184 | tf_op jit(solution)/shard_map/pallas_call | solution.py:185
  116.5 12.1 %collective-permute-done.20.other_ref = bf16[64,3072]{1,0:T(8,128)(2,1)S(1)} collective-permute-done((bf16[64,3072]{1,0:T(8,128)(2,1)S(1)}, bf16[64,3072]{1,0:T(8,128)(2,1)S(1)}, u32[]{:S(2)}, u32[]{:S(2)}) %collective-permute-start.20) | collective-permute-done | bytes 393248 | tf_op jit(solution)/shard_map/ppermute | solution.py:391
  128.6 1.1 shard_map.196
  129.8 0.9 collective-permute-start.25
  130.7 2.4 %collective-permute-start.26 = (bf16[64,3072]{1,0:T(8,128)(2,1)S(1)}, bf16[64,3072]{1,0:T(8,128)(2,1)S(1)}, u32[]{:S(2)}, u32[]{:S(2)}) collective-permute-start(bf16[64,3072]{1,0:T(8,128)(2,1)S(1)} %get-tuple-element.132.refs_0_), channel_id=1, source_target_pairs={{0,6},{2,0},{4,2},{6,4},{1,7},{3,1},{5,3},{7,5},{8,14},{10,8},{12,... | collective-permute-start | bytes 1179656 | tf_op jit(solution)/shard_map/ppermute | solution.py:391
  133.1 8.6 %collective-permute-done.25.refs_1_ = bf16[64,3072]{1,0:T(8,128)(2,1)S(1)} collective-permute-done((bf16[64,3072]{1,0:T(8,128)(2,1)S(1)}, bf16[64,3072]{1,0:T(8,128)(2,1)S(1)}, u32[]{:S(2)}, u32[]{:S(2)}) %collective-permute-start.25) | collective-permute-done | bytes 393248 | tf_op jit(solution)/shard_map/ppermute | solution.py:391
  141.9 3.3 %collective-permute-start.28 = (bf16[32,3072]{1,0:T(8,128)(2,1)S(1)}, bf16[32,3072]{1,0:T(8,128)(2,1)S(1)}, u32[]{:S(2)}, u32[]{:S(2)}) collective-permute-start(bf16[32,3072]{1,0:T(8,128)(2,1)S(1)} %slice.47), channel_id=1, source_target_pairs={{0,6},{2,0},{4,2},{6,4},{1,7},{3,1},{5,3},{7,5},{8,14},{10,8},{12,... | collective-permute-start | bytes 589832 | tf_op jit(solution)/shard_map/ppermute | solution.py:391
  145.2 4.3 %shard_map.197.refs_0_ = bf16[192,1536]{1,0:T(8,128)(2,1)S(1)} custom-call(s32[4]{0:T(128)S(1)} %get-tuple-element.144.order, bf16[3072,768]{1,0:T(8,128)(2,1)S(1)} %bitcast.7, f32[1,768]{1,0:T(1,128)S(1)} %reshape.27.bias_ref, f32[1,768]{1,0:T(1,128)S(1)} %reshape.28.bias_far_ref, bf16[64,3072]{1,0:T(8,128)(2,1)S(1)} %get-tuple-element.132.refs_0_, ...), custom_call_target="tpu_custom_call" | custom-call | flops 1811939328 | bytes 9437184 | tf_op jit(solution)/shard_map/pallas_call | solution.py:294
  149.5 3.7 %shard_map.198.refs_1_ = bf16[64,1536]{1,0:T(8,128)(2,1)S(1)} custom-call(s32[4]{0:T(128)S(1)} %get-tuple-element.144.order, bf16[3072,768]{1,0:T(8,128)(2,1)S(1)} %bitcast.7, f32[1,768]{1,0:T(1,128)S(1)} %reshape.27.bias_ref, f32[1,768]{1,0:T(1,128)S(1)} %reshape.28.bias_far_ref, bf16[32,3072]{1,0:T(8,128)(2,1)S(1)} %collective-permute-done.27.refs_0_, ...), custom_call_target="tpu_custom_call" | custom-call | flops 603979776 | bytes 9437184 | tf_op jit(solution)/shard_map/pallas_call | solution.py:294
  153.2 5.6 %shard_map.199 = bf16[256,3072]{1,0:T(8,128)(2,1)S(1)} custom-call(s32[4]{0:T(128)S(1)} %get-tuple-element.145.order, bf16[768,3072]{1,0:T(8,128)(2,1)S(1)} %bitcast.9, bf16[192,1536]{1,0:T(8,128)(2,1)S(1)} %shard_map.197.refs_0_, bf16[64,1536]{1,0:T(8,128)(2,1)S(1)} %shard_map.198.refs_1_, bf16[768,1152]{1,0:T(8,128)(2,1)} %collective-permute-done.12.refs_2_, ...), custom_call_target="tpu_custom_call" | custom-call | flops 2415919104 | bytes 9437184 | tf_op jit(solution)/shard_map/pallas_call | solution.py:365
  159.0 2.6 %collective-permute-start.29 = (bf16[64,3072]{1,0:T(8,128)(2,1)S(1)}, bf16[64,3072]{1,0:T(8,128)(2,1)S(1)}, u32[]{:S(2)}, u32[]{:S(2)}) collective-permute-start(bf16[64,3072]{1,0:T(8,128)(2,1)S(1)} %get-tuple-element.141), channel_id=1, source_target_pairs={{0,6},{2,0},{4,2},{6,4},{1,7},{3,1},{5,3},{7,5},{8,14},{10,8},{12,... | collective-permute-start | bytes 1179656 | tf_op jit(solution)/shard_map/ppermute | solution.py:391
  161.6 1.6 collective-permute-start.31
  163.2 8.0 %collective-permute-done.29 = bf16[64,3072]{1,0:T(8,128)(2,1)S(1)} collective-permute-done((bf16[64,3072]{1,0:T(8,128)(2,1)S(1)}, bf16[64,3072]{1,0:T(8,128)(2,1)S(1)}, u32[]{:S(2)}, u32[]{:S(2)}) %collective-permute-start.29) | collective-permute-done | bytes 393248 | tf_op jit(solution)/shard_map/ppermute | solution.py:391
  171.1 8.2 %collective-permute-done.30 = bf16[64,3072]{1,0:T(8,128)(2,1)S(1)} collective-permute-done((bf16[64,3072]{1,0:T(8,128)(2,1)S(1)}, bf16[64,3072]{1,0:T(8,128)(2,1)S(1)}, u32[]{:S(2)}, u32[]{:S(2)}) %collective-permute-start.30) | collective-permute-done | bytes 393248 | tf_op jit(solution)/shard_map/ppermute | solution.py:391
  179.3 1.0 add_convert_fusion
  (93 shorter events, 5.6 us)
Async XLA Ops:
  1.3 24.0 %collective-permute-start = (bf16[528,768]{1,0:T(8,128)(2,1)S(1)}, bf16[528,768]{1,0:T(8,128)(2,1)S(1)}, u32[]{:S(2)}, u32[]{:S(2)}) collective-permute-start(bf16[528,768]{1,0:T(8,128)(2,1)S(1)} %maximum_maximum_fusion.refs_1_.refs_2_), channel_id=1, source_target_pairs={{0,16},{16,32},{32,48},{48,64},{64,80},{80,96},{96,112},{112,0},{1... | collective-permute-start | bytes 2433032 | tf_op jit(solution)/shard_map/ppermute | solution.py:391
  3.3 22.0 %collective-permute-start.1 = (bf16[528,768]{1,0:T(8,128)(2,1)S(1)}, bf16[528,768]{1,0:T(8,128)(2,1)}, u32[]{:S(2)}, u32[]{:S(2)}) collective-permute-start(bf16[528,768]{1,0:T(8,128)(2,1)S(1)} %maximum_maximum_fusion.refs_1_.refs_2_), channel_id=1, source_target_pairs={{0,112},{16,0},{32,16},{48,32},{64,48},{80,64},{96,80},{112,96},{1... | collective-permute-start | bytes 2433032 | tf_op jit(solution)/shard_map/ppermute | solution.py:391
  7.3 10.7 %collective-permute-start.2 = (bf16[512,384]{1,0:T(8,128)(2,1)S(1)}, bf16[512,384]{1,0:T(8,128)(2,1)}, u32[]{:S(2)}, u32[]{:S(2)}) collective-permute-start(bf16[512,384]{1,0:T(8,128)(2,1)S(1)} %copy-done.6), channel_id=1, source_target_pairs={{0,128},{128,0},{1,129},{129,1},{2,130},{130,2},{3,131},{131,3},{4... | collective-permute-start | bytes 1179656 | tf_op jit(solution)/shard_map/ppermute | solution.py:391
  10.1 35.9 %collective-permute-start.8 = (bf16[384,1536]{1,0:T(8,128)(2,1)}, bf16[384,1536]{1,0:T(8,128)(2,1)}, u32[]{:S(2)}, u32[]{:S(2)}) collective-permute-start(bf16[384,1536]{1,0:T(8,128)(2,1)} %constant_dynamic-slice_fusion), channel_id=1, source_target_pairs={{0,2},{2,4},{4,6},{6,0},{1,3},{3,5},{5,7},{7,1},{8,10},{10,12},{12... | collective-permute-start | bytes 3538952 | tf_op jit(solution)/shard_map/ppermute | solution.py:391
  11.6 34.4 %collective-permute-start.9 = (bf16[384,1536]{1,0:T(8,128)(2,1)}, bf16[384,1536]{1,0:T(8,128)(2,1)}, u32[]{:S(2)}, u32[]{:S(2)}) collective-permute-start(bf16[384,1536]{1,0:T(8,128)(2,1)} %constant_dynamic-slice_fusion), channel_id=1, source_target_pairs={{0,6},{2,0},{4,2},{6,4},{1,7},{3,1},{5,3},{7,5},{8,14},{10,8},{12,... | collective-permute-start | bytes 3538952 | tf_op jit(solution)/shard_map/ppermute | solution.py:391
  18.0 28.0 %collective-permute-start.7 = (bf16[768,768]{1,0:T(8,128)(2,1)}, bf16[768,768]{1,0:T(8,128)(2,1)S(1)}, u32[]{:S(2)}, u32[]{:S(2)}) collective-permute-start(bf16[768,768]{1,0:T(8,128)(2,1)} %constant_dynamic-slice_fusion.1), channel_id=1, source_target_pairs={{0,136},{136,0},{8,128},{128,8},{1,137},{137,1},{9,129},{129,9},{2... | collective-permute-start | bytes 3538952 | tf_op jit(solution)/shard_map/ppermute | solution.py:395
  25.3 20.7 %collective-permute-start.3 = (bf16[528,768]{1,0:T(8,128)(2,1)S(1)}, bf16[528,768]{1,0:T(8,128)(2,1)}, u32[]{:S(2)}, u32[]{:S(2)}) collective-permute-start(bf16[528,768]{1,0:T(8,128)(2,1)S(1)} %collective-permute-done.refs_1_.refs_3_), channel_id=1, source_target_pairs={{0,16},{16,32},{32,48},{48,64},{64,80},{80,96},{96,112},{112,0},{1... | collective-permute-start | bytes 2433032 | tf_op jit(solution)/shard_map/ppermute | solution.py:391
  25.3 20.7 %collective-permute-start.4 = (bf16[528,768]{1,0:T(8,128)(2,1)}, bf16[528,768]{1,0:T(8,128)(2,1)}, u32[]{:S(2)}, u32[]{:S(2)}) collective-permute-start(bf16[528,768]{1,0:T(8,128)(2,1)} %collective-permute-done.1.refs_2_.refs_4_), channel_id=1, source_target_pairs={{0,112},{16,0},{32,16},{48,32},{64,48},{80,64},{96,80},{112,96},{1... | collective-permute-start | bytes 2433032 | tf_op jit(solution)/shard_map/ppermute | solution.py:391
  35.1 10.8 %copy-start.5 = (bf16[768,1152]{1,0:T(8,128)(2,1)S(1)}, bf16[768,1152]{1,0:T(8,128)(2,1)}, u32[]{:S(2)}) copy-start(bf16[768,1152]{1,0:T(8,128)(2,1)} %constant_dynamic-slice_fusion.3) | copy-start | bytes 5308420
  46.0 41.1 %collective-permute-start.12 = (bf16[768,1152]{1,0:T(8,128)(2,1)S(1)}, bf16[768,1152]{1,0:T(8,128)(2,1)}, u32[]{:S(2)}, u32[]{:S(2)}) collective-permute-start(bf16[768,1152]{1,0:T(8,128)(2,1)S(1)} %copy-done.5), channel_id=1, source_target_pairs={{0,136},{136,0},{8,128},{128,8},{1,137},{137,1},{9,129},{129,9},{2... | collective-permute-start | bytes 5308424 | tf_op jit(solution)/shard_map/ppermute | solution.py:395
  47.6 19.6 %collective-permute-start.5 = (bf16[528,768]{1,0:T(8,128)(2,1)}, bf16[528,768]{1,0:T(8,128)(2,1)S(1)}, u32[]{:S(2)}, u32[]{:S(2)}) collective-permute-start(bf16[528,768]{1,0:T(8,128)(2,1)} %collective-permute-done.3.refs_1_.refs_3_), channel_id=1, source_target_pairs={{0,16},{16,32},{32,48},{48,64},{64,80},{80,96},{96,112},{112,0},{1... | collective-permute-start | bytes 2433032 | tf_op jit(solution)/shard_map/ppermute | solution.py:391
  49.7 17.6 %collective-permute-start.6 = (bf16[528,768]{1,0:T(8,128)(2,1)}, bf16[528,768]{1,0:T(8,128)(2,1)S(1)}, u32[]{:S(2)}, u32[]{:S(2)}) collective-permute-start(bf16[528,768]{1,0:T(8,128)(2,1)} %collective-permute-done.4.refs_2_.refs_4_), channel_id=1, source_target_pairs={{0,112},{16,0},{32,16},{48,32},{64,48},{80,64},{96,80},{112,96},{1... | collective-permute-start | bytes 2433032 | tf_op jit(solution)/shard_map/ppermute | solution.py:391
  50.9 35.2 %collective-permute-start.13 = (bf16[768,768]{1,0:T(8,128)(2,1)S(1)}, bf16[768,768]{1,0:T(8,128)(2,1)S(1)}, u32[]{:S(2)}, u32[]{:S(2)}) collective-permute-start(bf16[768,768]{1,0:T(8,128)(2,1)S(1)} %collective-permute-done.7.refs_3_.refs_2_), channel_id=1, source_target_pairs={{0,128},{128,0},{1,129},{129,1},{2,130},{130,2},{3,131},{131,3},{4... | collective-permute-start | bytes 3538952 | tf_op jit(solution)/shard_map/ppermute | solution.py:391
  52.8 34.3 %collective-permute-start.14 = (bf16[384,1536]{1,0:T(8,128)(2,1)}, bf16[384,1536]{1,0:T(8,128)(2,1)}, u32[]{:S(2)}, u32[]{:S(2)}) collective-permute-start(bf16[384,1536]{1,0:T(8,128)(2,1)} %constant_dynamic-slice_fusion), channel_id=1, source_target_pairs={{0,4},{2,6},{4,0},{6,2},{1,5},{3,7},{5,1},{7,3},{8,12},{10,14},{12... | collective-permute-start | bytes 3538952 | tf_op jit(solution)/shard_map/ppermute | solution.py:391
  67.3 11.4 %collective-permute-start.10 = (bf16[272,768]{1,0:T(8,128)(2,1)S(1)}, bf16[272,768]{1,0:T(8,128)(2,1)S(1)}, u32[]{:S(2)}, u32[]{:S(2)}) collective-permute-start(bf16[272,768]{1,0:T(8,128)(2,1)S(1)} %slice.37), channel_id=1, source_target_pairs={{0,16},{16,32},{32,48},{48,64},{64,80},{80,96},{96,112},{112,0},{1... | collective-permute-start | bytes 1253384 | tf_op jit(solution)/shard_map/ppermute | solution.py:391
  69.1 9.5 %collective-permute-start.11 = (bf16[256,768]{1,0:T(8,128)(2,1)S(1)}, bf16[256,768]{1,0:T(8,128)(2,1)S(1)}, u32[]{:S(2)}, u32[]{:S(2)}) collective-permute-start(bf16[256,768]{1,0:T(8,128)(2,1)S(1)} %slice.38), channel_id=1, source_target_pairs={{0,112},{16,0},{32,16},{48,32},{64,48},{80,64},{96,80},{112,96},{1... | collective-permute-start | bytes 1179656 | tf_op jit(solution)/shard_map/ppermute | solution.py:391
  78.7 30.4 %copy-start = (bf16[384,3072]{1,0:T(8,128)(2,1)S(1)}, bf16[384,3072]{1,0:T(8,128)(2,1)}, u32[]{:S(2)}) copy-start(bf16[384,3072]{1,0:T(8,128)(2,1)} %own_w.1) | copy-start | bytes 7077892
  86.0 8.1 %copy-start.13 = (f32[768]{0:T(1024)S(1)}, f32[768]{0:T(1024)}, u32[]{:S(2)}) copy-start(f32[768]{0:T(1024)} %param.33) | copy-start | bytes 9220
  86.0 8.1 %copy-start.17 = (s32[4]{0:T(128)S(1)}, s32[4]{0:T(128)}, u32[]{:S(2)}) copy-start(s32[4]{0:T(128)} %constant.56.clone) | copy-start | bytes 52
  86.0 13.0 %copy-start.16 = (s32[8]{0:T(128)S(1)}, s32[8]{0:T(128)}, u32[]{:S(2)}) copy-start(s32[8]{0:T(128)} %constant.53.clone) | copy-start | bytes 100
  87.1 10.7 %collective-permute-start.15 = (bf16[384,1536]{1,0:T(8,128)(2,1)}, bf16[384,1536]{1,0:T(8,128)(2,1)}, u32[]{:S(2)}, u32[]{:S(2)}) collective-permute-start(bf16[384,1536]{1,0:T(8,128)(2,1)} %collective-permute-done.8.refs_0_), channel_id=1, source_target_pairs={{0,1},{1,0},{2,3},{3,2},{4,5},{5,4},{6,7},{7,6},{8,9},{9,8},{10,11... | collective-permute-start | bytes 3538952 | tf_op jit(solution)/shard_map/ppermute | solution.py:391
  87.1 10.8 %collective-permute-start.16 = (bf16[384,1536]{1,0:T(8,128)(2,1)}, bf16[384,1536]{1,0:T(8,128)(2,1)}, u32[]{:S(2)}, u32[]{:S(2)}) collective-permute-start(bf16[384,1536]{1,0:T(8,128)(2,1)} %collective-permute-done.9.refs_1_), channel_id=1, source_target_pairs={{0,1},{1,0},{2,3},{3,2},{4,5},{5,4},{6,7},{7,6},{8,9},{9,8},{10,11... | collective-permute-start | bytes 3538952 | tf_op jit(solution)/shard_map/ppermute | solution.py:391
  87.6 21.4 %collective-permute-start.17 = (bf16[384,1536]{1,0:T(8,128)(2,1)}, bf16[384,1536]{1,0:T(8,128)(2,1)}, u32[]{:S(2)}, u32[]{:S(2)}) collective-permute-start(bf16[384,1536]{1,0:T(8,128)(2,1)} %collective-permute-done.14.refs_2_), channel_id=1, source_target_pairs={{0,1},{1,0},{2,3},{3,2},{4,5},{5,4},{6,7},{7,6},{8,9},{9,8},{10,11... | collective-permute-start | bytes 3538952 | tf_op jit(solution)/shard_map/ppermute | solution.py:391
  87.7 40.9 %collective-permute-start.23 = (bf16[768,1152]{1,0:T(8,128)(2,1)}, bf16[768,1152]{1,0:T(8,128)(2,1)}, u32[]{:S(2)}, u32[]{:S(2)}) collective-permute-start(bf16[768,1152]{1,0:T(8,128)(2,1)} %collective-permute-done.12.refs_2_), channel_id=1, source_target_pairs={{0,1},{1,0},{2,3},{3,2},{4,5},{5,4},{6,7},{7,6},{8,9},{9,8},{10,11... | collective-permute-start | bytes 5308424 | tf_op jit(solution)/shard_map/ppermute | solution.py:391
  88.1 20.9 %all-to-all-start = ((bf16[8,128,512]{2,1,0:T(8,128)(2,1)}), bf16[8,128,512]{2,1,0:T(8,128)(2,1)}, u32[]{:S(2)}, u32[]{:S(2)}) async-start(bf16[8,128,512]{2,1,0:T(8,128)(2,1)} %bitcast.10), calls=%async_computation | async-start | bytes 2097152 | tf_op jit(solution)/shard_map/all_to_all | solution.py:504
  94.2 3.6 %collective-permute-start.18 = (f32[768]{0:T(1024)S(1)}, f32[768]{0:T(1024)S(1)}, u32[]{:S(2)}, u32[]{:S(2)}) collective-permute-start(f32[768]{0:T(1024)S(1)} %copy-done.13), channel_id=1, source_target_pairs={{0,136},{136,0},{8,128},{128,8},{1,137},{137,1},{9,129},{129,9},{2... | collective-permute-start | bytes 9224 | tf_op jit(solution)/shard_map/ppermute | solution.py:395
  97.8 17.5 %collective-permute-start.19 = (bf16[768,384]{1,0:T(8,128)(2,1)}, bf16[768,384]{1,0:T(8,128)(2,1)}, u32[]{:S(2)}, u32[]{:S(2)}) collective-permute-start(bf16[768,384]{1,0:T(8,128)(2,1)} %constant_dynamic-slice_fusion.2), channel_id=1, source_target_pairs={{0,136},{136,0},{8,128},{128,8},{1,137},{137,1},{9,129},{129,9},{2... | collective-permute-start | bytes 1769480 | tf_op jit(solution)/shard_map/ppermute | solution.py:395
  97.8 18.7 %collective-permute-start.21 = (bf16[768,768]{1,0:T(8,128)(2,1)S(1)}, bf16[768,768]{1,0:T(8,128)(2,1)}, u32[]{:S(2)}, u32[]{:S(2)}) collective-permute-start(bf16[768,768]{1,0:T(8,128)(2,1)S(1)} %collective-permute-done.7.refs_3_.refs_2_), channel_id=1, source_target_pairs={{0,1},{1,0},{2,3},{3,2},{4,5},{5,4},{6,7},{7,6},{8,9},{9,8},{10,11... | collective-permute-start | bytes 3538952 | tf_op jit(solution)/shard_map/ppermute | solution.py:391
  97.9 18.6 %collective-permute-start.22 = (bf16[768,768]{1,0:T(8,128)(2,1)}, bf16[768,768]{1,0:T(8,128)(2,1)}, u32[]{:S(2)}, u32[]{:S(2)}) collective-permute-start(bf16[768,768]{1,0:T(8,128)(2,1)} %copy-done.1), channel_id=1, source_target_pairs={{0,1},{1,0},{2,3},{3,2},{4,5},{5,4},{6,7},{7,6},{8,9},{9,8},{10,11... | collective-permute-start | bytes 3538952 | tf_op jit(solution)/shard_map/ppermute | solution.py:391
  109.0 36.1 %slice-start = ((s8[4718592]{0:T(1024)(128)(4,1)}), s8[4194304]{0:T(1024)(128)(4,1)S(1)}, s32[]{:S(2)}) async-start(s8[4718592]{0:T(1024)(128)(4,1)} %bitcast.6), calls=%async_computation.1 | async-start | bytes 8388608
  109.0 7.4 %copy-start.9 = (f32[3072]{0:T(1024)S(1)}, f32[3072]{0:T(1024)}, u32[]{:S(2)}) copy-start(f32[3072]{0:T(1024)} %param.26) | copy-start | bytes 36868
  109.1 19.5 %copy-start.4 = (bf16[64,3072]{1,0:T(8,128)(2,1)S(1)}, bf16[64,3072]{1,0:T(8,128)(2,1)}, u32[]{:S(2)}) copy-start(bf16[64,3072]{1,0:T(8,128)(2,1)} %residual_ref.1) | copy-start | bytes 1179652
  109.1 36.1 %slice-start.1 = ((s8[4718592]{0:T(1024)(128)(4,1)}), s8[524288]{0:T(1024)(128)(4,1)S(1)}, s32[]{:S(2)}) async-start(s8[4718592]{0:T(1024)(128)(4,1)} %bitcast.6), calls=%async_computation.2 | async-start | bytes 1048576
  115.2 29.9 %copy-start.15 = (f32[768]{0:T(1024)S(1)}, f32[768]{0:T(1024)}, u32[]{:S(2)}) copy-start(f32[768]{0:T(1024)} %copy-done.14) | copy-start | bytes 9220
  115.2 29.9 %copy-start.2 = (bf16[768,768]{1,0:T(8,128)(2,1)S(1)}, bf16[768,768]{1,0:T(8,128)(2,1)}, u32[]{:S(2)}) copy-start(bf16[768,768]{1,0:T(8,128)(2,1)} %copy-done.1) | copy-start | bytes 3538948
  115.3 13.4 %collective-permute-start.24 = (bf16[768,384]{1,0:T(8,128)(2,1)}, bf16[768,384]{1,0:T(8,128)(2,1)S(1)}, u32[]{:S(2)}, u32[]{:S(2)}) collective-permute-start(bf16[768,384]{1,0:T(8,128)(2,1)} %collective-permute-done.19.refs_3_), channel_id=1, source_target_pairs={{0,1},{1,0},{2,3},{3,2},{4,5},{5,4},{6,7},{7,6},{8,9},{9,8},{10,11... | collective-permute-start | bytes 1769480 | tf_op jit(solution)/shard_map/ppermute | solution.py:391
  115.6 13.0 %collective-permute-start.20 = (bf16[64,3072]{1,0:T(8,128)(2,1)S(1)}, bf16[64,3072]{1,0:T(8,128)(2,1)S(1)}, u32[]{:S(2)}, u32[]{:S(2)}) collective-permute-start(bf16[64,3072]{1,0:T(8,128)(2,1)S(1)} %get-tuple-element.124), channel_id=1, source_target_pairs={{0,8},{8,0},{1,9},{9,1},{2,10},{10,2},{3,11},{11,3},{4,12},{12,4},... | collective-permute-start | bytes 1179656 | tf_op jit(solution)/shard_map/ppermute | solution.py:391
  129.8 11.9 %collective-permute-start.25 = (bf16[64,3072]{1,0:T(8,128)(2,1)S(1)}, bf16[64,3072]{1,0:T(8,128)(2,1)S(1)}, u32[]{:S(2)}, u32[]{:S(2)}) collective-permute-start(bf16[64,3072]{1,0:T(8,128)(2,1)S(1)} %get-tuple-element.132.refs_0_), channel_id=1, source_target_pairs={{0,2},{2,4},{4,6},{6,0},{1,3},{3,5},{5,7},{7,1},{8,10},{10,12},{12... | collective-permute-start | bytes 1179656 | tf_op jit(solution)/shard_map/ppermute | solution.py:391
  130.7 11.1 %collective-permute-start.26 = (bf16[64,3072]{1,0:T(8,128)(2,1)S(1)}, bf16[64,3072]{1,0:T(8,128)(2,1)S(1)}, u32[]{:S(2)}, u32[]{:S(2)}) collective-permute-start(bf16[64,3072]{1,0:T(8,128)(2,1)S(1)} %get-tuple-element.132.refs_0_), channel_id=1, source_target_pairs={{0,6},{2,0},{4,2},{6,4},{1,7},{3,1},{5,3},{7,5},{8,14},{10,8},{12,... | collective-permute-start | bytes 1179656 | tf_op jit(solution)/shard_map/ppermute | solution.py:391
  141.7 11.5 %slice-start.2 = ((s8[4718592]{0:T(1024)(128)(4,1)}), s8[4194304]{0:T(1024)(128)(4,1)S(1)}, s32[]{:S(2)}) async-start(s8[4718592]{0:T(1024)(128)(4,1)} %bitcast.8), calls=%async_computation.3 | async-start | bytes 8388608
  141.7 7.7 %collective-permute-start.27 = (bf16[32,3072]{1,0:T(8,128)(2,1)S(1)}, bf16[32,3072]{1,0:T(8,128)(2,1)S(1)}, u32[]{:S(2)}, u32[]{:S(2)}) collective-permute-start(bf16[32,3072]{1,0:T(8,128)(2,1)S(1)} %slice.46), channel_id=1, source_target_pairs={{0,2},{2,4},{4,6},{6,0},{1,3},{3,5},{5,7},{7,1},{8,10},{10,12},{12... | collective-permute-start | bytes 589832 | tf_op jit(solution)/shard_map/ppermute | solution.py:391
  141.9 7.6 %collective-permute-start.28 = (bf16[32,3072]{1,0:T(8,128)(2,1)S(1)}, bf16[32,3072]{1,0:T(8,128)(2,1)S(1)}, u32[]{:S(2)}, u32[]{:S(2)}) collective-permute-start(bf16[32,3072]{1,0:T(8,128)(2,1)S(1)} %slice.47), channel_id=1, source_target_pairs={{0,6},{2,0},{4,2},{6,4},{1,7},{3,1},{5,3},{7,5},{8,14},{10,8},{12,... | collective-permute-start | bytes 589832 | tf_op jit(solution)/shard_map/ppermute | solution.py:391
  145.2 8.0 %slice-start.3 = ((s8[4718592]{0:T(1024)(128)(4,1)}), s8[524288]{0:T(1024)(128)(4,1)S(1)}, s32[]{:S(2)}) async-start(s8[4718592]{0:T(1024)(128)(4,1)} %bitcast.8), calls=%async_computation.4 | async-start | bytes 1048576
  158.9 20.4 %copy-start.7 = (f32[3072]{0:T(1024)S(1)}, f32[3072]{0:T(1024)}, u32[]{:S(2)}) copy-start(f32[3072]{0:T(1024)} %param.35) | copy-start | bytes 36868
  158.9 20.4 %copy-start.8 = (f32[3072]{0:T(1024)S(1)}, f32[3072]{0:T(1024)}, u32[]{:S(2)}) copy-start(f32[3072]{0:T(1024)} %param.29) | copy-start | bytes 36868
  159.0 12.1 %collective-permute-start.29 = (bf16[64,3072]{1,0:T(8,128)(2,1)S(1)}, bf16[64,3072]{1,0:T(8,128)(2,1)S(1)}, u32[]{:S(2)}, u32[]{:S(2)}) collective-permute-start(bf16[64,3072]{1,0:T(8,128)(2,1)S(1)} %get-tuple-element.141), channel_id=1, source_target_pairs={{0,6},{2,0},{4,2},{6,4},{1,7},{3,1},{5,3},{7,5},{8,14},{10,8},{12,... | collective-permute-start | bytes 1179656 | tf_op jit(solution)/shard_map/ppermute | solution.py:391
  161.6 17.7 %collective-permute-start.30 = (bf16[64,3072]{1,0:T(8,128)(2,1)S(1)}, bf16[64,3072]{1,0:T(8,128)(2,1)S(1)}, u32[]{:S(2)}, u32[]{:S(2)}) collective-permute-start(bf16[64,3072]{1,0:T(8,128)(2,1)S(1)} %get-tuple-element.143), channel_id=1, source_target_pairs={{0,2},{2,4},{4,6},{6,0},{1,3},{3,5},{5,7},{7,1},{8,10},{10,12},{12... | collective-permute-start | bytes 1179656 | tf_op jit(solution)/shard_map/ppermute | solution.py:391
  161.6 17.7 %collective-permute-start.31 = (bf16[64,3072]{1,0:T(8,128)(2,1)S(1)}, bf16[64,3072]{1,0:T(8,128)(2,1)S(1)}, u32[]{:S(2)}, u32[]{:S(2)}) collective-permute-start(bf16[64,3072]{1,0:T(8,128)(2,1)S(1)} %get-tuple-element.142), channel_id=1, source_target_pairs={{0,4},{2,6},{4,0},{6,2},{1,5},{3,7},{5,1},{7,3},{8,12},{10,14},{12... | collective-permute-start | bytes 1179656 | tf_op jit(solution)/shard_map/ppermute | solution.py:391
  (7 other events, 32.6 us)
